TPU v7x, 256 devices: a whole 4x4x8 slice. The times are simulated.
256 devices in a mesh: layer: 64 (over y, z_lo, x), dp: 4 (over z_hi, core).
Axes of the slice: x: 4, y: 4, z: 8 (z_hi: 2, z_lo: 4; z = z_hi * 4 + z_lo), core: 2. Of those that a mesh axis runs over, the one named last changes fastest.
Arguments:
- images: float32 [8, 16, 16, 128], P('dp'), may hold values from -6 to 6
- weights: bfloat16 [256, 3, 3, 128, 128], P('layer'), may hold values from -0.1875 to 0.1875
- biases: float32 [256, 128], P('layer'), may hold values from -3 to 3
- end_grad: float32 [8, 16, 16, 128], P('dp'), may hold values from -6 to 6
Outputs:
- interval_ends: float32 [64, 8, 16, 16, 128], P('layer', 'dp')
- start_adjoint: float32 [64, 8, 16, 16, 128], P('layer', 'dp')
- weight_grad: float32 [256, 3, 3, 128, 128], P('layer')
- bias_grad: float32 [256, 128], P('layer')
All inputs are finite; a program needn't handle non-finite values.
Results may differ from a plain program's by a relative error of at most 0.012.
The roundings to bfloat16 on the way count: a program that leaves them out, or rounds other values in their place, can miss the bound.
Values sent between devices are 32-bit elements; how exact they have to be, the bound alone decides.
No kernel may reach another device: no remote copies, remote signals or barrier semaphores. Data moves between devices by JAX's collectives and lax.ppermute only.
A program may use at most 128 MiB of HBM per device.

v0:
```python
import jax
import jax.numpy as jnp
from jax import lax
from jax.sharding import PartitionSpec as P

step_size = 0.25
conv_layout = ("NHWC", "HWIO", "NHWC")


def shifted(array, axis, by):
    size = lax.axis_size(axis)
    pairs = [(i, i + by) for i in range(size) if 0 <= i + by < size]
    return lax.ppermute(array, axis, pairs)


def entering(value, axis, join, neutral, backward):
    count, mine = (lax.axis_size(axis), lax.axis_index(axis))
    pieces = jax.tree.map(lambda part: lax.all_gather(part, axis), value)
    if backward:
        pieces = jax.tree.map(lambda part: part[::-1], pieces)
        mine = count - 1 - mine
    total = jax.tree.map(
        lambda part, zero: jnp.full_like(part, 0) + jnp.asarray(zero, part.dtype), value, neutral
    )

    def lap(position, total):
        longer = join(total, jax.tree.map(lambda part: part[position], pieces))
        return jax.tree.map(lambda new, old: jnp.where(position < mine, new, old), longer, total)

    return lax.fori_loop(0, count - 1, lap, total)


def convolve(states, kernel):
    return lax.conv_general_dilated(
        states.astype(jnp.bfloat16),
        kernel,
        (1, 1),
        "SAME",
        dimension_numbers=conv_layout,
        preferred_element_type=jnp.float32,
    )


def advance(states, weights, biases):
    inputs = []
    slopes = []
    for index in range(weights.shape[0]):
        rounded = states.astype(jnp.bfloat16)
        preact = convolve(rounded, weights[index]) + biases[index]
        activation = jnp.tanh(preact)
        inputs.append(rounded)
        slopes.append(activation)
        states = states + step_size * activation
    return (states, inputs, slopes)


def retreat(adjoint, transposed, slopes):
    for index in reversed(range(len(slopes))):
        change = step_size * (1.0 - slopes[index] * slopes[index]) * adjoint
        adjoint = adjoint + convolve(change, transposed[index])
    return adjoint


def kernel_grad(inputs_low, change_low):
    padded = jnp.pad(inputs_low, ((0, 0), (1, 1), (1, 1), (0, 0)))
    height = change_low.shape[1]
    width = change_low.shape[2]
    taps = []
    for row_at in range(3):
        line = []
        for col_at in range(3):
            window = padded[:, row_at : row_at + height, col_at : col_at + width, :]
            line.append(
                jnp.einsum("bhwc,bhwd->cd", window, change_low, preferred_element_type=jnp.float32)
            )
        taps.append(jnp.stack(line))
    return jnp.stack(taps)


def compose(earlier, later):
    product = jnp.dot(earlier[0], later[0], precision=lax.Precision.HIGHEST)
    moved = jnp.dot(earlier[1], later[0], precision=lax.Precision.HIGHEST) + later[1]
    return (product, moved)


def shards(images, weights, biases, end_grad):
    channels = weights.shape[-1]
    groups = lax.axis_size("layer")
    transposed = jnp.swapaxes(jnp.flip(weights, (1, 2)), 3, 4)
    identity = jnp.eye(channels, dtype=jnp.float32)
    matrix = identity + step_size * jnp.sum(weights[:, 1, 1].astype(jnp.float32), axis=0)
    is_first = lax.axis_index("layer") == 0
    is_last = lax.axis_index("layer") == groups - 1
    guess = jnp.einsum("bhwc,cd->bhwd", images, matrix, precision=lax.Precision.HIGHEST)
    arrived = shifted(guess, "layer", 1)
    starts = jnp.where(is_first, images, arrived)
    relaxed, _, _ = advance(starts, weights, biases)
    residual_rows = (relaxed - guess).reshape(1, groups, -1, channels)
    _, error = entering(
        (matrix, residual_rows), "layer", compose, (identity, jnp.zeros_like(residual_rows)), False
    )
    corrected = starts + error.reshape(starts.shape)
    interval_ends, inputs, slopes = advance(corrected, weights, biases)
    back = jnp.einsum("bhwd,cd->bhwc", end_grad, matrix, precision=lax.Precision.HIGHEST)
    arrived_back = shifted(back, "layer", -1)
    ends_adj = jnp.where(is_last, end_grad, arrived_back)
    again = retreat(ends_adj, transposed, slopes)
    adjoint_rows = (again - back).reshape(1, groups, -1, channels)
    _, adj_error = entering(
        (matrix.T, adjoint_rows), "layer", compose, (identity, jnp.zeros_like(adjoint_rows)), True
    )
    adjoint = ends_adj + adj_error.reshape(ends_adj.shape)
    divisor = 1.0 / (images.shape[0] * lax.axis_size("dp"))
    kernels = []
    offsets = []
    for index in reversed(range(len(slopes))):
        change = step_size * (1.0 - slopes[index] * slopes[index]) * adjoint
        change_low = change.astype(jnp.bfloat16)
        kernel_part = kernel_grad(inputs[index], change_low) * divisor
        offset_part = jnp.sum(change, axis=(0, 1, 2)) * divisor
        kernels.append(kernel_part)
        offsets.append(offset_part)
        adjoint = adjoint + convolve(change_low, transposed[index])
    weight_grad = jnp.stack(kernels[::-1])
    bias_grad = jnp.stack(offsets[::-1])
    weight_grad, bias_grad = lax.psum((weight_grad, bias_grad), "dp")
    return (interval_ends[None], adjoint[None], weight_grad, bias_grad)


def solution(mesh):
    in_specs = (
        P("dp", None, None, None),
        P("layer", None, None, None, None),
        P("layer", None),
        P("dp", None, None, None),
    )
    out_specs = (
        P("layer", "dp", None, None, None),
        P("layer", "dp", None, None, None),
        P("layer", None, None, None, None),
        P("layer", None),
    )
    return jax.shard_map(shards, mesh=mesh, in_specs=in_specs, out_specs=out_specs, check_vma=False)
```

profile of v0, /device:TPU:1, one launch (start us, length us, event | category | flops | bytes accessed | tf_op | source)
XLA Modules:
  0.0 1693.9 jit_solution(8998598685072067499)
XLA Ops:
  8.9 1.3 convolution_bitcast_fusion.3
  10.2 4.0 collective-permute-start
  15.0 4.1 collective-permute-done
  25.4 1.3 collective-permute-start.1
  29.4 295.7 %all-gather.6.cloned.1.call-done = f32[64,128,128]{2,1,0:T(8,128)} async-done(((f32[1,128,128]{2,1,0:T(8,128)}), f32[64,128,128]{2,1,0:T(8,128)}) %all-gather.6.cloned.1.call-update) | async-done | bytes 4194320 | tf_op jit(solution)/shard_map/all_gather | solution.py:18
  325.1 381.6 %all-gather.8.cloned.1.call-done = f32[64,1,64,8,128]{4,3,2,1,0:T(8,128)} async-done(((f32[1,1,64,8,128]{4,3,2,1,0:T(8,128)}), f32[64,1,64,8,128]{4,3,2,1,0:T(8,128)}) %all-gather.8.cloned.1.call-update) | async-done | bytes 16777232 | tf_op jit(solution)/shard_map/all_gather | solution.py:18
  706.7 141.6 %while.28 = (s32[]{:T(128)}, f32[1,64,8,128]{3,1,2,0:T(8,128)S(1)}, s32[]{:T(128)}, f32[64,128,128]{2,1,0:T(8,128)}, f32[64,1,64,8,128]{4,3,2,1,0:T(8,128)}, /*index=5*/s32[]{:T(128)}, s32[]{:T(128)}) while((s32[]{:T(128)}, f32[1,64,8,128]{3,1,2,0:T(8,128)S(1)}, s32[]{:T(128)}, f32[64,128,128]{2,1,0:T(8,128)}, ...), condition=%wide.region_2.3_spmd.clone, body=%wide.region_1.2_spmd.clone.sunk | while | flops 100925440 | bytes 2164835 | solution.py:30
  781.9 1.2 fusion.256
  808.9 1.2 fusion.256
  824.6 1.2 fusion.256
  853.7 1.4 subtract_multiply_fusion
  861.3 1.8 fusion.120
  863.4 130.6 %all-gather.12.cloned.1.call-done = f32[8192,128]{0,1:T(8,128)} async-done(((f32[128,128]{0,1:T(8,128)}), f32[8192,128]{0,1:T(8,128)}) %all-gather.12.cloned.1.call-update) | async-done | bytes 4194320 | tf_op jit(solution)/shard_map/all_gather | solution.py:18
  994.1 5.7 copy.223
  999.7 4.7 rev.10
  1004.5 362.5 %all-gather.10.cloned.1.call-done = f32[64,1,64,8,128]{4,3,2,1,0:T(8,128)} async-done(((f32[1,1,64,8,128]{4,3,2,1,0:T(8,128)}), f32[64,1,64,8,128]{4,3,2,1,0:T(8,128)}) %all-gather.10.cloned.1.call-update) | async-done | bytes 16777232 | tf_op jit(solution)/shard_map/all_gather | solution.py:18
  1366.9 11.5 rev.12
  1378.4 141.6 %while.29 = (s32[]{:T(128)}, f32[1,64,8,128]{3,1,2,0:T(8,128)S(1)}, s32[]{:T(128)}, f32[64,128,128]{2,1,0:T(8,128)}, f32[64,1,64,8,128]{4,3,2,1,0:T(8,128)}, /*index=5*/s32[]{:T(128)}, s32[]{:T(128)}) while((s32[]{:T(128)}, f32[1,64,8,128]{3,1,2,0:T(8,128)S(1)}, s32[]{:T(128)}, f32[64,128,128]{2,1,0:T(8,128)}, ...), condition=%wide.region_4.5_spmd.clone, body=%wide.region_3.4_spmd.clone.sunk | while | flops 100925440 | bytes 2164835 | solution.py:30
  1379.4 1.2 fusion.259
  1383.9 1.2 fusion.259
  1535.0 1.6 pad_maximum_fusion
  1539.2 49.8 %psum.15 = f32[4,128]{1,0:T(4,128)} all-reduce(f32[4,128]{1,0:T(4,128)S(1)} %pad_maximum_fusion.1), channel_id=1, replica_groups=mesh['layer'=64,'dp'=4] {'dp'}, use_global_device_ids=true, to_apply=%region_10.11 | all-reduce | flops 512 | bytes 4096 | tf_op jit(solution)/shard_map/psum | solution.py:126
  1590.1 94.0 %all-reduce.6.cloned.1.call-done = f32[4,3,3,128,128]{4,3,2,1,0:T(8,128)} async-done(((f32[4,3,3,128,128]{4,3,2,1,0:T(8,128)}), f32[4,3,3,128,128]{4,3,2,1,0:T(8,128)}) %all-reduce.6.cloned.1.call-update) | async-done | bytes 2359312 | tf_op jit(solution)/shard_map/psum | solution.py:126
  1684.1 3.3 copy.505
  (617 shorter events, 312.5 us)
Async XLA Ops:
  7.2 12.0 copy-start.2
  7.2 317.9 %all-gather.6.cloned.1.call-start = ((), (), s32[]{:S(2)}) async-start(), calls=%async_computation | async-start | bytes 4259840 | tf_op jit(solution)/shard_map/all_gather | solution.py:18
  8.8 697.9 %all-gather.8.cloned.1.call-start = ((), (), s32[]{:S(2)}) async-start(), calls=%async_computation.1 | async-start | bytes 17039360 | tf_op jit(solution)/shard_map/all_gather | solution.py:18
  10.2 8.9 collective-permute-start
  15.0 4.3 copy-start
  15.0 4.3 copy-start.13
  23.3 1.0 copy-start.3
  24.2 969.8 %all-gather.12.cloned.1.call-start = ((), (), s32[]{:S(2)}) async-start(), calls=%async_computation.4 | async-start | bytes 4259840 | tf_op jit(solution)/shard_map/all_gather | solution.py:18
  25.4 829.9 %collective-permute-start.1 = (f32[2,16,16,128]{3,2,1,0:T(8,128)}, f32[2,16,16,128]{3,2,1,0:T(8,128)}, u32[]{:S(2)}, u32[]{:S(2)}) collective-permute-start(f32[2,16,16,128]{3,2,1,0:T(8,128)} %convolution_bitcast_fusion.2), channel_id=1, source_target_pairs={{4,0},{8,4},{12,8},{16,12},{20,16},{24,20},{28,24},{32,28},{36,32}... | collective-permute-start | bytes 786440 | tf_op jit(solution)/shard_map/ppermute | solution.py:13
  27.3 1339.6 %all-gather.10.cloned.1.call-start = ((), (), s32[]{:S(2)}) async-start(), calls=%async_computation.2 | async-start | bytes 17039360 | tf_op jit(solution)/shard_map/all_gather | solution.py:18
  848.5 0.7 copy-start.14
  848.5 1.3 copy-start.5
  850.1 0.7 copy-start.7
  851.8 0.8 copy-start.9
  852.9 0.7 copy-start.11
  853.7 1.6 copy-start.4
  855.2 1.4 copy-start.1
  863.1 820.9 %all-reduce.6.cloned.1.call-start = ((), (), s32[]{:S(2)}) async-start(), calls=%async_computation.3 | async-start | bytes 4718592 | tf_op jit(solution)/shard_map/psum | solution.py:126
  1520.2 0.7 copy-start.15
  1523.9 0.9 copy-start.6
  1526.4 0.9 copy-start.8
  1528.9 0.9 copy-start.10
  1531.5 0.9 copy-start.12
  1537.7 0.7 copy-start.16
Sparse Core Ops, SparseCore 0:
  9.8 315.2 all-gather.5
  327.4 379.2 all-gather.7
  708.4 285.5 all-gather.11
  996.3 370.6 all-gather.9
  1536.7 147.3 all-reduce.5
where the time goes:
time: 1700 us; the launch traced here: 1690 us
  waiting for transfers between devices  1270 us (75%)
  matrix products  175 us (10%)
  local copies, waits for them, and re-layouts  163 us (10%)
  blocking collectives  49.8 us (3%)
    all_gather x4, waiting for transfers between devices, entering(): pieces = jax.tree.map(lambda part: lax.all_gather(part, axis), value)  1170 us
    dot_general x126, matrix products, compose(): jnp.dot(earlier[1], later[0], precision=lax.Precision.HIGHEST) + later[1]  153 us
    dynamic_slice x126, local copies, waits for them, and re-layouts, lap(): longer = join(total, jax.tree.map(lambda part: part[position], pieces))  122 us
    psum x1, waiting for transfers between devices, shards(): weight_grad, bias_grad = lax.psum((weight_grad, bias_grad), 'dp')  94 us
    psum x1, blocking collectives, shards(): weight_grad, bias_grad = lax.psum((weight_grad, bias_grad), 'dp')  49.8 us
  transfers between devices with their start and end apart: 7, of which 6 were waited for; matrix products, arithmetic and copies ran while one was open for 10% of the time, Pallas kernels for 0%

commit v1 on v0

v1 whole, which is shorter than its diff:
```python
import jax
import jax.numpy as jnp
from jax import lax
from jax.experimental import pallas as pl
from jax.experimental.pallas import tpu as pltpu
from jax.sharding import PartitionSpec as P

GROUP = 8
VMEM_LIMIT = 48 * 1024 * 1024
f32 = jnp.float32
bf16 = jnp.bfloat16


def shifted_columns(value, width):
    rows = value.shape[0]
    at = lax.broadcasted_iota(jnp.int32, value.shape, 0) % width
    left = jnp.where(at == 0, 0.0, pltpu.roll(value, 1, 0))
    right = jnp.where(at == width - 1, 0.0, pltpu.roll(value, rows - 1, 0))
    return jnp.concatenate([left.astype(bf16), value.astype(bf16), right.astype(bf16)], axis=1)


def clear_border(ref):
    height = ref.shape[1]
    edge = jnp.zeros((ref.shape[0], 1) + ref.shape[2:], ref.dtype)
    ref[:, 0:1] = edge
    ref[:, height - 1 : height] = edge


def rows_from(ref, row_at):
    images, height, width, lanes = ref.shape
    return ref[:, row_at : row_at + height - 2].reshape(images * (height - 2) * width, lanes)


def convolve(ref, value, kernel):
    images, height, width, lanes = ref.shape
    ref[:, 1 : height - 1] = shifted_columns(value, width).reshape(images, height - 2, width, lanes)
    total = None
    for row_at in range(3):
        part = jnp.dot(
            rows_from(ref, row_at),
            kernel[row_at * lanes : (row_at + 1) * lanes],
            preferred_element_type=f32,
        )
        total = part if total is None else total + part
    return total


def split(value):
    high = value.astype(bf16)
    low = (value - high.astype(f32)).astype(bf16)
    return high, low


def times(value, matrix, transpose=False):
    dims = (((1,), (1 if transpose else 0,)), ((), ()))
    high, low = split(value)
    mhigh, mlow = split(matrix)
    dot = lambda a, b: lax.dot_general(a, b, dims, preferred_element_type=f32)
    return dot(high, mhigh) + (dot(low, mhigh) + dot(high, mlow))


def call(body, outs, *args, scratch=(), flops=0, name=None):
    vmem = pl.BlockSpec(memory_space=pltpu.VMEM)
    smem = pl.BlockSpec(memory_space=pltpu.SMEM)
    size = sum(a.size * a.dtype.itemsize for a in args)
    size += sum(o.size * o.dtype.itemsize for o in outs)
    return pl.pallas_call(
        body,
        out_shape=tuple(outs),
        in_specs=[smem if a.dtype == jnp.int32 else vmem for a in args],
        out_specs=tuple(vmem for _ in outs),
        scratch_shapes=list(scratch),
        cost_estimate=pl.CostEstimate(flops=flops, bytes_accessed=size, transcendentals=0),
        compiler_params=pltpu.CompilerParams(vmem_limit_bytes=VMEM_LIMIT),
        name=name,
    )(*args)


def shape(dims, dtype=f32):
    return jax.ShapeDtypeStruct(dims, dtype)


def coarse_body(centre, out):
    total = centre[0].astype(f32)
    for index in range(1, centre.shape[0]):
        total = total + centre[index].astype(f32)
    out[...] = 0.25 * total


def transpose_body(weights, out):
    taps, channels = weights.shape[1], weights.shape[2]
    for index in range(weights.shape[0]):
        for tap in range(taps):
            flipped = weights[index, taps - 1 - tap].astype(f32).T
            out[index, tap * channels : (tap + 1) * channels] = flipped.astype(bf16)


def start_body(images, own, before, weights, biases, starts_out, residual_out, ref):
    clear_border(ref)
    field = images[...]
    starts = field + times(field, before[...])
    starts_out[...] = starts
    state = starts
    for index in range(weights.shape[0]):
        state = state + 0.25 * jnp.tanh(
            convolve(ref, state, weights.at[index]) + biases[index : index + 1]
        )
    residual_out[...] = state - (field + times(field, own[...]))


def ends_body(end_grad, own, after, ends_out, back_out):
    field = end_grad[...]
    ends_out[...] = field + times(field, after[...], True)
    back_out[...] = field + times(field, own[...], True)


def product_body(group, out):
    total = group[0]
    for index in range(1, group.shape[0]):
        total = total + (group[index] + times(total, group[index]))
    out[...] = total


def order(backward):
    return range(GROUP - 1, -1, -1) if backward else range(GROUP)


def total_body(backward, pieces, group, out):
    error = None
    for index in order(backward):
        if error is None:
            error = pieces[index]
        else:
            error = error + (times(error, group[index], backward) + pieces[index])
    out[...] = error


def replay_body(backward, mine, totals, products, pieces, group, out):
    error = jnp.zeros(totals.shape[1:], f32)
    for index in list(order(backward))[:-1]:
        longer = error + (times(error, products[index], backward) + totals[index])
        use = mine[0] < index if backward else mine[0] > index
        error = jnp.where(use, longer, error)
    for index in order(backward):
        out[index] = error
        if index != order(backward)[-1]:
            error = error + (times(error, group[index], backward) + pieces[index])


def forward_sweep(state, weights, biases, ref, inputs_out, slopes_out):
    for index in range(weights.shape[0]):
        activation = jnp.tanh(convolve(ref, state, weights.at[index]) + biases[index : index + 1])
        channels = state.shape[1]
        inputs_out[index] = ref[:, :, :, channels : 2 * channels]
        slopes_out[index] = 0.25 * (1.0 - activation * activation)
        state = state + 0.25 * activation
    return state


def middle_body(
    starts, error, ends_adj, back, weights, biases, transposed,
    corrected_out, ends_out, inputs_out, slopes_out, residual_out, ref,
):
    clear_border(ref)
    corrected = starts[...] + error[...]
    corrected_out[...] = corrected
    ends_out[...] = forward_sweep(corrected, weights, biases, ref, inputs_out, slopes_out)
    adjoint = ends_adj[...]
    for index in reversed(range(weights.shape[0])):
        change = slopes_out[index] * adjoint
        adjoint = adjoint + convolve(ref, change, transposed.at[index])
    residual_out[...] = adjoint - back[...]


def again_body(corrected, weights, biases, inputs_out, slopes_out, ref):
    clear_border(ref)
    forward_sweep(corrected[...], weights, biases, ref, inputs_out, slopes_out)


def finish_block(scale, adjoint, transposed, inputs, slope, ref):
    channels = adjoint.shape[1]
    change = slope * adjoint
    adjoint = adjoint + convolve(ref, change, transposed)
    offset = jnp.sum(change, axis=0, keepdims=True) * scale
    moved = rows_from(ref, 1)
    field = jnp.concatenate([rows_from(inputs, row_at) for row_at in range(3)], axis=1)
    kernel = scale * lax.dot_general(
        field, moved, (((0,), (0,)), ((), ())), preferred_element_type=f32
    )
    taps = [
        kernel[
            row_at * channels : (row_at + 1) * channels,
            (2 - col_at) * channels : (3 - col_at) * channels,
        ]
        for row_at in range(3)
        for col_at in range(3)
    ]
    return adjoint, taps, offset


def final_body(
    scale, ends_adj, error, transposed, inputs, slopes, adjoint_out, kernels_out, offsets_out, ref
):
    clear_border(ref)
    adjoint = ends_adj[...] + error[...]
    for index in reversed(range(transposed.shape[0])):
        adjoint, taps, offset = finish_block(
            scale, adjoint, transposed.at[index], inputs.at[index], slopes[index], ref
        )
        for tap in range(9):
            kernels_out[index, tap] = taps[tap]
        offsets_out[index : index + 1] = offset
    adjoint_out[...] = adjoint


def final_add_body(
    scale, ends_adj, error, transposed, inputs, slopes, kernels, offsets,
    kernels_out, offsets_out, ref,
):
    clear_border(ref)
    adjoint = ends_adj[...] + error[...]
    for index in reversed(range(transposed.shape[0])):
        adjoint, taps, offset = finish_block(
            scale, adjoint, transposed.at[index], inputs.at[index], slopes[index], ref
        )
        for tap in range(9):
            kernels_out[index, tap] = kernels[index, tap] + taps[tap]
        offsets_out[index : index + 1] = offsets[index : index + 1] + offset


def shards(images, weights, biases, end_grad):
    count, height, width, channels = images.shape
    blocks = weights.shape[0]
    rows = count * height * width
    layers = lax.axis_size("layer")
    outer = layers // GROUP
    near = [[a * GROUP + b for b in range(GROUP)] for a in range(outer)]
    far = [[a * GROUP + b for a in range(outer)] for b in range(GROUP)]
    dp = lax.axis_size("dp")
    partner = [(i, (i + dp // 2) % dp) for i in range(dp)]
    sibling = [(i, i ^ 1) for i in range(dp)]
    mine = (lax.axis_index("layer") // GROUP).astype(jnp.int32).reshape(1)
    scale = 1.0 / (count * dp)
    per_conv = 2 * rows * 9 * channels * channels

    def exchange(value, groups):
        return lax.all_to_all(value, "layer", 0, 0, axis_index_groups=groups)

    flat = weights.reshape(blocks, 9, channels, channels)
    kernels = weights.reshape(blocks, 9 * channels, channels)
    field = images.reshape(rows, channels)
    cotangent = end_grad.reshape(rows, channels)
    matrix_shape = (channels, channels)
    ref = pltpu.VMEM((count, height + 2, width, 3 * channels), bf16)

    (own,) = call(coarse_body, [shape(matrix_shape)], flat[:, 4], name="coarse")
    before = lax.ppermute(own, "layer", [(i, i + 1) for i in range(layers - 1)])
    after = lax.ppermute(own, "layer", [(i + 1, i) for i in range(layers - 1)])
    group = exchange(jnp.broadcast_to(own, (GROUP,) + matrix_shape), near)
    (transposed,) = call(
        transpose_body, [shape((blocks, 9 * channels, channels), bf16)], flat, name="flip"
    )

    starts, residual = call(
        start_body, [shape((rows, channels))] * 2, field, own, before, kernels, biases,
        scratch=[ref], flops=blocks * per_conv, name="start",
    )
    ends_adj, back = call(
        ends_body, [shape((rows, channels))] * 2, cotangent, own, after, name="ends"
    )
    (product,) = call(product_body, [shape(matrix_shape)], group, name="product")
    products = exchange(jnp.broadcast_to(product, (outer,) + matrix_shape), far)

    def scan(residual, backward):
        part = rows // GROUP
        pieces = exchange(residual.reshape(GROUP, part, channels), near)
        (total,) = call(
            lambda *refs: total_body(backward, *refs), [shape((part, channels))], pieces, group,
            name="total",
        )
        totals = exchange(jnp.broadcast_to(total, (outer, part, channels)), far)
        (error,) = call(
            lambda *refs: replay_body(backward, *refs), [shape((GROUP, part, channels))],
            mine, totals, products, pieces, group, name="replay",
        )
        return exchange(error, near).reshape(rows, channels)

    inputs_shape = shape((blocks, count, height + 2, width, channels), bf16)
    slopes_shape = shape((blocks, rows, channels))
    error = scan(residual, False)
    corrected, interval_ends, inputs, slopes, adj_residual = call(
        middle_body,
        [shape((rows, channels))] * 2 + [inputs_shape, slopes_shape, shape((rows, channels))],
        starts, error, ends_adj, back, kernels, biases, transposed,
        scratch=[ref], flops=2 * blocks * per_conv, name="middle",
    )
    other_corrected = lax.ppermute(corrected, "dp", partner)
    other_ends = lax.ppermute(ends_adj, "dp", partner)
    adj_error = scan(adj_residual, True)
    other_inputs, other_slopes = call(
        again_body, [inputs_shape, slopes_shape], other_corrected, kernels, biases,
        scratch=[ref], flops=blocks * per_conv, name="again",
    )
    other_error = lax.ppermute(adj_error, "dp", partner)
    kernels_shape = shape((blocks, 9, channels, channels))
    offsets_shape = shape((blocks, channels))
    adjoint, kernel_part, offset_part = call(
        lambda *refs: final_body(scale, *refs),
        [shape((rows, channels)), kernels_shape, offsets_shape],
        ends_adj, adj_error, transposed, inputs, slopes,
        scratch=[ref], flops=2 * blocks * per_conv, name="final",
    )
    kernel_part, offset_part = call(
        lambda *refs: final_add_body(scale, *refs), [kernels_shape, offsets_shape],
        other_ends, other_error, transposed, other_inputs, other_slopes, kernel_part, offset_part,
        scratch=[ref], flops=2 * blocks * per_conv, name="other",
    )
    weight_grad = kernel_part + lax.ppermute(kernel_part, "dp", sibling)
    bias_grad = offset_part + lax.ppermute(offset_part, "dp", sibling)
    full = (1, count, height, width, channels)
    return (
        interval_ends.reshape(full),
        adjoint.reshape(full),
        weight_grad.reshape(blocks, 3, 3, channels, channels),
        bias_grad,
    )


def solution(mesh):
    in_specs = (
        P("dp", None, None, None),
        P("layer", None, None, None, None),
        P("layer", None),
        P("dp", None, None, None),
    )
    out_specs = (
        P("layer", "dp", None, None, None),
        P("layer", "dp", None, None, None),
        P("layer", None, None, None, None),
        P("layer", None),
    )
    return jax.shard_map(shards, mesh=mesh, in_specs=in_specs, out_specs=out_specs, check_vma=False)
```

time: 1700 us -> 181 us (0.11)
  waiting for transfers between devices: 1270 us -> 40.7 us
  matrix products: 175 us -> 0 us
  local copies, waits for them, and re-layouts: 163 us -> 16.1 us
  starting transfers between devices: 5.85 us -> 47.1 us
  Pallas kernels: 0 us -> 26.3 us
    all_gather x4 -> x0, waiting for transfers between devices: 1170 us -> none  [entering(): pieces = jax.tree.map(lambda part: lax.all_gather(part, axis), value)]
    dot_general x164 -> x0, matrix products: 164 us -> none  [the longest x126 153 us: compose(): jnp.dot(earlier[1], later[0], precision=lax.Precision.HIGHEST) + later[1]]
    dynamic_slice x126 -> x0, local copies, waits for them, and re-layouts: 122 us -> none  [lap(): longer = join(total, jax.tree.map(lambda part: part[position], pieces))]
    psum x1 -> x0, waiting for transfers between devices: 94 us -> none  [shards(): weight_grad, bias_grad = lax.psum((weight_grad, bias_grad), 'dp')]
    psum x1 -> x0, blocking collectives: 49.8 us -> none  [shards(): weight_grad, bias_grad = lax.psum((weight_grad, bias_grad), 'dp')]
    all_to_all x0 -> x4, blocking collectives: none -> 46.9 us  [exchange(): return lax.all_to_all(value, 'layer', 0, 0, axis_index_groups=groups)]
    pallas_call x0 -> x13, Pallas kernels: none -> 26.3 us  [call(): pl.pallas_call(body, out_shape=tuple(outs), in_specs=[smem if a.dtype ==...]
    ppermute x2 -> x7, starting transfers between devices: 5.24 us -> 29.2 us  [the longest x1 9.09 us: shards(): weight_grad = kernel_part + lax.ppermute(kernel_part, 'dp', sibling)]
  transfers between devices with their start and end apart: 7 -> 11, of which waited for: 6 -> 8; matrix products, arithmetic and copies ran while one was open for 10% -> 0% of each run, Pallas kernels for 0% -> 4%
where the time goes in v1:
time: 181 us; the launch traced here: 180 us
  starting transfers between devices  47.1 us (26%)
  blocking collectives  46.9 us (26%)
  waiting for transfers between devices  40.7 us (22%)
  Pallas kernels  26.3 us (15%)
  local copies, waits for them, and re-layouts  16.1 us (9%)
  other arithmetic  2.4 us (1%)
    all_to_all x4, blocking collectives, exchange(): return lax.all_to_all(value, 'layer', 0, 0, axis_index_groups=groups)  46.9 us
    pallas_call x13, Pallas kernels, call(): pl.pallas_call(body, out_shape=tuple(outs), in_specs=[smem if a.dtype ==...  26.3 us
    all_to_all x4, starting transfers between devices, exchange(): return lax.all_to_all(value, 'layer', 0, 0, axis_index_groups=groups)  17.9 us
    all_to_all x4, waiting for transfers between devices, exchange(): return lax.all_to_all(value, 'layer', 0, 0, axis_index_groups=groups)  17.4 us
    unnamed x40, local copies, waits for them, and re-layouts  13.5 us
    ppermute x1, starting transfers between devices, shards(): weight_grad = kernel_part + lax.ppermute(kernel_part, 'dp', sibling)  9.09 us
    ppermute x1, starting transfers between devices, shards(): other_error = lax.ppermute(adj_error, 'dp', partner)  8.43 us
    ppermute x1, waiting for transfers between devices, shards(): other_error = lax.ppermute(adj_error, 'dp', partner)  7.55 us
  transfers between devices with their start and end apart: 11, of which 8 were waited for; matrix products, arithmetic and copies ran while one was open for 0% of the time, Pallas kernels for 4%

profile of v1, /device:TPU:1, one launch (start us, length us, event | category | flops | bytes accessed | tf_op | source)
XLA Modules:
  0.0 180.2 jit_solution(12470968294593025395)
XLA Ops:
  1.6 3.9 %collective-permute-start = (f32[128,128]{1,0:T(8,128)S(1)}, f32[128,128]{1,0:T(8,128)S(1)}, u32[]{:S(2)}, u32[]{:S(2)}) collective-permute-start(f32[128,128]{1,0:T(8,128)S(1)} %coarse.1.own), channel_id=1, source_target_pairs={{0,4},{4,8},{8,12},{12,16},{16,20},{20,24},{24,28},{28,32},{32,36}... | collective-permute-start | bytes 196616 | tf_op jit(solution)/shard_map/ppermute | solution.py:257
  9.8 2.5 %start.1 = (f32[512,128]{1,0:T(8,128)S(1)}, f32[512,128]{1,0:T(8,128)S(1)}) custom-call(f32[512,128]{1,0:T(8,128)S(1)} %bitcast.24, f32[128,128]{1,0:T(8,128)S(1)} %coarse.1.own, f32[128,128]{1,0:T(8,128)S(1)} %collective-permute-done.before, bf16[4,1152,128]{2,1,0:T(8,128)(2,1)S(1)} %bitcast.15, f32[4,128]{1,0:T(4,128)S(1)} %copy-done.12), custom_call_target="tpu_custom_call" | custom-call | flops 603979776 | bytes 2099200 | tf_op jit(solution)/shard_map/start/pallas_call | solution.py:67
  12.2 11.8 %all_to_all.40.refs_0_.refs_3_ = f32[8,64,128]{2,1,0:T(8,128)S(1)} all-to-all(f32[8,64,128]{2,1,0:T(8,128)S(1)} %bitcast.23), channel_id=1, replica_groups={{0,4,8,12,16,20,24,28},{32,36,40,44,48,52,56,60},{64,68,72,76,80,84,88,..., dimensions={0} | all-to-all | bytes 524288 | tf_op jit(solution)/shard_map/all_to_all | solution.py:247
  24.1 10.1 %all_to_all.41.refs_1_.group.refs_4_ = f32[8,128,128]{2,1,0:T(8,128)S(1)} all-to-all(f32[8,128,128]{2,1,0:T(8,128)S(1)} %broadcast_in_dim.12), channel_id=1, replica_groups={{0,4,8,12,16,20,24,28},{32,36,40,44,48,52,56,60},{64,68,72,76,80,84,88,..., dimensions={0} | all-to-all | bytes 1048576 | tf_op jit(solution)/shard_map/all_to_all | solution.py:247
  36.0 6.9 %all-to-all-start.2 = ((f32[8,64,128]{2,1,0:T(8,128)}), f32[8,64,128]{2,1,0:T(8,128)S(1)}, u32[]{:S(2)}, u32[]{:S(2)}) async-start(f32[8,64,128]{2,1,0:T(8,128)} %broadcast_in_dim.13), calls=%async_computation.2 | async-start | bytes 524288 | tf_op jit(solution)/shard_map/all_to_all | solution.py:247
  44.0 7.3 %all-to-all-done.2.refs_1_ = f32[8,64,128]{2,1,0:T(8,128)S(1)} async-done(((f32[8,64,128]{2,1,0:T(8,128)}), f32[8,64,128]{2,1,0:T(8,128)S(1)}, u32[]{:S(2)}, u32[]{:S(2)}) %all-to-all-start.2) | async-done | bytes 262176 | tf_op jit(solution)/shard_map/all_to_all | solution.py:247
  52.1 3.5 %all-to-all-start.3 = ((f32[8,128,128]{2,1,0:T(8,128)}), f32[8,128,128]{2,1,0:T(8,128)S(1)}, u32[]{:S(2)}, u32[]{:S(2)}) async-start(f32[8,128,128]{2,1,0:T(8,128)} %broadcast_in_dim.14), calls=%async_computation.3 | async-start | bytes 1048576 | tf_op jit(solution)/shard_map/all_to_all | solution.py:247
  55.7 10.1 %all-to-all-done.3.refs_2_ = f32[8,128,128]{2,1,0:T(8,128)S(1)} async-done(((f32[8,128,128]{2,1,0:T(8,128)}), f32[8,128,128]{2,1,0:T(8,128)S(1)}, u32[]{:S(2)}, u32[]{:S(2)}) %all-to-all-start.3) | async-done | bytes 524320 | tf_op jit(solution)/shard_map/all_to_all | solution.py:247
  65.7 2.9 %replay.2 = f32[8,64,128]{2,1,0:T(8,128)} custom-call(s32[1]{0:T(128)} %bitcast.4.refs_0_, f32[8,64,128]{2,1,0:T(8,128)S(1)} %all-to-all-done.2.refs_1_, f32[8,128,128]{2,1,0:T(8,128)S(1)} %all-to-all-done.3.refs_2_, f32[8,64,128]{2,1,0:T(8,128)S(1)} %all_to_all.40.refs_0_.refs_3_, f32[8,128,128]{2,1,0:T(8,128)S(1)} %all_to_all.41.refs_1_.group.refs_4_), custom_call_target="tpu_custom_call" | custom-call | bytes 1835012 | tf_op jit(solution)/shard_map/replay/pallas_call | solution.py:67
  68.6 4.0 %all-to-all-start.4 = ((f32[8,64,128]{2,1,0:T(8,128)}), f32[8,64,128]{2,1,0:T(8,128)}, u32[]{:S(2)}, u32[]{:S(2)}) async-start(f32[8,64,128]{2,1,0:T(8,128)} %replay.2), calls=%async_computation.4 | async-start | bytes 524288 | tf_op jit(solution)/shard_map/all_to_all | solution.py:247
  74.3 3.3 %collective-permute-done.1.after = f32[128,128]{1,0:T(8,128)S(1)} collective-permute-done((f32[128,128]{1,0:T(8,128)S(1)}, f32[128,128]{1,0:T(8,128)S(1)}, u32[]{:S(2)}, u32[]{:S(2)}) %collective-permute-start.1) | collective-permute-done | bytes 65568 | tf_op jit(solution)/shard_map/ppermute | solution.py:258
  83.3 5.6 %middle.1 = (f32[512,128]{1,0:T(8,128)S(1)}, f32[512,128]{1,0:T(8,128)}, bf16[4,2,18,16,128]{4,3,2,1,0:T(8,128)(2,1)S(1)}, f32[4,512,128]{2,1,0:T(8,128)S(1)}, f32[512,128]{1,0:T(8,128)S(1)}) custom-call(f32[512,128]{1,0:T(8,128)S(1)} %copy-done.17, f32[512,128]{1,0:T(8,128)} %bitcast.6.error, f32[512,128]{1,0:T(8,128)S(1)} %copy-done.7, ...), custom_call_target="tpu_custom_call" | custom-call | flops 1207959552 | bytes 5834752 | tf_op jit(solution)/shard_map/middle/pallas_call | solution.py:67
  88.8 12.7 %all_to_all.42.refs_0_.refs_3_ = f32[8,64,128]{2,1,0:T(8,128)S(1)} all-to-all(f32[8,64,128]{2,1,0:T(8,128)S(1)} %bitcast.22), channel_id=1, replica_groups={{0,4,8,12,16,20,24,28},{32,36,40,44,48,52,56,60},{64,68,72,76,80,84,88,..., dimensions={0} | all-to-all | bytes 524288 | tf_op jit(solution)/shard_map/all_to_all | solution.py:247
  102.9 12.3 %all_to_all.43.refs_1_ = f32[8,64,128]{2,1,0:T(8,128)S(1)} all-to-all(f32[8,64,128]{2,1,0:T(8,128)S(1)} %broadcast_in_dim.15), channel_id=1, replica_groups={{0,32,64,96,128,160,192,224},{4,36,68,100,132,164,196,228},{8,40,72,104..., dimensions={0} | all-to-all | bytes 524288 | tf_op jit(solution)/shard_map/all_to_all | solution.py:247
  115.2 2.6 %replay.3 = f32[8,64,128]{2,1,0:T(8,128)S(1)} custom-call(s32[1]{0:T(128)} %bitcast.4.refs_0_, f32[8,64,128]{2,1,0:T(8,128)S(1)} %all_to_all.43.refs_1_, f32[8,128,128]{2,1,0:T(8,128)S(1)} %all-to-all-done.3.refs_2_, f32[8,64,128]{2,1,0:T(8,128)S(1)} %all_to_all.42.refs_0_.refs_3_, f32[8,128,128]{2,1,0:T(8,128)S(1)} %all_to_all.41.refs_1_.group.refs_4_), custom_call_target="tpu_custom_call" | custom-call | bytes 1835012 | tf_op jit(solution)/shard_map/replay/pallas_call | solution.py:67
  118.6 3.4 %all-to-all-start.7 = ((f32[8,64,128]{2,1,0:T(8,128)}), f32[8,64,128]{2,1,0:T(8,128)S(1)}, u32[]{:S(2)}, u32[]{:S(2)}) async-start(f32[8,64,128]{2,1,0:T(8,128)} %copy-done.3), calls=%async_computation.7 | async-start | bytes 524288 | tf_op jit(solution)/shard_map/all_to_all | solution.py:247
  122.0 6.2 %collective-permute-start.4 = (f32[512,128]{1,0:T(8,128)}, f32[512,128]{1,0:T(8,128)S(1)}, u32[]{:S(2)}, u32[]{:S(2)}) collective-permute-start(f32[512,128]{1,0:T(8,128)} %copy-done.9), channel_id=1, source_target_pairs={{0,2},{1,3},{2,0},{3,1},{4,6},{5,7},{6,4},{7,5},{8,10},{9,11},{10,... | collective-permute-start | bytes 786440 | tf_op jit(solution)/shard_map/ppermute | solution.py:297
  128.3 8.4 %collective-permute-start.3 = (f32[512,128]{1,0:T(8,128)S(1)}, f32[512,128]{1,0:T(8,128)S(1)}, u32[]{:S(2)}, u32[]{:S(2)}) collective-permute-start(f32[512,128]{1,0:T(8,128)S(1)} %bitcast.20), channel_id=1, source_target_pairs={{0,2},{1,3},{2,0},{3,1},{4,6},{5,7},{6,4},{7,5},{8,10},{9,11},{10,... | collective-permute-start | bytes 786440 | tf_op jit(solution)/shard_map/ppermute | solution.py:304
  144.4 2.8 %final.1 = (f32[512,128]{1,0:T(8,128)}, f32[4,9,128,128]{3,2,1,0:T(8,128)S(1)}, f32[4,128]{1,0:T(4,128)S(1)}) custom-call(f32[512,128]{1,0:T(8,128)S(1)} %copy-done.8, f32[512,128]{1,0:T(8,128)S(1)} %bitcast.21, bf16[4,1152,128]{2,1,0:T(8,128)(2,1)S(1)} %flip.1.transposed.refs_2_, bf16[4,2,18,16,128]{4,3,2,1,0:T(8,128)(2,1)S(1)} %copy-done.19, ...), custom_call_target="tpu_custom_call" | custom-call | flops 1207959552 | bytes 5965824 | tf_op jit(solution)/shard_map/final/pallas_call | solution.py:67
  148.6 4.8 %collective-permute-done.2.refs_0_ = f32[512,128]{1,0:T(8,128)S(1)} collective-permute-done((f32[512,128]{1,0:T(8,128)}, f32[512,128]{1,0:T(8,128)S(1)}, u32[]{:S(2)}, u32[]{:S(2)}) %collective-permute-start.2) | collective-permute-done | bytes 262176 | tf_op jit(solution)/shard_map/ppermute | solution.py:298
  153.4 7.5 %collective-permute-done.3.refs_1_ = f32[512,128]{1,0:T(8,128)S(1)} collective-permute-done((f32[512,128]{1,0:T(8,128)S(1)}, f32[512,128]{1,0:T(8,128)S(1)}, u32[]{:S(2)}, u32[]{:S(2)}) %collective-permute-start.3) | collective-permute-done | bytes 262176 | tf_op jit(solution)/shard_map/ppermute | solution.py:304
  160.9 3.6 %other.1 = (f32[4,9,128,128]{3,2,1,0:T(8,128)S(1)}, f32[4,128]{1,0:T(4,128)S(1)}) custom-call(f32[512,128]{1,0:T(8,128)S(1)} %collective-permute-done.2.refs_0_, f32[512,128]{1,0:T(8,128)S(1)} %collective-permute-done.3.refs_1_, bf16[4,1152,128]{2,1,0:T(8,128)(2,1)S(1)} %flip.1.transposed.refs_2_, ...), custom_call_target="tpu_custom_call" | custom-call | flops 1207959552 | bytes 8065024 | tf_op jit(solution)/shard_map/other/pallas_call | solution.py:67
  164.6 9.1 %collective-permute-start.5 = (f32[4,9,128,128]{3,2,1,0:T(8,128)S(1)}, f32[4,9,128,128]{3,2,1,0:T(8,128)S(1)}, u32[]{:S(2)}, u32[]{:S(2)}) collective-permute-start(f32[4,9,128,128]{3,2,1,0:T(8,128)S(1)} %get-tuple-element.34), channel_id=1, source_target_pairs={{0,1},{1,0},{2,3},{3,2},{4,5},{5,4},{6,7},{7,6},{8,9},{9,8},{10,11... | collective-permute-start | bytes 7077896 | tf_op jit(solution)/shard_map/ppermute | solution.py:318
  173.8 4.1 %collective-permute-done.6 = f32[4,128]{1,0:T(4,128)S(1)} collective-permute-done((f32[4,128]{1,0:T(4,128)S(1)}, f32[4,128]{1,0:T(4,128)S(1)}, u32[]{:S(2)}, u32[]{:S(2)}) %collective-permute-start.6) | collective-permute-done | bytes 2080 | tf_op jit(solution)/shard_map/ppermute | solution.py:319
  (62 shorter events, 29.8 us)
Async XLA Ops:
  1.6 5.3 %collective-permute-start = (f32[128,128]{1,0:T(8,128)S(1)}, f32[128,128]{1,0:T(8,128)S(1)}, u32[]{:S(2)}, u32[]{:S(2)}) collective-permute-start(f32[128,128]{1,0:T(8,128)S(1)} %coarse.1.own), channel_id=1, source_target_pairs={{0,4},{4,8},{8,12},{12,16},{16,20},{20,24},{24,28},{28,32},{32,36}... | collective-permute-start | bytes 196616 | tf_op jit(solution)/shard_map/ppermute | solution.py:257
  6.9 1.3 copy-start.1
  12.2 11.8 %copy-start.16 = (f32[512,128]{1,0:T(8,128)}, f32[512,128]{1,0:T(8,128)S(1)}, u32[]{:S(2)}) copy-start(f32[512,128]{1,0:T(8,128)S(1)} %get-tuple-element.20.starts) | copy-start | bytes 786436
  36.0 15.3 %all-to-all-start.2 = ((f32[8,64,128]{2,1,0:T(8,128)}), f32[8,64,128]{2,1,0:T(8,128)S(1)}, u32[]{:S(2)}, u32[]{:S(2)}) async-start(f32[8,64,128]{2,1,0:T(8,128)} %broadcast_in_dim.13), calls=%async_computation.2 | async-start | bytes 524288 | tf_op jit(solution)/shard_map/all_to_all | solution.py:247
  42.9 31.1 %copy-start.2 = (bf16[4,3,3,128,128]{4,3,2,1,0:T(8,128)(2,1)S(1)}, bf16[4,3,3,128,128]{4,3,2,1,0:T(8,128)(2,1)}, u32[]{:S(2)}) copy-start(bf16[4,3,3,128,128]{4,3,2,1,0:T(8,128)(2,1)} %param.5) | copy-start | bytes 3538948
  52.1 13.6 %all-to-all-start.3 = ((f32[8,128,128]{2,1,0:T(8,128)}), f32[8,128,128]{2,1,0:T(8,128)S(1)}, u32[]{:S(2)}, u32[]{:S(2)}) async-start(f32[8,128,128]{2,1,0:T(8,128)} %broadcast_in_dim.14), calls=%async_computation.3 | async-start | bytes 1048576 | tf_op jit(solution)/shard_map/all_to_all | solution.py:247
  65.7 14.7 %copy-start.13 = (f32[4,128]{1,0:T(4,128)S(1)}, f32[4,128]{1,0:T(4,128)}, u32[]{:S(2)}) copy-start(f32[4,128]{1,0:T(4,128)} %biases.5) | copy-start | bytes 6148
  68.6 11.8 %all-to-all-start.4 = ((f32[8,64,128]{2,1,0:T(8,128)}), f32[8,64,128]{2,1,0:T(8,128)}, u32[]{:S(2)}, u32[]{:S(2)}) async-start(f32[8,64,128]{2,1,0:T(8,128)} %replay.2), calls=%async_computation.4 | async-start | bytes 524288 | tf_op jit(solution)/shard_map/all_to_all | solution.py:247
  72.6 5.0 %collective-permute-start.1 = (f32[128,128]{1,0:T(8,128)S(1)}, f32[128,128]{1,0:T(8,128)S(1)}, u32[]{:S(2)}, u32[]{:S(2)}) collective-permute-start(f32[128,128]{1,0:T(8,128)S(1)} %coarse.1.own), channel_id=1, source_target_pairs={{4,0},{8,4},{12,8},{16,12},{20,16},{24,20},{28,24},{32,28},{36,32}... | collective-permute-start | bytes 196616 | tf_op jit(solution)/shard_map/ppermute | solution.py:258
  77.7 1.0 copy-start.4
  80.4 1.0 copy-start.7
  88.8 14.1 %copy-start.9 = (f32[512,128]{1,0:T(8,128)}, f32[512,128]{1,0:T(8,128)S(1)}, u32[]{:S(2)}) copy-start(f32[512,128]{1,0:T(8,128)S(1)} %get-tuple-element.29) | copy-start | bytes 786436
  88.8 14.1 %copy-start.14 = (f32[4,512,128]{2,1,0:T(8,128)}, f32[4,512,128]{2,1,0:T(8,128)S(1)}, u32[]{:S(2)}) copy-start(f32[4,512,128]{2,1,0:T(8,128)S(1)} %get-tuple-element.27.refs_4_) | copy-start | bytes 3145732
  88.8 26.4 %copy-start.18 = (bf16[4,2,18,16,128]{4,3,2,1,0:T(8,128)(2,1)}, bf16[4,2,18,16,128]{4,3,2,1,0:T(8,128)(2,1)S(1)}, u32[]{:S(2)}) copy-start(bf16[4,2,18,16,128]{4,3,2,1,0:T(8,128)(2,1)S(1)} %get-tuple-element.26.refs_3_) | copy-start | bytes 1769476
  118.6 9.8 %all-to-all-start.7 = ((f32[8,64,128]{2,1,0:T(8,128)}), f32[8,64,128]{2,1,0:T(8,128)S(1)}, u32[]{:S(2)}, u32[]{:S(2)}) async-start(f32[8,64,128]{2,1,0:T(8,128)} %copy-done.3), calls=%async_computation.7 | async-start | bytes 524288 | tf_op jit(solution)/shard_map/all_to_all | solution.py:247
  122.0 17.0 %collective-permute-start.4 = (f32[512,128]{1,0:T(8,128)}, f32[512,128]{1,0:T(8,128)S(1)}, u32[]{:S(2)}, u32[]{:S(2)}) collective-permute-start(f32[512,128]{1,0:T(8,128)} %copy-done.9), channel_id=1, source_target_pairs={{0,2},{1,3},{2,0},{3,1},{4,6},{5,7},{6,4},{7,5},{8,10},{9,11},{10,... | collective-permute-start | bytes 786440 | tf_op jit(solution)/shard_map/ppermute | solution.py:297
  128.2 25.1 %collective-permute-start.2 = (f32[512,128]{1,0:T(8,128)}, f32[512,128]{1,0:T(8,128)S(1)}, u32[]{:S(2)}, u32[]{:S(2)}) collective-permute-start(f32[512,128]{1,0:T(8,128)} %copy-done.6), channel_id=1, source_target_pairs={{0,2},{1,3},{2,0},{3,1},{4,6},{5,7},{6,4},{7,5},{8,10},{9,11},{10,... | collective-permute-start | bytes 786440 | tf_op jit(solution)/shard_map/ppermute | solution.py:298
  128.3 32.6 %collective-permute-start.3 = (f32[512,128]{1,0:T(8,128)S(1)}, f32[512,128]{1,0:T(8,128)S(1)}, u32[]{:S(2)}, u32[]{:S(2)}) collective-permute-start(f32[512,128]{1,0:T(8,128)S(1)} %bitcast.20), channel_id=1, source_target_pairs={{0,2},{1,3},{2,0},{3,1},{4,6},{5,7},{6,4},{7,5},{8,10},{9,11},{10,... | collective-permute-start | bytes 786440 | tf_op jit(solution)/shard_map/ppermute | solution.py:304
  141.2 1.0 copy-start.8
  142.1 1.2 copy-start.15
  143.3 1.1 copy-start.19
  147.2 1.4 copy-start
  164.6 13.8 %collective-permute-start.5 = (f32[4,9,128,128]{3,2,1,0:T(8,128)S(1)}, f32[4,9,128,128]{3,2,1,0:T(8,128)S(1)}, u32[]{:S(2)}, u32[]{:S(2)}) collective-permute-start(f32[4,9,128,128]{3,2,1,0:T(8,128)S(1)} %get-tuple-element.34), channel_id=1, source_target_pairs={{0,1},{1,0},{2,3},{3,2},{4,5},{5,4},{6,7},{7,6},{8,9},{9,8},{10,11... | collective-permute-start | bytes 7077896 | tf_op jit(solution)/shard_map/ppermute | solution.py:318
  173.7 4.2 %collective-permute-start.6 = (f32[4,128]{1,0:T(4,128)S(1)}, f32[4,128]{1,0:T(4,128)S(1)}, u32[]{:S(2)}, u32[]{:S(2)}) collective-permute-start(f32[4,128]{1,0:T(4,128)S(1)} %get-tuple-element.35), channel_id=1, source_target_pairs={{0,1},{1,0},{2,3},{3,2},{4,5},{5,4},{6,7},{7,6},{8,9},{9,8},{10,11... | collective-permute-start | bytes 6152 | tf_op jit(solution)/shard_map/ppermute | solution.py:319
  (7 other events, 5.7 us)

commit v2 on v1

v2 whole, which is shorter than its diff:
```python
import math

import jax
import jax.numpy as jnp
from jax import lax
from jax.experimental import pallas as pl
from jax.experimental.pallas import tpu as pltpu
from jax.sharding import PartitionSpec as P

GROUP = 8
EXTRA = 8
VMEM_LIMIT = 12 * 1024 * 1024
f32 = jnp.float32
bf16 = jnp.bfloat16


def shifted_columns(value, width):
    rows = value.shape[0]
    at = lax.broadcasted_iota(jnp.int32, value.shape, 0) % width
    left = jnp.where(at == 0, 0.0, pltpu.roll(value, 1, 0))
    right = jnp.where(at == width - 1, 0.0, pltpu.roll(value, rows - 1, 0))
    return jnp.concatenate([left.astype(bf16), value.astype(bf16), right.astype(bf16)], axis=1)


def clear_border(ref):
    height = ref.shape[1]
    edge = jnp.zeros((ref.shape[0], 1) + ref.shape[2:], ref.dtype)
    ref[:, 0:1] = edge
    ref[:, height - 1 : height] = edge


def rows_from(ref, row_at):
    images, height, width, lanes = ref.shape
    return ref[:, row_at : row_at + height - 2].reshape(images * (height - 2) * width, lanes)


def convolve(ref, value, kernel):
    images, height, width, lanes = ref.shape
    ref[:, 1 : height - 1] = shifted_columns(value, width).reshape(images, height - 2, width, lanes)
    total = None
    for row_at in range(3):
        part = jnp.dot(
            rows_from(ref, row_at),
            kernel[row_at * lanes : (row_at + 1) * lanes],
            preferred_element_type=f32,
        )
        total = part if total is None else total + part
    return total


def split(value):
    high = value.astype(bf16)
    low = (value - high.astype(f32)).astype(bf16)
    return high, low


def times(value, matrix, transpose=False):
    dims = (((1,), (1 if transpose else 0,)), ((), ()))
    high, low = split(value)
    mhigh, mlow = split(matrix)
    dot = lambda a, b: lax.dot_general(a, b, dims, preferred_element_type=f32)
    return dot(high, mhigh) + (dot(low, mhigh) + dot(high, mlow))


VMEM = pl.BlockSpec(memory_space=pltpu.VMEM)
SMEM = pl.BlockSpec(memory_space=pltpu.SMEM)
HBM = pl.BlockSpec(memory_space=pltpu.HBM)


def call(body, outs, *args, ins=None, out_specs=None, scratch=(), flops=0, aliases=None, name=None):
    size = sum(a.size * a.dtype.itemsize for a in args)
    size += sum(math.prod(o.shape) * jnp.dtype(o.dtype).itemsize for o in outs)
    return pl.pallas_call(
        body,
        out_shape=tuple(outs),
        in_specs=list(ins) if ins else [VMEM] * len(args),
        out_specs=tuple(out_specs) if out_specs else (VMEM,) * len(outs),
        scratch_shapes=list(scratch),
        input_output_aliases=aliases or {},
        cost_estimate=pl.CostEstimate(flops=flops, bytes_accessed=size, transcendentals=0),
        compiler_params=pltpu.CompilerParams(vmem_limit_bytes=VMEM_LIMIT),
        name=name,
    )(*args)


def shape(dims, dtype=f32):
    return pltpu.VMEM(dims, dtype)


def stored(dims, dtype=f32):
    return pltpu.HBM(dims, dtype)


def in_hbm(value):
    return pltpu.with_memory_space_constraint(value, pltpu.HBM)


def coarse_body(weights, out, centre, sem):
    copy = pltpu.make_async_copy(weights.at[:, 4], centre, sem)
    copy.start()
    copy.wait()
    total = centre[0].astype(f32)
    for index in range(1, centre.shape[0]):
        total = total + centre[index].astype(f32)
    out[...] = 0.25 * total


def load_body(
    weights, images, biases, end_grad, weights_out, images_out, biases_out, end_out, sems
):
    pairs = [(weights, weights_out), (images, images_out), (biases, biases_out)]
    pairs.append((end_grad, end_out))
    copies = [pltpu.make_async_copy(a, b, sems.at[at]) for at, (a, b) in enumerate(pairs)]
    for copy in copies:
        copy.start()
    for copy in copies:
        copy.wait()


def flip_body(weights, transposed):
    taps, channels = weights.shape[1], weights.shape[2]
    for index in range(weights.shape[0]):
        for tap in range(taps):
            flipped = weights[index, taps - 1 - tap].astype(f32).T
            transposed[index, tap * channels : (tap + 1) * channels] = flipped.astype(bf16)


def start_body(images, own, before, weights, biases, payload, ref):
    clear_border(ref)
    field = images[...]
    state = field + times(field, before[...])
    for index in range(weights.shape[0]):
        state = state + 0.25 * jnp.tanh(
            convolve(ref, state, weights.at[index]) + biases[index : index + 1]
        )
    matrix = own[...]
    residual = state - (field + times(field, matrix))
    part = residual.shape[0] // GROUP
    for index in range(GROUP):
        payload[index, :part] = residual[index * part : (index + 1) * part]
        payload[index, part:] = matrix


def ends_body(images, end_grad, own, before, after, starts_out, ends_out, back_out):
    field = images[...]
    starts_out[...] = field + times(field, before[...])
    field = end_grad[...]
    ends_out[...] = field + times(field, after[...], True)
    back_out[...] = field + times(field, own[...], True)


def total_body(pieces, payload, locals_out):
    part = locals_out.shape[1]
    error = pieces[0, :part]
    product = pieces[0, part:]
    for index in range(1, GROUP):
        matrix = pieces[index, part:]
        locals_out[index] = error
        error = error + (times(error, matrix) + pieces[index, :part])
        product = product + (matrix + times(product, matrix))
    payload[:part] = error
    payload[part:] = product


def pair_body(part, spot, mine, theirs, out):
    upper = spot[1] == 1
    early = jnp.where(upper, theirs[...], mine[...])
    late = jnp.where(upper, mine[...], theirs[...])
    out[...] = early + (times(early, late[part:]) + late)


def back_pair_body(part, spot, mine, theirs, mine_full, theirs_full, out):
    upper = spot[1] == 1
    early = jnp.where(upper, mine[...], theirs[...])
    late = jnp.where(upper, theirs[...], mine[...])
    matrix = jnp.where(upper, theirs_full[part:], mine_full[part:])
    out[...] = early + (times(early, matrix, True) + late)


def products_body(part, pieces, prefix_out, suffix_out):
    before = pieces[0, part:]
    after = pieces[GROUP - 1, part:]
    for index in range(1, GROUP):
        prefix_out[index] = before
        suffix_out[GROUP - 1 - index] = after
        if index < GROUP - 1:
            matrix = pieces[index, part:]
            before = before + (matrix + times(before, matrix))
            matrix = pieces[GROUP - 1 - index, part:]
            after = after + (matrix + times(matrix, after))


def back_total_body(part, pieces, first, payload, locals_out):
    error = pieces[GROUP - 1]
    for index in range(GROUP - 2, -1, -1):
        locals_out[index] = error
        error = error + (times(error, first[index, part:], True) + pieces[index])
    payload[...] = error


def replay_body(spot, theirs, far1, far2, far3, locals_in, prefix_in, out, prefix, sem):
    copy = pltpu.make_async_copy(prefix_in, prefix, sem)
    copy.start()
    part = out.shape[1]
    error = jnp.where(spot[0] >= 3, far3[:part], 0.0)
    for distance, group in ((2, far2), (1, far1)):
        longer = error + (times(error, group[part:]) + group[:part])
        error = jnp.where(spot[0] >= distance, longer, error)
    longer = error + (times(error, theirs[part:]) + theirs[:part])
    error = jnp.where(spot[1] == 1, longer, error)
    out[0] = error
    copy.wait()
    for index in range(1, GROUP):
        out[index] = error + (times(error, prefix[index]) + locals_in[index])


def back_replay_body(
    spot, theirs, far1, far2, far3, theirs_full, full1, full2, locals_in, suffix_in,
    out, suffix, sem,
):
    copy = pltpu.make_async_copy(suffix_in, suffix, sem)
    copy.start()
    part = out.shape[1]
    error = far3[...]
    for group, full in ((far2, full2), (far1, full1)):
        error = error + (times(error, full[part:], True) + group[...])
    longer = error + (times(error, theirs_full[part:], True) + theirs[...])
    error = jnp.where(spot[1] == 0, longer, error)
    out[GROUP - 1] = error
    copy.wait()
    for index in range(GROUP - 1):
        out[index] = error + (times(error, suffix[index], True) + locals_in[index])


def forward_sweep(state, weights, biases, ref, inputs, slopes, stores, fetches=None):
    for index in range(weights.shape[0]):
        if fetches is not None:
            fetches[index].wait()
        activation = jnp.tanh(convolve(ref, state, weights.at[index]) + biases[index : index + 1])
        channels = state.shape[1]
        inputs[index] = ref[:, :, :, channels : 2 * channels]
        slopes[index] = 0.25 * (1.0 - activation * activation)
        for store in stores[index]:
            store.start()
        state = state + 0.25 * activation
    return state


def sweep_stores(inputs, slopes, inputs_out, slopes_out, sems):
    blocks = inputs.shape[0]
    return [
        [
            pltpu.make_async_copy(inputs.at[index], inputs_out.at[index], sems.at[index]),
            pltpu.make_async_copy(slopes.at[index], slopes_out.at[index], sems.at[blocks + index]),
        ]
        for index in range(blocks)
    ]


def middle_body(
    error, starts_in, ends_in, back_in, weights_in, transposed_in, biases_in,
    corrected_out, ends_out, inputs_out, slopes_out, residual_out,
    ref, corrected, ends, inputs, slopes, starts, ends_adj, back, weights, transposed, biases,
    sems, loads,
):
    blocks = weights.shape[0]
    pairs = [(starts_in, starts), (biases_in, biases)]
    pairs += [(weights_in.at[index], weights.at[index]) for index in range(blocks)]
    pairs += [(transposed_in, transposed), (ends_in, ends_adj), (back_in, back)]
    fetches = [pltpu.make_async_copy(a, b, loads.at[at]) for at, (a, b) in enumerate(pairs)]
    for fetch in fetches:
        fetch.start()
    clear_border(ref)
    stores = sweep_stores(inputs, slopes, inputs_out, slopes_out, sems)
    fetches[0].wait()
    fetches[1].wait()
    corrected[...] = starts[...] + error[...]
    first = pltpu.make_async_copy(corrected, corrected_out, sems.at[2 * blocks])
    first.start()
    ends[...] = forward_sweep(
        corrected[...], weights, biases, ref, inputs, slopes, stores, fetches[2 : 2 + blocks]
    )
    for fetch in fetches[2 + blocks :]:
        fetch.wait()
    last = pltpu.make_async_copy(ends, ends_out, sems.at[2 * blocks + 1])
    last.start()
    adjoint = ends_adj[...]
    for index in reversed(range(blocks)):
        change = slopes[index] * adjoint
        adjoint = adjoint + convolve(ref, change, transposed.at[index])
    residual_out[...] = adjoint - back[...]
    for store in sum(stores, [first, last]):
        store.wait()


def again_body(corrected, weights, biases, inputs_out, slopes_out, ref, inputs, slopes, sems):
    clear_border(ref)
    stores = sweep_stores(inputs, slopes, inputs_out, slopes_out, sems)
    forward_sweep(corrected[...], weights, biases, ref, inputs, slopes, stores)
    for store in sum(stores, []):
        store.wait()


def finish_block(scale, adjoint, transposed, inputs, slope, ref):
    channels = adjoint.shape[1]
    change = slope * adjoint
    adjoint = adjoint + convolve(ref, change, transposed)
    offset = jnp.sum(change, axis=0, keepdims=True) * scale
    moved = rows_from(ref, 1)
    field = jnp.concatenate([rows_from(inputs, row_at) for row_at in range(3)], axis=1)
    kernel = scale * lax.dot_general(
        field, moved, (((0,), (0,)), ((), ())), preferred_element_type=f32
    )
    taps = [
        kernel[
            row_at * channels : (row_at + 1) * channels,
            (2 - col_at) * channels : (3 - col_at) * channels,
        ]
        for row_at in range(3)
        for col_at in range(3)
    ]
    taps.append(jnp.broadcast_to(offset, (EXTRA, channels)))
    return adjoint, jnp.concatenate(taps, axis=0)


def final_body(scale, moving, transposed, inputs, slopes, adjoint_out, kernels_out, ref):
    clear_border(ref)
    adjoint = moving[...]
    for index in reversed(range(transposed.shape[0])):
        adjoint, kernels_out[index] = finish_block(
            scale, adjoint, transposed.at[index], inputs.at[index], slopes[index], ref
        )
    adjoint_out[...] = adjoint


def other_body(
    scale, first, last, moving, transposed, inputs, slopes, kernels, adjoint_out, kernels_out, ref
):
    clear_border(ref)
    adjoint = moving[...]
    for index in reversed(range(first, last)):
        adjoint, kernel = finish_block(
            scale, adjoint, transposed.at[index], inputs.at[index], slopes[index], ref
        )
        kernels_out[index - first] = kernels[index] + kernel
    if adjoint_out is not None:
        adjoint_out[...] = adjoint


def join_body(first, mine, theirs, late_offsets, kernels_out, offsets_out, total, sems):
    size = kernels_out.shape[1]
    count = mine.shape[0]
    part = size // 3
    copies = []
    for index in range(count):
        for at in range(3):
            rows = pl.ds(at * part, part)
            total[index, rows] = mine[index, rows] + theirs[index, rows]
            copy = pltpu.make_async_copy(
                total.at[index, rows], kernels_out.at[first + index, rows], sems.at[3 * index + at]
            )
            copy.start()
            copies.append(copy)
    offsets_out[:count] = mine[:, size] + theirs[:, size]
    if late_offsets is not None:
        offsets_out[count:] = late_offsets[...]
    for copy in copies:
        copy.wait()


def shards(images, weights, biases, end_grad):
    count, height, width, channels = images.shape
    blocks = weights.shape[0]
    rows = count * height * width
    part = rows // GROUP
    layers = lax.axis_size("layer")
    outer = layers // GROUP
    near = [[a * GROUP + b for b in range(GROUP)] for a in range(outer)]
    pair = [(i, i ^ GROUP) for i in range(layers)]
    around = [[(i, (i + 2 * GROUP * d) % layers) for i in range(layers)] for d in (1, 2, 3)]
    down = [[(i, i - 2 * GROUP * d) for i in range(2 * GROUP * d, layers)] for d in (1, 2, 3)]
    dp = lax.axis_size("dp")
    partner = [(i, (i + dp // 2) % dp) for i in range(dp)]
    sibling = [(i, i ^ 1) for i in range(dp)]
    spot = lax.axis_index("layer").astype(jnp.int32)
    spot = jnp.stack([spot >> 4, (spot >> 3) & 1])
    scale = 1.0 / (count * dp)
    per_conv = 2 * rows * 9 * channels * channels
    half = blocks // 2

    def exchange(value, groups):
        return lax.all_to_all(value, "layer", 0, 0, axis_index_groups=groups)

    plane = shape((rows, channels))
    kept = stored((rows, channels))
    matrix = shape((channels, channels))
    pieces_shape = shape((GROUP, part, channels))
    pieces_kept = stored((GROUP, part, channels))
    both_kept = stored((GROUP, part + channels, channels))
    both = shape((part + channels, channels))
    piece = shape((part, channels))
    matrices = stored((GROUP, channels, channels))
    taps_shape = shape((blocks, 9, channels, channels), bf16)
    sweep_shape = (blocks, 9 * channels, channels)
    inputs_dims = (blocks, count, height + 2, width, channels)
    slopes_dims = (blocks, rows, channels)
    offsets_shape = shape((blocks, channels))
    kernels_shape = shape((blocks, 9 * channels + EXTRA, channels))
    half_kernels = shape((half, 9 * channels + EXTRA, channels))
    result = jax.ShapeDtypeStruct((rows, channels), f32)
    gradients = jax.ShapeDtypeStruct((blocks, 9 * channels, channels), f32)
    half_offsets = jax.ShapeDtypeStruct((half, channels), f32)
    ref = pltpu.VMEM((count, height + 2, width, 3 * channels), bf16)
    dma = pltpu.SemaphoreType.DMA
    sweep_scratch = [pltpu.VMEM(inputs_dims, bf16), pltpu.VMEM(slopes_dims, f32)]

    flat = weights.reshape(blocks, 9, channels, channels)
    kernels = weights.reshape(sweep_shape)
    (own,) = call(
        coarse_body, [matrix], in_hbm(flat), ins=[HBM],
        scratch=[pltpu.VMEM((blocks, channels, channels), bf16), dma(())], name="coarse",
    )
    before = lax.ppermute(own, "layer", [(i, i + 1) for i in range(layers - 1)])
    after = lax.ppermute(own, "layer", [(i + 1, i) for i in range(layers - 1)])
    held, field, offsets, cotangent = call(
        load_body, [taps_shape, plane, offsets_shape, plane],
        in_hbm(flat), in_hbm(images.reshape(rows, channels)), in_hbm(biases),
        in_hbm(end_grad.reshape(rows, channels)),
        ins=[HBM] * 4, scratch=[dma((4,))], name="load",
    )

    (payload,) = call(
        start_body, [both_kept], field, own, before, held.reshape(sweep_shape), offsets,
        scratch=[ref], flops=blocks * per_conv, name="start",
    )
    first = exchange(payload, near)
    first, after = lax.optimization_barrier((first, after))
    starts, ends_adj, back = call(
        ends_body, [kept] * 3, field, cotangent, own, before, after, name="ends"
    )
    (transposed,) = call(flip_body, [stored(sweep_shape, bf16)], flat, name="flip")
    full, prefixes = call(total_body, [both, pieces_shape], first, name="total")
    their_full = lax.ppermute(full, "layer", pair)
    (pair_full,) = call(
        lambda *refs: pair_body(part, *refs), [both], spot, full, their_full,
        ins=[SMEM, VMEM, VMEM], name="pair",
    )
    around_full = [lax.ppermute(pair_full, "layer", to) for to in around]
    prefix, suffix = call(
        lambda *refs: products_body(part, *refs), [matrices] * 2, first, name="products"
    )
    replay_scratch = [pltpu.VMEM((GROUP, channels, channels), f32), dma(())]
    (error,) = call(
        replay_body, [pieces_kept], spot, their_full, *around_full, prefixes, in_hbm(prefix),
        ins=[SMEM] + [VMEM] * 5 + [HBM], scratch=replay_scratch, name="replay",
    )
    error, suffix, ends_adj, back, transposed, starts = lax.optimization_barrier(
        (error, suffix, ends_adj, back, transposed, starts)
    )
    error = exchange(error, near).reshape(rows, channels)

    corrected, interval_ends, inputs, slopes, adj_residual = call(
        middle_body, [kept, result, stored(inputs_dims, bf16), stored(slopes_dims), kept],
        error, in_hbm(starts), in_hbm(ends_adj), in_hbm(back), in_hbm(kernels),
        in_hbm(transposed), in_hbm(biases),
        ins=[VMEM] + [HBM] * 6, out_specs=[HBM, HBM, HBM, HBM, VMEM],
        scratch=[ref] + [pltpu.VMEM((rows, channels), f32)] * 2 + sweep_scratch
        + [pltpu.VMEM((rows, channels), f32)] * 3 + [pltpu.VMEM(sweep_shape, bf16)] * 2
        + [pltpu.VMEM((blocks, channels), f32), dma((2 * blocks + 2,)), dma((blocks + 5,))],
        flops=2 * blocks * per_conv, name="middle",
    )
    other_corrected = lax.ppermute(corrected, "dp", partner)
    pieces = exchange(adj_residual.reshape(GROUP, part, channels), near)
    total, prefixes = call(
        lambda *refs: back_total_body(part, *refs), [piece, pieces_kept], pieces, first,
        name="back_total",
    )
    total, other_corrected = lax.optimization_barrier((total, other_corrected))
    their_total = lax.ppermute(total, "layer", pair)
    (pair_total,) = call(
        lambda *refs: back_pair_body(part, *refs), [piece],
        spot, total, their_total, full, their_full, ins=[SMEM] + [VMEM] * 4, name="back_pair",
    )
    down_total = [lax.ppermute(pair_total, "layer", to) for to in down]
    other_inputs, other_slopes = call(
        again_body, [stored(inputs_dims, bf16), stored(slopes_dims)],
        other_corrected, kernels, offsets, out_specs=[HBM] * 2,
        scratch=[ref] + sweep_scratch + [dma((2 * blocks,))], flops=blocks * per_conv, name="again",
    )
    (adj_error,) = call(
        back_replay_body, [pieces_kept], spot, their_total, *down_total, their_full,
        around_full[2], around_full[1], prefixes, in_hbm(suffix),
        ins=[SMEM] + [VMEM] * 8 + [HBM], scratch=replay_scratch, name="back_replay",
    )
    adj_error, other_inputs, other_slopes = lax.optimization_barrier(
        (adj_error, other_inputs, other_slopes)
    )
    moving = ends_adj + exchange(adj_error, near).reshape(rows, channels)
    other_moving = lax.ppermute(moving, "dp", partner)
    adjoint, kernel_part = call(
        lambda *refs: final_body(scale, *refs), [result, kernels_shape],
        moving, transposed, inputs, slopes,
        scratch=[ref], flops=2 * blocks * per_conv, name="final",
    )
    other_moving, late = call(
        lambda *refs: other_body(scale, half, blocks, *refs), [plane, half_kernels],
        other_moving, transposed, other_inputs, other_slopes, kernel_part,
        scratch=[ref], flops=blocks * per_conv, name="other_late",
    )
    their_late = lax.ppermute(late, "dp", sibling)
    (early,) = call(
        lambda moving, a, b, c, d, out, ref: other_body(
            scale, 0, half, moving, a, b, c, d, None, out, ref
        ),
        [half_kernels], other_moving, transposed, other_inputs, other_slopes, kernel_part,
        scratch=[ref], flops=blocks * per_conv, name="other_early",
    )
    their_early = lax.ppermute(early, "dp", sibling)
    join_scratch = [pltpu.VMEM((half, 9 * channels, channels), f32), dma((3 * half,))]
    weight_grad, late_offsets = call(
        lambda mine, theirs, *refs: join_body(half, mine, theirs, None, *refs),
        [gradients, half_offsets], late, their_late,
        out_specs=[HBM, VMEM], scratch=join_scratch, name="join_late",
    )
    weight_grad, bias_grad = call(
        lambda mine, theirs, offsets, _, *refs: join_body(0, mine, theirs, offsets, *refs),
        [gradients, jax.ShapeDtypeStruct((blocks, channels), f32)],
        early, their_early, late_offsets, weight_grad,
        ins=[VMEM, VMEM, VMEM, HBM], out_specs=[HBM, VMEM], scratch=join_scratch,
        aliases={3: 0}, name="join_early",
    )
    dims = (1, count, height, width, channels)
    return (
        interval_ends.reshape(dims),
        adjoint.reshape(dims),
        weight_grad.reshape(blocks, 3, 3, channels, channels),
        bias_grad,
    )


def solution(mesh):
    in_specs = (
        P("dp", None, None, None),
        P("layer", None, None, None, None),
        P("layer", None),
        P("dp", None, None, None),
    )
    out_specs = (
        P("layer", "dp", None, None, None),
        P("layer", "dp", None, None, None),
        P("layer", None, None, None, None),
        P("layer", None),
    )
    return jax.shard_map(shards, mesh=mesh, in_specs=in_specs, out_specs=out_specs, check_vma=False)
```

time: 181 us -> 148 us (0.82)
  blocking collectives: 46.9 us -> 21.9 us
  local copies, waits for them, and re-layouts: 16.1 us -> 0.04 us
  waiting for transfers between devices: 40.7 us -> 26.2 us
  starting transfers between devices: 47.1 us -> 60.2 us
  Pallas kernels: 26.3 us -> 37.8 us
  other arithmetic: 2.4 us -> 0.1 us
    all_to_all x4 -> x2, blocking collectives: 46.9 us -> 21.9 us  [exchange(): return lax.all_to_all(value, 'layer', 0, 0, axis_index_groups=groups)]
    ppermute x4 -> x11, starting transfers between devices: 17.7 us -> 38.9 us  [the longest x1 13.5 us: shards(): their_total = lax.ppermute(total, 'layer', pair)]
    all_to_all x4 -> x2, waiting for transfers between devices: 17.4 us -> 0.01 us  [exchange(): return lax.all_to_all(value, 'layer', 0, 0, axis_index_groups=groups)]
    unnamed x40 -> x18, local copies, waits for them, and re-layouts: 13.5 us -> 0.04 us
    pallas_call x13 -> x19, Pallas kernels: 26.3 us -> 37.8 us  [call(): pl.pallas_call(body, out_shape=tuple(outs), in_specs=list(ins) if ins els...]
    all_to_all x4 -> x2, starting transfers between devices: 17.9 us -> 9.48 us  [exchange(): return lax.all_to_all(value, 'layer', 0, 0, axis_index_groups=groups)]
    ppermute x1, waiting for transfers between devices: 3.32 us -> 10.4 us  [shards(): after = lax.ppermute(own, 'layer', [(i + 1, i) for i in range(layers - 1)])]
    ppermute x4 -> x11, waiting for transfers between devices: 16.4 us -> 12.5 us  [the longest x1 6.05 us: shards(): other_moving = lax.ppermute(moving, 'dp', partner)]
  transfers between devices with their start and end apart: 11 -> 16, of which waited for: 8 -> 10; matrix products, arithmetic and copies ran while one was open for 0% -> 0% of each run, Pallas kernels for 4% -> 11%
where the time goes in v2:
time: 148 us; the launch traced here: 147 us
  starting transfers between devices  60.2 us (41%)
  Pallas kernels  37.8 us (26%)
  waiting for transfers between devices  26.2 us (18%)
  blocking collectives  21.9 us (15%)
    pallas_call x19, Pallas kernels, call(): pl.pallas_call(body, out_shape=tuple(outs), in_specs=list(ins) if ins els...  37.8 us
    all_to_all x2, blocking collectives, exchange(): return lax.all_to_all(value, 'layer', 0, 0, axis_index_groups=groups)  21.9 us
    ppermute x1, starting transfers between devices, shards(): their_total = lax.ppermute(total, 'layer', pair)  13.5 us
    ppermute x1, starting transfers between devices, shards(): their_late = lax.ppermute(late, 'dp', sibling)  11.3 us
    ppermute x1, waiting for transfers between devices, shards(): after = lax.ppermute(own, 'layer', [(i + 1, i) for i in range(layers - 1)])  10.4 us
    all_to_all x2, starting transfers between devices, exchange(): return lax.all_to_all(value, 'layer', 0, 0, axis_index_groups=groups)  9.48 us
    ppermute x1, starting transfers between devices, shards(): other_corrected = lax.ppermute(corrected, 'dp', partner)  6.59 us
    ppermute x3, starting transfers between devices, shards(): around_full = [lax.ppermute(pair_full, 'layer', to) for to in around]  6.08 us
  transfers between devices with their start and end apart: 16, of which 10 were waited for; matrix products, arithmetic and copies ran while one was open for 0% of the time, Pallas kernels for 11%

profile of v2, /device:TPU:1, one launch (start us, length us, event | category | flops | bytes accessed | tf_op | source)
XLA Modules:
  0.0 147.2 jit_solution(4234104273581909150)
XLA Ops:
  1.6 3.9 %collective-permute-start = (f32[128,128]{1,0:T(8,128)S(1)}, f32[128,128]{1,0:T(8,128)S(1)}, u32[]{:S(2)}, u32[]{:S(2)}) collective-permute-start(f32[128,128]{1,0:T(8,128)S(1)} %coarse.1.own), channel_id=1, source_target_pairs={{0,4},{4,8},{8,12},{12,16},{16,20},{20,24},{24,28},{28,32},{32,36}... | collective-permute-start | bytes 196616 | tf_op jit(solution)/shard_map/ppermute | solution.py:423
  7.0 3.3 %start.1 = f32[8,192,128]{2,1,0:T(8,128)} custom-call(f32[512,128]{1,0:T(8,128)S(1)} %get-tuple-element.45.images, f32[128,128]{1,0:T(8,128)S(1)} %coarse.1.own, f32[128,128]{1,0:T(8,128)S(1)} %collective-permute-done.before, bf16[4,1152,128]{2,1,0:T(8,128)(2,1)S(1)} %bitcast.19, f32[4,128]{1,0:T(4,128)S(1)} %get-tuple-element.47.biases), custom_call_target="tpu_custom_call" | custom-call | flops 603979776 | bytes 2361344 | tf_op jit(solution)/shard_map/start/pallas_call | solution.py:73
  10.3 5.9 %all-to-all-start = ((f32[8,192,128]{2,1,0:T(8,128)}), f32[8,192,128]{2,1,0:T(8,128)S(1)}, u32[]{:S(2)}, u32[]{:S(2)}) async-start(f32[8,192,128]{2,1,0:T(8,128)} %start.1), calls=%async_computation | async-start | bytes 1572864 | tf_op jit(solution)/shard_map/all_to_all | solution.py:392
  17.6 10.4 %collective-permute-done.1.after = f32[128,128]{1,0:T(8,128)S(1)} collective-permute-done((f32[128,128]{1,0:T(8,128)S(1)}, f32[128,128]{1,0:T(8,128)S(1)}, u32[]{:S(2)}, u32[]{:S(2)}) %collective-permute-start.1) | collective-permute-done | bytes 65568 | tf_op jit(solution)/shard_map/ppermute | solution.py:424
  29.2 3.3 %collective-permute-start.2 = (f32[192,128]{1,0:T(8,128)S(1)}, f32[192,128]{1,0:T(8,128)S(1)}, u32[]{:S(2)}, u32[]{:S(2)}) collective-permute-start(f32[192,128]{1,0:T(8,128)S(1)} %get-tuple-element.49.refs_1_.refs_3_), channel_id=1, source_target_pairs={{0,32},{4,36},{8,40},{12,44},{16,48},{20,52},{24,56},{28,60},{32,0... | collective-permute-start | bytes 294920 | tf_op jit(solution)/shard_map/ppermute | solution.py:443
  32.5 1.9 %collective-permute-done.2.refs_2_.theirs.refs_4_.theirs_full = f32[192,128]{1,0:T(8,128)S(1)} collective-permute-done((f32[192,128]{1,0:T(8,128)S(1)}, f32[192,128]{1,0:T(8,128)S(1)}, u32[]{:S(2)}, u32[]{:S(2)}) %collective-permute-start.2) | collective-permute-done | bytes 98336 | tf_op jit(solution)/shard_map/ppermute | solution.py:443
  35.2 5.3 %collective-permute-start.5 = (f32[192,128]{1,0:T(8,128)S(1)}, f32[192,128]{1,0:T(8,128)S(1)}, u32[]{:S(2)}, u32[]{:S(2)}) collective-permute-start(f32[192,128]{1,0:T(8,128)S(1)} %pair.1), channel_id=1, source_target_pairs={{0,192},{4,196},{8,200},{12,204},{16,208},{20,212},{24,216},{28,22... | collective-permute-start | bytes 294920 | tf_op jit(solution)/shard_map/ppermute | solution.py:448
  42.6 1.9 %products.1 = (f32[8,128,128]{2,1,0:T(8,128)}, f32[8,128,128]{2,1,0:T(8,128)}) custom-call(f32[8,192,128]{2,1,0:T(8,128)S(1)} %all-to-all-done.pieces.refs_0_.refs_1_), custom_call_target="tpu_custom_call" | custom-call | bytes 1835008 | tf_op jit(solution)/shard_map/products/pallas_call | solution.py:73
  46.3 3.0 %replay.1 = f32[8,64,128]{2,1,0:T(8,128)} custom-call(s32[2]{0:T(128)S(1)} %pad_add_fusion.refs_0_.spot, f32[192,128]{1,0:T(8,128)S(1)} %collective-permute-done.2.refs_2_.theirs.refs_4_.theirs_full, f32[192,128]{1,0:T(8,128)S(1)} %collective-permute-done.3.far1, f32[192,128]{1,0:T(8,128)S(1)} %collective-permute-done.4.far2.full2, ...), custom_call_target="tpu_custom_call" | custom-call | bytes 1441800 | tf_op jit(solution)/shard_map/replay/pallas_call | solution.py:73
  49.2 12.0 %all_to_all.20 = f32[8,64,128]{2,1,0:T(8,128)S(1)} all-to-all(f32[8,64,128]{2,1,0:T(8,128)} %replay.1), channel_id=1, replica_groups={{0,4,8,12,16,20,24,28},{32,36,40,44,48,52,56,60},{64,68,72,76,80,84,88,..., dimensions={0} | all-to-all | bytes 524288 | tf_op jit(solution)/shard_map/all_to_all | solution.py:392
  61.3 6.2 %middle.1 = (f32[512,128]{1,0:T(8,128)}, f32[512,128]{1,0:T(8,128)}, bf16[4,2,18,16,128]{4,3,2,1,0:T(8,128)(2,1)}, f32[4,512,128]{2,1,0:T(8,128)}, f32[512,128]{1,0:T(8,128)}) custom-call(f32[512,128]{1,0:T(8,128)S(1)} %bitcast.20, f32[512,128]{1,0:T(8,128)} %get-tuple-element.59.starts_in, f32[512,128]{1,0:T(8,128)} %get-tuple-element.60.ends_in, ...), custom_call_target="tpu_custom_call" | custom-call | flops 1207959552 | bytes 5834752 | tf_op jit(solution)/shard_map/middle/pallas_call | solution.py:73
  67.4 3.6 %all-to-all-start.2 = ((f32[8,64,128]{2,1,0:T(8,128)}), f32[8,64,128]{2,1,0:T(8,128)S(1)}, u32[]{:S(2)}, u32[]{:S(2)}) async-start(f32[8,64,128]{2,1,0:T(8,128)} %bitcast.22), calls=%async_computation.2 | async-start | bytes 524288 | tf_op jit(solution)/shard_map/all_to_all | solution.py:392
  71.0 6.6 %collective-permute-start.6 = (f32[512,128]{1,0:T(8,128)}, f32[512,128]{1,0:T(8,128)S(1)}, u32[]{:S(2)}, u32[]{:S(2)}) collective-permute-start(f32[512,128]{1,0:T(8,128)} %get-tuple-element.66), channel_id=1, source_target_pairs={{0,2},{1,3},{2,0},{3,1},{4,6},{5,7},{6,4},{7,5},{8,10},{9,11},{10,... | collective-permute-start | bytes 786440 | tf_op jit(solution)/shard_map/ppermute | solution.py:472
  77.6 1.8 %back_total.1 = (f32[64,128]{1,0:T(8,128)S(1)}, f32[8,64,128]{2,1,0:T(8,128)}) custom-call(f32[8,64,128]{2,1,0:T(8,128)S(1)} %all-to-all-done.2.refs_0_, f32[8,192,128]{2,1,0:T(8,128)S(1)} %all-to-all-done.pieces.refs_0_.refs_1_), custom_call_target="tpu_custom_call" | custom-call | bytes 1343488 | tf_op jit(solution)/shard_map/back_total/pallas_call | solution.py:73
  79.4 3.3 %collective-permute-done.6.corrected = f32[512,128]{1,0:T(8,128)S(1)} collective-permute-done((f32[512,128]{1,0:T(8,128)}, f32[512,128]{1,0:T(8,128)S(1)}, u32[]{:S(2)}, u32[]{:S(2)}) %collective-permute-start.6) | collective-permute-done | bytes 262176 | tf_op jit(solution)/shard_map/ppermute | solution.py:472
  82.7 13.5 %collective-permute-start.7 = (f32[64,128]{1,0:T(8,128)S(1)}, f32[64,128]{1,0:T(8,128)S(1)}, u32[]{:S(2)}, u32[]{:S(2)}) collective-permute-start(f32[64,128]{1,0:T(8,128)S(1)} %get-tuple-element.67.refs_1_), channel_id=1, source_target_pairs={{0,32},{4,36},{8,40},{12,44},{16,48},{20,52},{24,56},{28,60},{32,0... | collective-permute-start | bytes 98312 | tf_op jit(solution)/shard_map/ppermute | solution.py:479
  102.3 2.9 %again.1 = (bf16[4,2,18,16,128]{4,3,2,1,0:T(8,128)(2,1)}, f32[4,512,128]{2,1,0:T(8,128)}) custom-call(f32[512,128]{1,0:T(8,128)S(1)} %collective-permute-done.6.corrected, bf16[4,1152,128]{2,1,0:T(8,128)(2,1)S(1)} %bitcast.18, f32[4,128]{1,0:T(4,128)S(1)} %get-tuple-element.47.biases), custom_call_target="tpu_custom_call" | custom-call | flops 603979776 | bytes 3082240 | tf_op jit(solution)/shard_map/again/pallas_call | solution.py:73
  106.0 3.3 %back_replay.1 = f32[8,64,128]{2,1,0:T(8,128)} custom-call(s32[2]{0:T(128)S(1)} %pad_add_fusion.refs_0_.spot, f32[64,128]{1,0:T(8,128)S(1)} %collective-permute-done.7.refs_2_.theirs, f32[64,128]{1,0:T(8,128)S(1)} %collective-permute-done.8.far1, f32[64,128]{1,0:T(8,128)S(1)} %collective-permute-done.9.far2, f32[64,128]{1,0:T(8,128)S(1)} %collective-permute-done.10.far3, ...), custom_call_target="tpu_custom_call" | custom-call | bytes 1474568 | tf_op jit(solution)/shard_map/back_replay/pallas_call | solution.py:73
  109.3 9.9 %all_to_all.21 = f32[8,64,128]{2,1,0:T(8,128)S(1)} all-to-all(f32[8,64,128]{2,1,0:T(8,128)} %back_replay.1), channel_id=1, replica_groups={{0,4,8,12,16,20,24,28},{32,36,40,44,48,52,56,60},{64,68,72,76,80,84,88,..., dimensions={0} | all-to-all | bytes 524288 | tf_op jit(solution)/shard_map/all_to_all | solution.py:392
  119.8 2.8 %final.1 = (f32[512,128]{1,0:T(8,128)}, f32[4,1160,128]{2,1,0:T(8,128)S(1)}) custom-call(f32[512,128]{1,0:T(8,128)S(1)} %bitcast_add_fusion.refs_0_, bf16[4,1152,128]{2,1,0:T(8,128)(2,1)S(1)} %copy-done.2, bf16[4,2,18,16,128]{4,3,2,1,0:T(8,128)(2,1)S(1)} %copy-done.7, f32[4,512,128]{2,1,0:T(8,128)S(1)} %copy-done.6), custom_call_target="tpu_custom_call" | custom-call | flops 1207959552 | bytes 5718016 | tf_op jit(solution)/shard_map/final/pallas_call | solution.py:73
  122.6 6.1 %collective-permute-done.11.refs_0_ = f32[512,128]{1,0:T(8,128)S(1)} collective-permute-done((f32[512,128]{1,0:T(8,128)S(1)}, f32[512,128]{1,0:T(8,128)S(1)}, u32[]{:S(2)}, u32[]{:S(2)}) %collective-permute-start.11) | collective-permute-done | bytes 262176 | tf_op jit(solution)/shard_map/ppermute | solution.py:499
  129.9 11.3 %collective-permute-start.13 = (f32[2,1160,128]{2,1,0:T(8,128)S(1)}, f32[2,1160,128]{2,1,0:T(8,128)S(1)}, u32[]{:S(2)}, u32[]{:S(2)}) collective-permute-start(f32[2,1160,128]{2,1,0:T(8,128)S(1)} %get-tuple-element.81.mine), channel_id=1, source_target_pairs={{0,1},{1,0},{2,3},{3,2},{4,5},{5,4},{6,7},{7,6},{8,9},{9,8},{10,11... | collective-permute-start | bytes 3563528 | tf_op jit(solution)/shard_map/ppermute | solution.py:510
  142.2 1.5 %collective-permute-done.13.theirs = f32[2,1160,128]{2,1,0:T(8,128)S(1)} collective-permute-done((f32[2,1160,128]{2,1,0:T(8,128)S(1)}, f32[2,1160,128]{2,1,0:T(8,128)S(1)}, u32[]{:S(2)}, u32[]{:S(2)}) %collective-permute-start.13) | collective-permute-done | bytes 1187872 | tf_op jit(solution)/shard_map/ppermute | solution.py:510
  145.4 1.6 %join_early.1 = (f32[4,1152,128]{2,1,0:T(8,128)}, f32[4,128]{1,0:T(4,128)}) custom-call(f32[2,1160,128]{2,1,0:T(8,128)S(1)} %other_early.1.mine, f32[2,1160,128]{2,1,0:T(8,128)S(1)} %collective-permute-done.12.theirs, f32[2,128]{1,0:T(2,128)S(1)} %get-tuple-element.82.offsets, f32[4,1152,128]{2,1,0:T(8,128)} %get-tuple-element.83._), custom_call_target="tpu_custom_call", output_to_operand_aliasing={{0}: (3, {})} | custom-call | bytes 7097344 | tf_op jit(solution)/shard_map/join_early/pallas_call | solution.py:73
  (49 shorter events, 20.8 us)
Async XLA Ops:
  1.6 5.4 %collective-permute-start = (f32[128,128]{1,0:T(8,128)S(1)}, f32[128,128]{1,0:T(8,128)S(1)}, u32[]{:S(2)}, u32[]{:S(2)}) collective-permute-start(f32[128,128]{1,0:T(8,128)S(1)} %coarse.1.own), channel_id=1, source_target_pairs={{0,4},{4,8},{8,12},{12,16},{16,20},{20,24},{24,28},{28,32},{32,36}... | collective-permute-start | bytes 196616 | tf_op jit(solution)/shard_map/ppermute | solution.py:423
  10.3 30.9 %copy-start = (bf16[4,3,3,128,128]{4,3,2,1,0:T(8,128)(2,1)S(1)}, bf16[4,3,3,128,128]{4,3,2,1,0:T(8,128)(2,1)}, u32[]{:S(2)}) copy-start(bf16[4,3,3,128,128]{4,3,2,1,0:T(8,128)(2,1)} %param.5) | copy-start | bytes 3538948
  10.3 17.6 %all-to-all-start = ((f32[8,192,128]{2,1,0:T(8,128)}), f32[8,192,128]{2,1,0:T(8,128)S(1)}, u32[]{:S(2)}, u32[]{:S(2)}) async-start(f32[8,192,128]{2,1,0:T(8,128)} %start.1), calls=%async_computation | async-start | bytes 1572864 | tf_op jit(solution)/shard_map/all_to_all | solution.py:392
  16.3 11.7 %collective-permute-start.1 = (f32[128,128]{1,0:T(8,128)S(1)}, f32[128,128]{1,0:T(8,128)S(1)}, u32[]{:S(2)}, u32[]{:S(2)}) collective-permute-start(f32[128,128]{1,0:T(8,128)S(1)} %coarse.1.own), channel_id=1, source_target_pairs={{4,0},{8,4},{12,8},{16,12},{20,16},{24,20},{28,24},{32,28},{36,32}... | collective-permute-start | bytes 196616 | tf_op jit(solution)/shard_map/ppermute | solution.py:424
  29.2 5.3 %collective-permute-start.2 = (f32[192,128]{1,0:T(8,128)S(1)}, f32[192,128]{1,0:T(8,128)S(1)}, u32[]{:S(2)}, u32[]{:S(2)}) collective-permute-start(f32[192,128]{1,0:T(8,128)S(1)} %get-tuple-element.49.refs_1_.refs_3_), channel_id=1, source_target_pairs={{0,32},{4,36},{8,40},{12,44},{16,48},{20,52},{24,56},{28,60},{32,0... | collective-permute-start | bytes 294920 | tf_op jit(solution)/shard_map/ppermute | solution.py:443
  35.2 10.7 %collective-permute-start.5 = (f32[192,128]{1,0:T(8,128)S(1)}, f32[192,128]{1,0:T(8,128)S(1)}, u32[]{:S(2)}, u32[]{:S(2)}) collective-permute-start(f32[192,128]{1,0:T(8,128)S(1)} %pair.1), channel_id=1, source_target_pairs={{0,192},{4,196},{8,200},{12,204},{16,208},{20,212},{24,216},{28,22... | collective-permute-start | bytes 294920 | tf_op jit(solution)/shard_map/ppermute | solution.py:448
  40.5 5.4 %collective-permute-start.4 = (f32[192,128]{1,0:T(8,128)S(1)}, f32[192,128]{1,0:T(8,128)S(1)}, u32[]{:S(2)}, u32[]{:S(2)}) collective-permute-start(f32[192,128]{1,0:T(8,128)S(1)} %pair.1), channel_id=1, source_target_pairs={{0,128},{4,132},{8,136},{12,140},{16,144},{20,148},{24,152},{28,15... | collective-permute-start | bytes 294920 | tf_op jit(solution)/shard_map/ppermute | solution.py:448
  40.6 5.7 %collective-permute-start.3 = (f32[192,128]{1,0:T(8,128)S(1)}, f32[192,128]{1,0:T(8,128)S(1)}, u32[]{:S(2)}, u32[]{:S(2)}) collective-permute-start(f32[192,128]{1,0:T(8,128)S(1)} %pair.1), channel_id=1, source_target_pairs={{0,64},{4,68},{8,72},{12,76},{16,80},{20,84},{24,88},{28,92},{32,9... | collective-permute-start | bytes 294920 | tf_op jit(solution)/shard_map/ppermute | solution.py:448
  67.4 34.9 %copy-start.1 = (bf16[4,3,3,128,128]{4,3,2,1,0:T(8,128)(2,1)S(1)}, bf16[4,3,3,128,128]{4,3,2,1,0:T(8,128)(2,1)}, u32[]{:S(2)}) copy-start(bf16[4,3,3,128,128]{4,3,2,1,0:T(8,128)(2,1)} %param.5) | copy-start | bytes 3538948
  67.4 10.2 %all-to-all-start.2 = ((f32[8,64,128]{2,1,0:T(8,128)}), f32[8,64,128]{2,1,0:T(8,128)S(1)}, u32[]{:S(2)}, u32[]{:S(2)}) async-start(f32[8,64,128]{2,1,0:T(8,128)} %bitcast.22), calls=%async_computation.2 | async-start | bytes 524288 | tf_op jit(solution)/shard_map/all_to_all | solution.py:392
  71.0 11.7 %collective-permute-start.6 = (f32[512,128]{1,0:T(8,128)}, f32[512,128]{1,0:T(8,128)S(1)}, u32[]{:S(2)}, u32[]{:S(2)}) collective-permute-start(f32[512,128]{1,0:T(8,128)} %get-tuple-element.66), channel_id=1, source_target_pairs={{0,2},{1,3},{2,0},{3,1},{4,6},{5,7},{6,4},{7,5},{8,10},{9,11},{10,... | collective-permute-start | bytes 786440 | tf_op jit(solution)/shard_map/ppermute | solution.py:472
  82.7 14.8 %collective-permute-start.7 = (f32[64,128]{1,0:T(8,128)S(1)}, f32[64,128]{1,0:T(8,128)S(1)}, u32[]{:S(2)}, u32[]{:S(2)}) collective-permute-start(f32[64,128]{1,0:T(8,128)S(1)} %get-tuple-element.67.refs_1_), channel_id=1, source_target_pairs={{0,32},{4,36},{8,40},{12,44},{16,48},{20,52},{24,56},{28,60},{32,0... | collective-permute-start | bytes 98312 | tf_op jit(solution)/shard_map/ppermute | solution.py:479
  98.3 7.0 %collective-permute-start.10 = (f32[64,128]{1,0:T(8,128)S(1)}, f32[64,128]{1,0:T(8,128)S(1)}, u32[]{:S(2)}, u32[]{:S(2)}) collective-permute-start(f32[64,128]{1,0:T(8,128)S(1)} %back_pair.1), channel_id=1, source_target_pairs={{192,0},{196,4},{200,8},{204,12},{208,16},{212,20},{216,24},{220,2... | collective-permute-start | bytes 98312 | tf_op jit(solution)/shard_map/ppermute | solution.py:484
  99.7 6.2 %collective-permute-start.9 = (f32[64,128]{1,0:T(8,128)S(1)}, f32[64,128]{1,0:T(8,128)S(1)}, u32[]{:S(2)}, u32[]{:S(2)}) collective-permute-start(f32[64,128]{1,0:T(8,128)S(1)} %back_pair.1), channel_id=1, source_target_pairs={{128,0},{132,4},{136,8},{140,12},{144,16},{148,20},{152,24},{156,2... | collective-permute-start | bytes 98312 | tf_op jit(solution)/shard_map/ppermute | solution.py:484
  101.0 5.0 %collective-permute-start.8 = (f32[64,128]{1,0:T(8,128)S(1)}, f32[64,128]{1,0:T(8,128)S(1)}, u32[]{:S(2)}, u32[]{:S(2)}) collective-permute-start(f32[64,128]{1,0:T(8,128)S(1)} %back_pair.1), channel_id=1, source_target_pairs={{64,0},{68,4},{72,8},{76,12},{80,16},{84,20},{88,24},{92,28},{96,3... | collective-permute-start | bytes 98312 | tf_op jit(solution)/shard_map/ppermute | solution.py:484
  102.3 17.5 %copy-start.7 = (bf16[4,2,18,16,128]{4,3,2,1,0:T(8,128)(2,1)S(1)}, bf16[4,2,18,16,128]{4,3,2,1,0:T(8,128)(2,1)}, u32[]{:S(2)}) copy-start(bf16[4,2,18,16,128]{4,3,2,1,0:T(8,128)(2,1)} %get-tuple-element.74.refs_2_) | copy-start | bytes 1769476
  105.3 13.9 %copy-start.8 = (f32[512,128]{1,0:T(8,128)S(1)}, f32[512,128]{1,0:T(8,128)}, u32[]{:S(2)}) copy-start(f32[512,128]{1,0:T(8,128)} %get-tuple-element.60.ends_in) | copy-start | bytes 786436
  106.0 13.8 %copy-start.2 = (bf16[4,1152,128]{2,1,0:T(8,128)(2,1)S(1)}, bf16[4,1152,128]{2,1,0:T(8,128)(2,1)}, u32[]{:S(2)}) copy-start(bf16[4,1152,128]{2,1,0:T(8,128)(2,1)} %flip.1.transposed_in.refs_1_.a) | copy-start | bytes 3538948
  106.0 13.8 %copy-start.6 = (f32[4,512,128]{2,1,0:T(8,128)S(1)}, f32[4,512,128]{2,1,0:T(8,128)}, u32[]{:S(2)}) copy-start(f32[4,512,128]{2,1,0:T(8,128)} %get-tuple-element.75.refs_3_) | copy-start | bytes 3145732
  119.2 9.5 %collective-permute-start.11 = (f32[512,128]{1,0:T(8,128)S(1)}, f32[512,128]{1,0:T(8,128)S(1)}, u32[]{:S(2)}, u32[]{:S(2)}) collective-permute-start(f32[512,128]{1,0:T(8,128)S(1)} %bitcast_add_fusion.refs_0_), channel_id=1, source_target_pairs={{0,2},{1,3},{2,0},{3,1},{4,6},{5,7},{6,4},{7,5},{8,10},{9,11},{10,... | collective-permute-start | bytes 786440 | tf_op jit(solution)/shard_map/ppermute | solution.py:499
  119.8 8.9 %copy-start.3 = (f32[4,512,128]{2,1,0:T(8,128)S(1)}, f32[4,512,128]{2,1,0:T(8,128)}, u32[]{:S(2)}) copy-start(f32[4,512,128]{2,1,0:T(8,128)} %get-tuple-element.78.refs_3_.c) | copy-start | bytes 3145732
  119.8 8.9 %copy-start.4 = (bf16[4,2,18,16,128]{4,3,2,1,0:T(8,128)(2,1)S(1)}, bf16[4,2,18,16,128]{4,3,2,1,0:T(8,128)(2,1)}, u32[]{:S(2)}) copy-start(bf16[4,2,18,16,128]{4,3,2,1,0:T(8,128)(2,1)} %get-tuple-element.77.refs_2_.b) | copy-start | bytes 1769476
  129.9 13.8 %collective-permute-start.13 = (f32[2,1160,128]{2,1,0:T(8,128)S(1)}, f32[2,1160,128]{2,1,0:T(8,128)S(1)}, u32[]{:S(2)}, u32[]{:S(2)}) collective-permute-start(f32[2,1160,128]{2,1,0:T(8,128)S(1)} %get-tuple-element.81.mine), channel_id=1, source_target_pairs={{0,1},{1,0},{2,3},{3,2},{4,5},{5,4},{6,7},{7,6},{8,9},{9,8},{10,11... | collective-permute-start | bytes 3563528 | tf_op jit(solution)/shard_map/ppermute | solution.py:510
  142.1 3.3 %collective-permute-start.12 = (f32[2,1160,128]{2,1,0:T(8,128)S(1)}, f32[2,1160,128]{2,1,0:T(8,128)S(1)}, u32[]{:S(2)}, u32[]{:S(2)}) collective-permute-start(f32[2,1160,128]{2,1,0:T(8,128)S(1)} %other_early.1.mine), channel_id=1, source_target_pairs={{0,1},{1,0},{2,3},{3,2},{4,5},{5,4},{6,7},{7,6},{8,9},{9,8},{10,11... | collective-permute-start | bytes 3563528 | tf_op jit(solution)/shard_map/ppermute | solution.py:518
  (1 other events, 7.7 us)

commit v3 on v2

--- a/solution.py
+++ b/solution.py
@@ -36,16 +36,16 @@
 
 def convolve(ref, value, kernel):
     images, height, width, lanes = ref.shape
-    ref[:, 1 : height - 1] = shifted_columns(value, width).reshape(images, height - 2, width, lanes)
-    total = None
-    for row_at in range(3):
-        part = jnp.dot(
-            rows_from(ref, row_at),
-            kernel[row_at * lanes : (row_at + 1) * lanes],
-            preferred_element_type=f32,
+    rows = (height - 2) * width
+    parts = []
+    for image in range(images):
+        moved = shifted_columns(value[image * rows : (image + 1) * rows], width)
+        ref[image, 1 : height - 1] = moved.reshape(height - 2, width, lanes)
+        window = [ref[image, at : at + height - 2].reshape(rows, lanes) for at in range(3)]
+        parts.append(
+            jnp.dot(jnp.concatenate(window, axis=1), kernel[...], preferred_element_type=f32)
         )
-        total = part if total is None else total + part
-    return total
+    return jnp.concatenate(parts, axis=0)
 
 
 def split(value):
@@ -106,13 +106,16 @@
 
 
 def load_body(
-    weights, images, biases, end_grad, weights_out, images_out, biases_out, end_out, sems
+    own, weights, images, biases, end_grad,
+    copies_out, weights_out, images_out, biases_out, end_out, sems,
 ):
     pairs = [(weights, weights_out), (images, images_out), (biases, biases_out)]
     pairs.append((end_grad, end_out))
     copies = [pltpu.make_async_copy(a, b, sems.at[at]) for at, (a, b) in enumerate(pairs)]
     for copy in copies:
         copy.start()
+    for index in range(GROUP):
+        copies_out[index] = own[...]
     for copy in copies:
         copy.wait()
 
@@ -125,7 +128,7 @@
             transposed[index, tap * channels : (tap + 1) * channels] = flipped.astype(bf16)
 
 
-def start_body(images, own, before, weights, biases, payload, ref):
+def start_body(images, own, before, weights, biases, residual, ref):
     clear_border(ref)
     field = images[...]
     state = field + times(field, before[...])
@@ -133,12 +136,7 @@
         state = state + 0.25 * jnp.tanh(
             convolve(ref, state, weights.at[index]) + biases[index : index + 1]
         )
-    matrix = own[...]
-    residual = state - (field + times(field, matrix))
-    part = residual.shape[0] // GROUP
-    for index in range(GROUP):
-        payload[index, :part] = residual[index * part : (index + 1) * part]
-        payload[index, part:] = matrix
+    residual[...] = state - (field + times(field, own[...]))
 
 
 def ends_body(images, end_grad, own, before, after, starts_out, ends_out, back_out):
@@ -149,87 +147,101 @@
     back_out[...] = field + times(field, own[...], True)
 
 
-def total_body(pieces, payload, locals_out):
-    part = locals_out.shape[1]
-    error = pieces[0, :part]
-    product = pieces[0, part:]
+def total_body(pieces, group, total, locals_out):
+    error = pieces[0]
     for index in range(1, GROUP):
-        matrix = pieces[index, part:]
         locals_out[index] = error
-        error = error + (times(error, matrix) + pieces[index, :part])
-        product = product + (matrix + times(product, matrix))
-    payload[:part] = error
-    payload[part:] = product
-
-
-def pair_body(part, spot, mine, theirs, out):
+        error = error + (times(error, group[index]) + pieces[index])
+    total[...] = error
+
+
+def pair_body(spot, mine, theirs, my_product, their_product, out):
     upper = spot[1] == 1
     early = jnp.where(upper, theirs[...], mine[...])
     late = jnp.where(upper, mine[...], theirs[...])
-    out[...] = early + (times(early, late[part:]) + late)
-
-
-def back_pair_body(part, spot, mine, theirs, mine_full, theirs_full, out):
+    product = jnp.where(upper, my_product[...], their_product[...])
+    out[...] = early + (times(early, product) + late)
+
+
+def pair_product_body(spot, mine, theirs, out):
+    upper = spot[1] == 1
+    early = jnp.where(upper, theirs[...], mine[...])
+    late = jnp.where(upper, mine[...], theirs[...])
+    out[...] = early + (times(early, late) + late)
+
+
+def back_pair_body(spot, mine, theirs, my_product, their_product, out):
     upper = spot[1] == 1
     early = jnp.where(upper, mine[...], theirs[...])
     late = jnp.where(upper, theirs[...], mine[...])
-    matrix = jnp.where(upper, theirs_full[part:], mine_full[part:])
-    out[...] = early + (times(early, matrix, True) + late)
-
-
-def products_body(part, pieces, prefix_out, suffix_out):
-    before = pieces[0, part:]
-    after = pieces[GROUP - 1, part:]
+    product = jnp.where(upper, their_product[...], my_product[...])
+    out[...] = early + (times(early, product, True) + late)
+
+
+def products_body(group, product_out, prefix_out, suffix_out):
+    before = group[0]
+    after = group[GROUP - 1]
     for index in range(1, GROUP):
         prefix_out[index] = before
         suffix_out[GROUP - 1 - index] = after
+        matrix = group[index]
+        before = before + (matrix + times(before, matrix))
         if index < GROUP - 1:
-            matrix = pieces[index, part:]
-            before = before + (matrix + times(before, matrix))
-            matrix = pieces[GROUP - 1 - index, part:]
+            matrix = group[GROUP - 1 - index]
             after = after + (matrix + times(matrix, after))
-
-
-def back_total_body(part, pieces, first, payload, locals_out):
+    product_out[...] = before
+
+
+def back_total_body(pieces, group, total, locals_out):
     error = pieces[GROUP - 1]
     for index in range(GROUP - 2, -1, -1):
         locals_out[index] = error
-        error = error + (times(error, first[index, part:], True) + pieces[index])
-    payload[...] = error
-
-
-def replay_body(spot, theirs, far1, far2, far3, locals_in, prefix_in, out, prefix, sem):
+        error = error + (times(error, group[index], True) + pieces[index])
+    total[...] = error
+
+
+def replay_body(
+    spot, theirs, far1, far2, far3, their_product, product1, product2, locals_in, prefix_in,
+    result, prefix, out, sem, sems,
+):
+    stores = [pltpu.make_async_copy(out.at[at], result.at[at], sems.at[at]) for at in range(GROUP)]
     copy = pltpu.make_async_copy(prefix_in, prefix, sem)
     copy.start()
-    part = out.shape[1]
-    error = jnp.where(spot[0] >= 3, far3[:part], 0.0)
-    for distance, group in ((2, far2), (1, far1)):
-        longer = error + (times(error, group[part:]) + group[:part])
-        error = jnp.where(spot[0] >= distance, longer, error)
-    longer = error + (times(error, theirs[part:]) + theirs[:part])
+    error = far3[...]
+    for group, product in ((far2, product2), (far1, product1)):
+        error = error + (times(error, product[...]) + group[...])
+    longer = error + (times(error, their_product[...]) + theirs[...])
     error = jnp.where(spot[1] == 1, longer, error)
     out[0] = error
+    stores[0].start()
     copy.wait()
     for index in range(1, GROUP):
         out[index] = error + (times(error, prefix[index]) + locals_in[index])
+        stores[index].start()
+    for store in stores:
+        store.wait()
 
 
 def back_replay_body(
-    spot, theirs, far1, far2, far3, theirs_full, full1, full2, locals_in, suffix_in,
-    out, suffix, sem,
+    spot, theirs, far1, far2, far3, their_product, product1, product2, locals_in, suffix_in,
+    result, suffix, out, sem, sems,
 ):
+    stores = [pltpu.make_async_copy(out.at[at], result.at[at], sems.at[at]) for at in range(GROUP)]
     copy = pltpu.make_async_copy(suffix_in, suffix, sem)
     copy.start()
-    part = out.shape[1]
     error = far3[...]
-    for group, full in ((far2, full2), (far1, full1)):
-        error = error + (times(error, full[part:], True) + group[...])
-    longer = error + (times(error, theirs_full[part:], True) + theirs[...])
+    for group, product in ((far2, product2), (far1, product1)):
+        error = error + (times(error, product[...], True) + group[...])
+    longer = error + (times(error, their_product[...], True) + theirs[...])
     error = jnp.where(spot[1] == 0, longer, error)
     out[GROUP - 1] = error
+    stores[GROUP - 1].start()
     copy.wait()
     for index in range(GROUP - 1):
         out[index] = error + (times(error, suffix[index], True) + locals_in[index])
+        stores[index].start()
+    for store in stores:
+        store.wait()
 
 
 def forward_sweep(state, weights, biases, ref, inputs, slopes, stores, fetches=None):
@@ -258,13 +270,12 @@
 
 
 def middle_body(
-    error, starts_in, ends_in, back_in, weights_in, transposed_in, biases_in,
-    corrected_out, ends_out, inputs_out, slopes_out, residual_out,
-    ref, corrected, ends, inputs, slopes, starts, ends_adj, back, weights, transposed, biases,
-    sems, loads,
+    corrected, ends_in, back_in, weights_in, transposed_in, biases_in,
+    ends_out, inputs_out, slopes_out, residual_out,
+    ref, ends, inputs, slopes, ends_adj, back, weights, transposed, biases, sems, loads,
 ):
     blocks = weights.shape[0]
-    pairs = [(starts_in, starts), (biases_in, biases)]
+    pairs = [(biases_in, biases)]
     pairs += [(weights_in.at[index], weights.at[index]) for index in range(blocks)]
     pairs += [(transposed_in, transposed), (ends_in, ends_adj), (back_in, back)]
     fetches = [pltpu.make_async_copy(a, b, loads.at[at]) for at, (a, b) in enumerate(pairs)]
@@ -273,23 +284,19 @@
     clear_border(ref)
     stores = sweep_stores(inputs, slopes, inputs_out, slopes_out, sems)
     fetches[0].wait()
-    fetches[1].wait()
-    corrected[...] = starts[...] + error[...]
-    first = pltpu.make_async_copy(corrected, corrected_out, sems.at[2 * blocks])
-    first.start()
     ends[...] = forward_sweep(
-        corrected[...], weights, biases, ref, inputs, slopes, stores, fetches[2 : 2 + blocks]
-    )
-    for fetch in fetches[2 + blocks :]:
+        corrected[...], weights, biases, ref, inputs, slopes, stores, fetches[1 : 1 + blocks]
+    )
+    for fetch in fetches[1 + blocks :]:
         fetch.wait()
-    last = pltpu.make_async_copy(ends, ends_out, sems.at[2 * blocks + 1])
+    last = pltpu.make_async_copy(ends, ends_out, sems.at[2 * blocks])
     last.start()
     adjoint = ends_adj[...]
     for index in reversed(range(blocks)):
         change = slopes[index] * adjoint
         adjoint = adjoint + convolve(ref, change, transposed.at[index])
     residual_out[...] = adjoint - back[...]
-    for store in sum(stores, [first, last]):
+    for store in sum(stores, [last]):
         store.wait()
 
 
@@ -347,23 +354,20 @@
         adjoint_out[...] = adjoint
 
 
-def join_body(first, mine, theirs, late_offsets, kernels_out, offsets_out, total, sems):
+def join_body(first, mine, theirs, late, kernels_out, offsets_out, total, offsets, sems):
     size = kernels_out.shape[1]
     count = mine.shape[0]
-    part = size // 3
-    copies = []
+    offsets[:count] = mine[:, size] + theirs[:, size]
+    if late is not None:
+        offsets[count:] = late[...]
+    copies = [pltpu.make_async_copy(offsets, offsets_out, sems.at[count])]
+    copies[0].start()
     for index in range(count):
-        for at in range(3):
-            rows = pl.ds(at * part, part)
-            total[index, rows] = mine[index, rows] + theirs[index, rows]
-            copy = pltpu.make_async_copy(
-                total.at[index, rows], kernels_out.at[first + index, rows], sems.at[3 * index + at]
-            )
-            copy.start()
-            copies.append(copy)
-    offsets_out[:count] = mine[:, size] + theirs[:, size]
-    if late_offsets is not None:
-        offsets_out[count:] = late_offsets[...]
+        total[index] = mine[index, :size] + theirs[index, :size]
+        copies.append(
+            pltpu.make_async_copy(total.at[index], kernels_out.at[first + index], sems.at[index])
+        )
+        copies[-1].start()
     for copy in copies:
         copy.wait()
 
@@ -378,6 +382,7 @@
     near = [[a * GROUP + b for b in range(GROUP)] for a in range(outer)]
     pair = [(i, i ^ GROUP) for i in range(layers)]
     around = [[(i, (i + 2 * GROUP * d) % layers) for i in range(layers)] for d in (1, 2, 3)]
+    up = [[(i, i + 2 * GROUP * d) for i in range(layers - 2 * GROUP * d)] for d in (1, 2, 3)]
     down = [[(i, i - 2 * GROUP * d) for i in range(2 * GROUP * d, layers)] for d in (1, 2, 3)]
     dp = lax.axis_size("dp")
     partner = [(i, (i + dp // 2) % dp) for i in range(dp)]
@@ -396,8 +401,6 @@
     matrix = shape((channels, channels))
     pieces_shape = shape((GROUP, part, channels))
     pieces_kept = stored((GROUP, part, channels))
-    both_kept = stored((GROUP, part + channels, channels))
-    both = shape((part + channels, channels))
     piece = shape((part, channels))
     matrices = stored((GROUP, channels, channels))
     taps_shape = shape((blocks, 9, channels, channels), bf16)
@@ -422,64 +425,75 @@
     )
     before = lax.ppermute(own, "layer", [(i, i + 1) for i in range(layers - 1)])
     after = lax.ppermute(own, "layer", [(i + 1, i) for i in range(layers - 1)])
-    held, field, offsets, cotangent = call(
-        load_body, [taps_shape, plane, offsets_shape, plane],
+    copies, held, field, offsets, cotangent = call(
+        load_body, [matrices, taps_shape, plane, offsets_shape, plane], own,
         in_hbm(flat), in_hbm(images.reshape(rows, channels)), in_hbm(biases),
         in_hbm(end_grad.reshape(rows, channels)),
-        ins=[HBM] * 4, scratch=[dma((4,))], name="load",
-    )
-
-    (payload,) = call(
-        start_body, [both_kept], field, own, before, held.reshape(sweep_shape), offsets,
+        ins=[VMEM] + [HBM] * 4, scratch=[dma((4,))], name="load",
+    )
+    group = exchange(copies, near)
+
+    (residual,) = call(
+        start_body, [kept], field, own, before, held.reshape(sweep_shape), offsets,
         scratch=[ref], flops=blocks * per_conv, name="start",
     )
-    first = exchange(payload, near)
-    first, after = lax.optimization_barrier((first, after))
+    residual, group = lax.optimization_barrier((residual, group))
+    first = exchange(residual.reshape(GROUP, part, channels), near)
+    product, prefix, suffix = call(
+        products_body, [matrix, matrices, matrices], group, name="products"
+    )
+    their_product = lax.ppermute(product, "layer", pair)
+    (pair_product,) = call(
+        pair_product_body, [matrix], spot, product, their_product, ins=[SMEM, VMEM, VMEM],
+        name="pair_product",
+    )
+    around_product = [lax.ppermute(pair_product, "layer", to) for to in around]
     starts, ends_adj, back = call(
         ends_body, [kept] * 3, field, cotangent, own, before, after, name="ends"
     )
     (transposed,) = call(flip_body, [stored(sweep_shape, bf16)], flat, name="flip")
-    full, prefixes = call(total_body, [both, pieces_shape], first, name="total")
-    their_full = lax.ppermute(full, "layer", pair)
-    (pair_full,) = call(
-        lambda *refs: pair_body(part, *refs), [both], spot, full, their_full,
-        ins=[SMEM, VMEM, VMEM], name="pair",
-    )
-    around_full = [lax.ppermute(pair_full, "layer", to) for to in around]
-    prefix, suffix = call(
-        lambda *refs: products_body(part, *refs), [matrices] * 2, first, name="products"
-    )
-    replay_scratch = [pltpu.VMEM((GROUP, channels, channels), f32), dma(())]
+    first, starts, ends_adj, back, transposed = lax.optimization_barrier(
+        (first, starts, ends_adj, back, transposed)
+    )
+    total, prefixes = call(total_body, [piece, pieces_shape], first, group, name="total")
+    their_total = lax.ppermute(total, "layer", pair)
+    (pair_total,) = call(
+        pair_body, [piece], spot, total, their_total, product, their_product,
+        ins=[SMEM] + [VMEM] * 4, name="pair",
+    )
+    up_total = [lax.ppermute(pair_total, "layer", to) for to in up]
+    replay_scratch = [
+        pltpu.VMEM((GROUP, channels, channels), f32), pltpu.VMEM((GROUP, part, channels), f32),
+        dma(()), dma((GROUP,)),
+    ]
     (error,) = call(
-        replay_body, [pieces_kept], spot, their_full, *around_full, prefixes, in_hbm(prefix),
-        ins=[SMEM] + [VMEM] * 5 + [HBM], scratch=replay_scratch, name="replay",
-    )
-    error, suffix, ends_adj, back, transposed, starts = lax.optimization_barrier(
-        (error, suffix, ends_adj, back, transposed, starts)
-    )
-    error = exchange(error, near).reshape(rows, channels)
-
-    corrected, interval_ends, inputs, slopes, adj_residual = call(
-        middle_body, [kept, result, stored(inputs_dims, bf16), stored(slopes_dims), kept],
-        error, in_hbm(starts), in_hbm(ends_adj), in_hbm(back), in_hbm(kernels),
+        replay_body, [pieces_kept], spot, their_total, *up_total, their_product,
+        around_product[0], around_product[1], prefixes, in_hbm(prefix),
+        ins=[SMEM] + [VMEM] * 8 + [HBM], out_specs=[HBM], scratch=replay_scratch, name="replay",
+    )
+    error, suffix = lax.optimization_barrier((error, suffix))
+    corrected = starts + exchange(error, near).reshape(rows, channels)
+    other_corrected = lax.ppermute(corrected, "dp", partner)
+
+    interval_ends, inputs, slopes, adj_residual = call(
+        middle_body, [result, stored(inputs_dims, bf16), stored(slopes_dims), kept],
+        corrected, in_hbm(ends_adj), in_hbm(back), in_hbm(kernels),
         in_hbm(transposed), in_hbm(biases),
-        ins=[VMEM] + [HBM] * 6, out_specs=[HBM, HBM, HBM, HBM, VMEM],
-        scratch=[ref] + [pltpu.VMEM((rows, channels), f32)] * 2 + sweep_scratch
-        + [pltpu.VMEM((rows, channels), f32)] * 3 + [pltpu.VMEM(sweep_shape, bf16)] * 2
-        + [pltpu.VMEM((blocks, channels), f32), dma((2 * blocks + 2,)), dma((blocks + 5,))],
+        ins=[VMEM] + [HBM] * 5, out_specs=[HBM, HBM, HBM, VMEM],
+        scratch=[ref, pltpu.VMEM((rows, channels), f32)] + sweep_scratch
+        + [pltpu.VMEM((rows, channels), f32)] * 2 + [pltpu.VMEM(sweep_shape, bf16)] * 2
+        + [pltpu.VMEM((blocks, channels), f32), dma((2 * blocks + 1,)), dma((blocks + 4,))],
         flops=2 * blocks * per_conv, name="middle",
     )
-    other_corrected = lax.ppermute(corrected, "dp", partner)
     pieces = exchange(adj_residual.reshape(GROUP, part, channels), near)
     total, prefixes = call(
-        lambda *refs: back_total_body(part, *refs), [piece, pieces_kept], pieces, first,
+        back_total_body, [piece, pieces_kept], pieces, group,
         name="back_total",
     )
-    total, other_corrected = lax.optimization_barrier((total, other_corrected))
     their_total = lax.ppermute(total, "layer", pair)
     (pair_total,) = call(
-        lambda *refs: back_pair_body(part, *refs), [piece],
-        spot, total, their_total, full, their_full, ins=[SMEM] + [VMEM] * 4, name="back_pair",
+        back_pair_body, [piece], spot, total, their_total, product, their_product,
+        ins=[SMEM] + [VMEM] * 4, name="back_pair",
     )
     down_total = [lax.ppermute(pair_total, "layer", to) for to in down]
     other_inputs, other_slopes = call(
@@ -488,9 +502,10 @@
         scratch=[ref] + sweep_scratch + [dma((2 * blocks,))], flops=blocks * per_conv, name="again",
     )
     (adj_error,) = call(
-        back_replay_body, [pieces_kept], spot, their_total, *down_total, their_full,
-        around_full[2], around_full[1], prefixes, in_hbm(suffix),
-        ins=[SMEM] + [VMEM] * 8 + [HBM], scratch=replay_scratch, name="back_replay",
+        back_replay_body, [pieces_kept], spot, their_total, *down_total, their_product,
+        around_product[2], around_product[1], prefixes, in_hbm(suffix),
+        ins=[SMEM] + [VMEM] * 8 + [HBM], out_specs=[HBM], scratch=replay_scratch,
+        name="back_replay",
     )
     adj_error, other_inputs, other_slopes = lax.optimization_barrier(
         (adj_error, other_inputs, other_slopes)
@@ -516,18 +531,19 @@
         scratch=[ref], flops=blocks * per_conv, name="other_early",
     )
     their_early = lax.ppermute(early, "dp", sibling)
-    join_scratch = [pltpu.VMEM((half, 9 * channels, channels), f32), dma((3 * half,))]
+    sums = pltpu.VMEM((half, 9 * channels, channels), f32)
     weight_grad, late_offsets = call(
         lambda mine, theirs, *refs: join_body(half, mine, theirs, None, *refs),
         [gradients, half_offsets], late, their_late,
-        out_specs=[HBM, VMEM], scratch=join_scratch, name="join_late",
+        out_specs=[HBM, HBM], name="join_late",
+        scratch=[sums, pltpu.VMEM((half, channels), f32), dma((half + 1,))],
     )
     weight_grad, bias_grad = call(
         lambda mine, theirs, offsets, _, *refs: join_body(0, mine, theirs, offsets, *refs),
         [gradients, jax.ShapeDtypeStruct((blocks, channels), f32)],
         early, their_early, late_offsets, weight_grad,
-        ins=[VMEM, VMEM, VMEM, HBM], out_specs=[HBM, VMEM], scratch=join_scratch,
-        aliases={3: 0}, name="join_early",
+        ins=[VMEM, VMEM, VMEM, HBM], out_specs=[HBM, HBM], aliases={3: 0}, name="join_early",
+        scratch=[sums, pltpu.VMEM((blocks, channels), f32), dma((half + 1,))],
     )
     dims = (1, count, height, width, channels)
     return (

time: 148 us -> 150 us (1.014)
  starting transfers between devices: 60.2 us -> 63.9 us
  blocking collectives: 21.9 us -> 18.8 us
  local copies, waits for them, and re-layouts: 0.04 us -> 2.32 us
    ppermute x1 -> x2, starting transfers between devices: 13.5 us -> 1.2 us  [shards(): their_total = lax.ppermute(total, 'layer', pair)]
    ppermute x4 -> x7, starting transfers between devices: 9.34 us -> 20.6 us  [the longest x3 8.82 us: shards(): around_product = [lax.ppermute(pair_product, 'layer', to) for to in around]]
    ppermute x1, waiting for transfers between devices: 10.4 us -> 0.01 us  [shards(): after = lax.ppermute(own, 'layer', [(i + 1, i) for i in range(layers - 1)])]
    all_to_all x2 -> x3, starting transfers between devices: 9.48 us -> 16.8 us  [exchange(): return lax.all_to_all(value, 'layer', 0, 0, axis_index_groups=groups)]
    ppermute x1 -> x2, waiting for transfers between devices: 1.3 us -> 7.73 us  [shards(): their_total = lax.ppermute(total, 'layer', pair)]
    ppermute x1, waiting for transfers between devices: 0.01 us -> 3.38 us  [shards(): before = lax.ppermute(own, 'layer', [(i, i + 1) for i in range(layers - 1)])]
    ppermute x1, waiting for transfers between devices: 3.32 us -> 0.01 us  [shards(): other_corrected = lax.ppermute(corrected, 'dp', partner)]
    all_to_all x2, blocking collectives: 21.9 us -> 18.8 us  [exchange(): return lax.all_to_all(value, 'layer', 0, 0, axis_index_groups=groups)]
  transfers between devices with their start and end apart: 16 -> 21, of which waited for: 10 -> 10; matrix products, arithmetic and copies ran while one was open for 0% -> 0% of each run, Pallas kernels for 11% -> 13%
where the time goes in v3:
time: 150 us; the launch traced here: 148 us
  starting transfers between devices  63.9 us (43%)
  Pallas kernels  36.8 us (25%)
  waiting for transfers between devices  25 us (17%)
  blocking collectives  18.8 us (13%)
  local copies, waits for them, and re-layouts  2.32 us (2%)
    pallas_call x20, Pallas kernels, call(): pl.pallas_call(body, out_shape=tuple(outs), in_specs=list(ins) if ins els...  36.8 us
    all_to_all x2, blocking collectives, exchange(): return lax.all_to_all(value, 'layer', 0, 0, axis_index_groups=groups)  18.8 us
    all_to_all x3, starting transfers between devices, exchange(): return lax.all_to_all(value, 'layer', 0, 0, axis_index_groups=groups)  16.8 us
    ppermute x1, starting transfers between devices, shards(): their_late = lax.ppermute(late, 'dp', sibling)  9.62 us
    ppermute x3, starting transfers between devices, shards(): around_product = [lax.ppermute(pair_product, 'layer', to) for to in around]  8.82 us
    ppermute x1, waiting for transfers between devices, shards(): other_moving = lax.ppermute(moving, 'dp', partner)  7.83 us
    ppermute x2, waiting for transfers between devices, shards(): their_total = lax.ppermute(total, 'layer', pair)  7.73 us
    ppermute x3, starting transfers between devices, shards(): up_total = [lax.ppermute(pair_total, 'layer', to) for to in up]  6.46 us
  transfers between devices with their start and end apart: 21, of which 10 were waited for; matrix products, arithmetic and copies ran while one was open for 0% of the time, Pallas kernels for 13%

profile of v3, /device:TPU:1, one launch (start us, length us, event | category | flops | bytes accessed | tf_op | source)
XLA Modules:
  0.0 148.1 jit_solution(10896204228655409702)
XLA Ops:
  1.6 2.2 %load.1 = (f32[8,128,128]{2,1,0:T(8,128)}, bf16[4,9,128,128]{3,2,1,0:T(8,128)(2,1)S(1)}, f32[512,128]{1,0:T(8,128)S(1)}, f32[4,128]{1,0:T(4,128)S(1)}, f32[512,128]{1,0:T(8,128)S(1)}) custom-call(f32[128,128]{1,0:T(8,128)S(1)} %coarse.1.own, bf16[4,9,128,128]{3,2,1,0:T(8,128)(2,1)} %bitcast.17, f32[512,128]{1,0:T(8,128)} %bitcast.25, f32[4,128]{1,0:T(4,128)} %biases_in.1, ...), custom_call_target="tpu_custom_call" | custom-call | bytes 4001792 | tf_op jit(solution)/shard_map/load/pallas_call | solution.py:73
  4.8 6.2 %all-to-all-start = ((f32[8,128,128]{2,1,0:T(8,128)}), f32[8,128,128]{2,1,0:T(8,128)S(1)}, u32[]{:S(2)}, u32[]{:S(2)}) async-start(f32[8,128,128]{2,1,0:T(8,128)} %get-tuple-element.48), calls=%async_computation | async-start | bytes 1048576 | tf_op jit(solution)/shard_map/all_to_all | solution.py:397
  11.0 3.4 %collective-permute-start = (f32[128,128]{1,0:T(8,128)S(1)}, f32[128,128]{1,0:T(8,128)S(1)}, u32[]{:S(2)}, u32[]{:S(2)}) collective-permute-start(f32[128,128]{1,0:T(8,128)S(1)} %coarse.1.own), channel_id=1, source_target_pairs={{0,4},{4,8},{8,12},{12,16},{16,20},{20,24},{24,28},{28,32},{32,36}... | collective-permute-start | bytes 196616 | tf_op jit(solution)/shard_map/ppermute | solution.py:426
  14.4 3.4 %collective-permute-done.before = f32[128,128]{1,0:T(8,128)S(1)} collective-permute-done((f32[128,128]{1,0:T(8,128)S(1)}, f32[128,128]{1,0:T(8,128)S(1)}, u32[]{:S(2)}, u32[]{:S(2)}) %collective-permute-start) | collective-permute-done | bytes 65568 | tf_op jit(solution)/shard_map/ppermute | solution.py:426
  19.1 2.7 %start.1 = f32[512,128]{1,0:T(8,128)} custom-call(f32[512,128]{1,0:T(8,128)S(1)} %get-tuple-element.45.images, f32[128,128]{1,0:T(8,128)S(1)} %coarse.1.own, f32[128,128]{1,0:T(8,128)S(1)} %collective-permute-done.before, bf16[4,1152,128]{2,1,0:T(8,128)(2,1)S(1)} %bitcast.21, f32[4,128]{1,0:T(4,128)S(1)} %get-tuple-element.47.biases), custom_call_target="tpu_custom_call" | custom-call | flops 603979776 | bytes 1837056 | tf_op jit(solution)/shard_map/start/pallas_call | solution.py:73
  21.8 7.1 %all-to-all-start.1 = ((f32[8,64,128]{2,1,0:T(8,128)}), f32[8,64,128]{2,1,0:T(8,128)S(1)}, u32[]{:S(2)}, u32[]{:S(2)}) async-start(f32[8,64,128]{2,1,0:T(8,128)} %bitcast.23), calls=%async_computation.1 | async-start | bytes 524288 | tf_op jit(solution)/shard_map/all_to_all | solution.py:397
  33.5 5.4 %collective-permute-start.3 = (f32[128,128]{1,0:T(8,128)S(1)}, f32[128,128]{1,0:T(8,128)S(1)}, u32[]{:S(2)}, u32[]{:S(2)}) collective-permute-start(f32[128,128]{1,0:T(8,128)S(1)} %get-tuple-element.58.my_product.mine), channel_id=1, source_target_pairs={{0,32},{4,36},{8,40},{12,44},{16,48},{20,52},{24,56},{28,60},{32,0... | collective-permute-start | bytes 196616 | tf_op jit(solution)/shard_map/ppermute | solution.py:445
  41.2 7.4 %collective-permute-start.8 = (f32[128,128]{1,0:T(8,128)S(1)}, f32[128,128]{1,0:T(8,128)S(1)}, u32[]{:S(2)}, u32[]{:S(2)}) collective-permute-start(f32[128,128]{1,0:T(8,128)S(1)} %pair_product.1), channel_id=1, source_target_pairs={{0,128},{4,132},{8,136},{12,140},{16,144},{20,148},{24,152},{28,15... | collective-permute-start | bytes 196616 | tf_op jit(solution)/shard_map/ppermute | solution.py:450
  51.0 2.5 %collective-permute-done.2.theirs = f32[64,128]{1,0:T(8,128)S(1)} collective-permute-done((f32[64,128]{1,0:T(8,128)S(1)}, f32[64,128]{1,0:T(8,128)S(1)}, u32[]{:S(2)}, u32[]{:S(2)}) %collective-permute-start.2) | collective-permute-done | bytes 32800 | tf_op jit(solution)/shard_map/ppermute | solution.py:459
  54.2 2.7 %collective-permute-start.6 = (f32[64,128]{1,0:T(8,128)S(1)}, f32[64,128]{1,0:T(8,128)S(1)}, u32[]{:S(2)}, u32[]{:S(2)}) collective-permute-start(f32[64,128]{1,0:T(8,128)S(1)} %pair.1), channel_id=1, source_target_pairs={{0,192},{4,196},{8,200},{12,204},{16,208},{20,212},{24,216},{28,22... | collective-permute-start | bytes 98312 | tf_op jit(solution)/shard_map/ppermute | solution.py:464
  58.1 2.5 %collective-permute-start.4 = (f32[64,128]{1,0:T(8,128)S(1)}, f32[64,128]{1,0:T(8,128)S(1)}, u32[]{:S(2)}, u32[]{:S(2)}) collective-permute-start(f32[64,128]{1,0:T(8,128)S(1)} %pair.1), channel_id=1, source_target_pairs={{0,64},{4,68},{8,72},{12,76},{16,80},{20,84},{24,88},{28,92},{32,9... | collective-permute-start | bytes 98312 | tf_op jit(solution)/shard_map/ppermute | solution.py:464
  61.6 2.9 %replay.1 = f32[8,64,128]{2,1,0:T(8,128)} custom-call(s32[2]{0:T(128)S(1)} %pad_add_fusion.spot, f32[64,128]{1,0:T(8,128)S(1)} %collective-permute-done.2.theirs, f32[64,128]{1,0:T(8,128)S(1)} %collective-permute-done.4.far1, f32[64,128]{1,0:T(8,128)S(1)} %collective-permute-done.5.far2, f32[64,128]{1,0:T(8,128)S(1)} %collective-permute-done.6.far3, ...), custom_call_target="tpu_custom_call" | custom-call | bytes 1376264 | tf_op jit(solution)/shard_map/replay/pallas_call | solution.py:73
  64.6 9.4 %all_to_all.25 = f32[8,64,128]{2,1,0:T(8,128)S(1)} all-to-all(f32[8,64,128]{2,1,0:T(8,128)} %replay.1), channel_id=1, replica_groups={{0,4,8,12,16,20,24,28},{32,36,40,44,48,52,56,60},{64,68,72,76,80,84,88,..., dimensions={0} | all-to-all | bytes 524288 | tf_op jit(solution)/shard_map/all_to_all | solution.py:397
  74.0 5.3 %middle.1 = (f32[512,128]{1,0:T(8,128)}, bf16[4,2,18,16,128]{4,3,2,1,0:T(8,128)(2,1)}, f32[4,512,128]{2,1,0:T(8,128)}, f32[512,128]{1,0:T(8,128)}) custom-call(f32[512,128]{1,0:T(8,128)S(1)} %bitcast_add_fusion.1.corrected, f32[512,128]{1,0:T(8,128)} %get-tuple-element.63.ends_in, f32[512,128]{1,0:T(8,128)} %get-tuple-element.64.back_in, ...), custom_call_target="tpu_custom_call" | custom-call | flops 1207959552 | bytes 5310464 | tf_op jit(solution)/shard_map/middle/pallas_call | solution.py:73
  79.4 3.6 %all-to-all-start.3 = ((f32[8,64,128]{2,1,0:T(8,128)}), f32[8,64,128]{2,1,0:T(8,128)S(1)}, u32[]{:S(2)}, u32[]{:S(2)}) async-start(f32[8,64,128]{2,1,0:T(8,128)} %bitcast.24), calls=%async_computation.3 | async-start | bytes 524288 | tf_op jit(solution)/shard_map/all_to_all | solution.py:397
  82.9 4.3 %collective-permute-start.14 = (f32[512,128]{1,0:T(8,128)S(1)}, f32[512,128]{1,0:T(8,128)S(1)}, u32[]{:S(2)}, u32[]{:S(2)}) collective-permute-start(f32[512,128]{1,0:T(8,128)S(1)} %bitcast_add_fusion.1.corrected), channel_id=1, source_target_pairs={{0,2},{1,3},{2,0},{3,1},{4,6},{5,7},{6,4},{7,5},{8,10},{9,11},{10,... | collective-permute-start | bytes 786440 | tf_op jit(solution)/shard_map/ppermute | solution.py:476
  92.1 5.3 %collective-permute-done.9.theirs = f32[64,128]{1,0:T(8,128)S(1)} collective-permute-done((f32[64,128]{1,0:T(8,128)S(1)}, f32[64,128]{1,0:T(8,128)S(1)}, u32[]{:S(2)}, u32[]{:S(2)}) %collective-permute-start.9) | collective-permute-done | bytes 32800 | tf_op jit(solution)/shard_map/ppermute | solution.py:493
  102.1 2.5 %again.1 = (bf16[4,2,18,16,128]{4,3,2,1,0:T(8,128)(2,1)}, f32[4,512,128]{2,1,0:T(8,128)}) custom-call(f32[512,128]{1,0:T(8,128)S(1)} %collective-permute-done.14.corrected, bf16[4,1152,128]{2,1,0:T(8,128)(2,1)S(1)} %bitcast.20, f32[4,128]{1,0:T(4,128)S(1)} %get-tuple-element.47.biases), custom_call_target="tpu_custom_call" | custom-call | flops 603979776 | bytes 3082240 | tf_op jit(solution)/shard_map/again/pallas_call | solution.py:73
  105.6 3.3 %back_replay.1 = f32[8,64,128]{2,1,0:T(8,128)} custom-call(s32[2]{0:T(128)S(1)} %pad_add_fusion.spot, f32[64,128]{1,0:T(8,128)S(1)} %collective-permute-done.9.theirs, f32[64,128]{1,0:T(8,128)S(1)} %collective-permute-done.10.far1, f32[64,128]{1,0:T(8,128)S(1)} %collective-permute-done.11.far2, f32[64,128]{1,0:T(8,128)S(1)} %collective-permute-done.12.far3, ...), custom_call_target="tpu_custom_call" | custom-call | bytes 1376264 | tf_op jit(solution)/shard_map/back_replay/pallas_call | solution.py:73
  108.9 9.4 %all_to_all.26 = f32[8,64,128]{2,1,0:T(8,128)S(1)} all-to-all(f32[8,64,128]{2,1,0:T(8,128)} %back_replay.1), channel_id=1, replica_groups={{0,4,8,12,16,20,24,28},{32,36,40,44,48,52,56,60},{64,68,72,76,80,84,88,..., dimensions={0} | all-to-all | bytes 524288 | tf_op jit(solution)/shard_map/all_to_all | solution.py:397
  118.4 2.7 %collective-permute-start.15 = (f32[512,128]{1,0:T(8,128)S(1)}, f32[512,128]{1,0:T(8,128)S(1)}, u32[]{:S(2)}, u32[]{:S(2)}) collective-permute-start(f32[512,128]{1,0:T(8,128)S(1)} %bitcast_add_fusion.refs_0_), channel_id=1, source_target_pairs={{0,2},{1,3},{2,0},{3,1},{4,6},{5,7},{6,4},{7,5},{8,10},{9,11},{10,... | collective-permute-start | bytes 786440 | tf_op jit(solution)/shard_map/ppermute | solution.py:514
  121.1 2.8 %final.1 = (f32[512,128]{1,0:T(8,128)}, f32[4,1160,128]{2,1,0:T(8,128)S(1)}) custom-call(f32[512,128]{1,0:T(8,128)S(1)} %bitcast_add_fusion.refs_0_, bf16[4,1152,128]{2,1,0:T(8,128)(2,1)S(1)} %copy-done.2, bf16[4,2,18,16,128]{4,3,2,1,0:T(8,128)(2,1)S(1)} %copy-done.9, f32[4,512,128]{2,1,0:T(8,128)S(1)} %copy-done.8), custom_call_target="tpu_custom_call" | custom-call | flops 1207959552 | bytes 5718016 | tf_op jit(solution)/shard_map/final/pallas_call | solution.py:73
  124.0 7.8 %collective-permute-done.15.refs_0_ = f32[512,128]{1,0:T(8,128)S(1)} collective-permute-done((f32[512,128]{1,0:T(8,128)S(1)}, f32[512,128]{1,0:T(8,128)S(1)}, u32[]{:S(2)}, u32[]{:S(2)}) %collective-permute-start.15) | collective-permute-done | bytes 262176 | tf_op jit(solution)/shard_map/ppermute | solution.py:514
  133.0 9.6 %collective-permute-start.17 = (f32[2,1160,128]{2,1,0:T(8,128)S(1)}, f32[2,1160,128]{2,1,0:T(8,128)S(1)}, u32[]{:S(2)}, u32[]{:S(2)}) collective-permute-start(f32[2,1160,128]{2,1,0:T(8,128)S(1)} %get-tuple-element.81.mine), channel_id=1, source_target_pairs={{0,1},{1,0},{2,3},{3,2},{4,5},{5,4},{6,7},{7,6},{8,9},{9,8},{10,11... | collective-permute-start | bytes 3563528 | tf_op jit(solution)/shard_map/ppermute | solution.py:525
  (67 shorter events, 32.6 us)
Async XLA Ops:
  4.8 16.9 %all-to-all-start = ((f32[8,128,128]{2,1,0:T(8,128)}), f32[8,128,128]{2,1,0:T(8,128)S(1)}, u32[]{:S(2)}, u32[]{:S(2)}) async-start(f32[8,128,128]{2,1,0:T(8,128)} %get-tuple-element.48), calls=%async_computation | async-start | bytes 1048576 | tf_op jit(solution)/shard_map/all_to_all | solution.py:397
  11.0 6.7 %collective-permute-start = (f32[128,128]{1,0:T(8,128)S(1)}, f32[128,128]{1,0:T(8,128)S(1)}, u32[]{:S(2)}, u32[]{:S(2)}) collective-permute-start(f32[128,128]{1,0:T(8,128)S(1)} %coarse.1.own), channel_id=1, source_target_pairs={{0,4},{4,8},{8,12},{12,16},{16,20},{20,24},{24,28},{28,32},{32,36}... | collective-permute-start | bytes 196616 | tf_op jit(solution)/shard_map/ppermute | solution.py:426
  21.8 26.8 %all-to-all-start.1 = ((f32[8,64,128]{2,1,0:T(8,128)}), f32[8,64,128]{2,1,0:T(8,128)S(1)}, u32[]{:S(2)}, u32[]{:S(2)}) async-start(f32[8,64,128]{2,1,0:T(8,128)} %bitcast.23), calls=%async_computation.1 | async-start | bytes 524288 | tf_op jit(solution)/shard_map/all_to_all | solution.py:397
  28.8 10.1 %collective-permute-start.1 = (f32[128,128]{1,0:T(8,128)S(1)}, f32[128,128]{1,0:T(8,128)S(1)}, u32[]{:S(2)}, u32[]{:S(2)}) collective-permute-start(f32[128,128]{1,0:T(8,128)S(1)} %coarse.1.own), channel_id=1, source_target_pairs={{4,0},{8,4},{12,8},{16,12},{20,16},{24,20},{28,24},{32,28},{36,32}... | collective-permute-start | bytes 196616 | tf_op jit(solution)/shard_map/ppermute | solution.py:427
  33.5 7.0 %collective-permute-start.3 = (f32[128,128]{1,0:T(8,128)S(1)}, f32[128,128]{1,0:T(8,128)S(1)}, u32[]{:S(2)}, u32[]{:S(2)}) collective-permute-start(f32[128,128]{1,0:T(8,128)S(1)} %get-tuple-element.58.my_product.mine), channel_id=1, source_target_pairs={{0,32},{4,36},{8,40},{12,44},{16,48},{20,52},{24,56},{28,60},{32,0... | collective-permute-start | bytes 196616 | tf_op jit(solution)/shard_map/ppermute | solution.py:445
  41.2 19.4 %collective-permute-start.8 = (f32[128,128]{1,0:T(8,128)S(1)}, f32[128,128]{1,0:T(8,128)S(1)}, u32[]{:S(2)}, u32[]{:S(2)}) collective-permute-start(f32[128,128]{1,0:T(8,128)S(1)} %pair_product.1), channel_id=1, source_target_pairs={{0,128},{4,132},{8,136},{12,140},{16,144},{20,148},{24,152},{28,15... | collective-permute-start | bytes 196616 | tf_op jit(solution)/shard_map/ppermute | solution.py:450
  49.7 24.3 %copy-start.11 = (f32[512,128]{1,0:T(8,128)S(1)}, f32[512,128]{1,0:T(8,128)}, u32[]{:S(2)}) copy-start(f32[512,128]{1,0:T(8,128)} %get-tuple-element.54) | copy-start | bytes 786436
  49.7 3.8 %collective-permute-start.2 = (f32[64,128]{1,0:T(8,128)S(1)}, f32[64,128]{1,0:T(8,128)S(1)}, u32[]{:S(2)}, u32[]{:S(2)}) collective-permute-start(f32[64,128]{1,0:T(8,128)S(1)} %get-tuple-element.57.mine), channel_id=1, source_target_pairs={{0,32},{4,36},{8,40},{12,44},{16,48},{20,52},{24,56},{28,60},{32,0... | collective-permute-start | bytes 98312 | tf_op jit(solution)/shard_map/ppermute | solution.py:459
  50.3 10.4 %collective-permute-start.7 = (f32[128,128]{1,0:T(8,128)S(1)}, f32[128,128]{1,0:T(8,128)S(1)}, u32[]{:S(2)}, u32[]{:S(2)}) collective-permute-start(f32[128,128]{1,0:T(8,128)S(1)} %pair_product.1), channel_id=1, source_target_pairs={{0,64},{4,68},{8,72},{12,76},{16,80},{20,84},{24,88},{28,92},{32,9... | collective-permute-start | bytes 196616 | tf_op jit(solution)/shard_map/ppermute | solution.py:450
  54.2 6.5 %collective-permute-start.6 = (f32[64,128]{1,0:T(8,128)S(1)}, f32[64,128]{1,0:T(8,128)S(1)}, u32[]{:S(2)}, u32[]{:S(2)}) collective-permute-start(f32[64,128]{1,0:T(8,128)S(1)} %pair.1), channel_id=1, source_target_pairs={{0,192},{4,196},{8,200},{12,204},{16,208},{20,212},{24,216},{28,22... | collective-permute-start | bytes 98312 | tf_op jit(solution)/shard_map/ppermute | solution.py:464
  56.8 3.8 %collective-permute-start.5 = (f32[64,128]{1,0:T(8,128)S(1)}, f32[64,128]{1,0:T(8,128)S(1)}, u32[]{:S(2)}, u32[]{:S(2)}) collective-permute-start(f32[64,128]{1,0:T(8,128)S(1)} %pair.1), channel_id=1, source_target_pairs={{0,128},{4,132},{8,136},{12,140},{16,144},{20,148},{24,152},{28,15... | collective-permute-start | bytes 98312 | tf_op jit(solution)/shard_map/ppermute | solution.py:464
  58.1 3.5 %collective-permute-start.4 = (f32[64,128]{1,0:T(8,128)S(1)}, f32[64,128]{1,0:T(8,128)S(1)}, u32[]{:S(2)}, u32[]{:S(2)}) collective-permute-start(f32[64,128]{1,0:T(8,128)S(1)} %pair.1), channel_id=1, source_target_pairs={{0,64},{4,68},{8,72},{12,76},{16,80},{20,84},{24,88},{28,92},{32,9... | collective-permute-start | bytes 98312 | tf_op jit(solution)/shard_map/ppermute | solution.py:464
  79.3 22.7 %copy-start.1 = (bf16[4,3,3,128,128]{4,3,2,1,0:T(8,128)(2,1)S(1)}, bf16[4,3,3,128,128]{4,3,2,1,0:T(8,128)(2,1)}, u32[]{:S(2)}) copy-start(bf16[4,3,3,128,128]{4,3,2,1,0:T(8,128)(2,1)} %param.5) | copy-start | bytes 3538948
  79.4 9.6 %all-to-all-start.3 = ((f32[8,64,128]{2,1,0:T(8,128)}), f32[8,64,128]{2,1,0:T(8,128)S(1)}, u32[]{:S(2)}, u32[]{:S(2)}) async-start(f32[8,64,128]{2,1,0:T(8,128)} %bitcast.24), calls=%async_computation.3 | async-start | bytes 524288 | tf_op jit(solution)/shard_map/all_to_all | solution.py:397
  82.9 19.1 %collective-permute-start.14 = (f32[512,128]{1,0:T(8,128)S(1)}, f32[512,128]{1,0:T(8,128)S(1)}, u32[]{:S(2)}, u32[]{:S(2)}) collective-permute-start(f32[512,128]{1,0:T(8,128)S(1)} %bitcast_add_fusion.1.corrected), channel_id=1, source_target_pairs={{0,2},{1,3},{2,0},{3,1},{4,6},{5,7},{6,4},{7,5},{8,10},{9,11},{10,... | collective-permute-start | bytes 786440 | tf_op jit(solution)/shard_map/ppermute | solution.py:476
  90.8 6.6 %collective-permute-start.9 = (f32[64,128]{1,0:T(8,128)S(1)}, f32[64,128]{1,0:T(8,128)S(1)}, u32[]{:S(2)}, u32[]{:S(2)}) collective-permute-start(f32[64,128]{1,0:T(8,128)S(1)} %get-tuple-element.68.mine), channel_id=1, source_target_pairs={{0,32},{4,36},{8,40},{12,44},{16,48},{20,52},{24,56},{28,60},{32,0... | collective-permute-start | bytes 98312 | tf_op jit(solution)/shard_map/ppermute | solution.py:493
  91.4 13.2 %collective-permute-start.13 = (f32[128,128]{1,0:T(8,128)S(1)}, f32[128,128]{1,0:T(8,128)S(1)}, u32[]{:S(2)}, u32[]{:S(2)}) collective-permute-start(f32[128,128]{1,0:T(8,128)S(1)} %pair_product.1), channel_id=1, source_target_pairs={{0,192},{4,196},{8,200},{12,204},{16,208},{20,212},{24,216},{28,22... | collective-permute-start | bytes 196616 | tf_op jit(solution)/shard_map/ppermute | solution.py:450
  98.1 6.5 %collective-permute-start.12 = (f32[64,128]{1,0:T(8,128)S(1)}, f32[64,128]{1,0:T(8,128)S(1)}, u32[]{:S(2)}, u32[]{:S(2)}) collective-permute-start(f32[64,128]{1,0:T(8,128)S(1)} %back_pair.1), channel_id=1, source_target_pairs={{192,0},{196,4},{200,8},{204,12},{208,16},{212,20},{216,24},{220,2... | collective-permute-start | bytes 98312 | tf_op jit(solution)/shard_map/ppermute | solution.py:498
  99.4 6.2 %collective-permute-start.11 = (f32[64,128]{1,0:T(8,128)S(1)}, f32[64,128]{1,0:T(8,128)S(1)}, u32[]{:S(2)}, u32[]{:S(2)}) collective-permute-start(f32[64,128]{1,0:T(8,128)S(1)} %back_pair.1), channel_id=1, source_target_pairs={{128,0},{132,4},{136,8},{140,12},{144,16},{148,20},{152,24},{156,2... | collective-permute-start | bytes 98312 | tf_op jit(solution)/shard_map/ppermute | solution.py:498
  100.7 4.9 %collective-permute-start.10 = (f32[64,128]{1,0:T(8,128)S(1)}, f32[64,128]{1,0:T(8,128)S(1)}, u32[]{:S(2)}, u32[]{:S(2)}) collective-permute-start(f32[64,128]{1,0:T(8,128)S(1)} %back_pair.1), channel_id=1, source_target_pairs={{64,0},{68,4},{72,8},{76,12},{80,16},{84,20},{88,24},{92,28},{96,3... | collective-permute-start | bytes 98312 | tf_op jit(solution)/shard_map/ppermute | solution.py:498
  102.0 19.1 %copy-start.9 = (bf16[4,2,18,16,128]{4,3,2,1,0:T(8,128)(2,1)S(1)}, bf16[4,2,18,16,128]{4,3,2,1,0:T(8,128)(2,1)}, u32[]{:S(2)}) copy-start(bf16[4,2,18,16,128]{4,3,2,1,0:T(8,128)(2,1)} %get-tuple-element.74.refs_2_) | copy-start | bytes 1769476
  118.4 13.4 %collective-permute-start.15 = (f32[512,128]{1,0:T(8,128)S(1)}, f32[512,128]{1,0:T(8,128)S(1)}, u32[]{:S(2)}, u32[]{:S(2)}) collective-permute-start(f32[512,128]{1,0:T(8,128)S(1)} %bitcast_add_fusion.refs_0_), channel_id=1, source_target_pairs={{0,2},{1,3},{2,0},{3,1},{4,6},{5,7},{6,4},{7,5},{8,10},{9,11},{10,... | collective-permute-start | bytes 786440 | tf_op jit(solution)/shard_map/ppermute | solution.py:514
  133.0 12.1 %collective-permute-start.17 = (f32[2,1160,128]{2,1,0:T(8,128)S(1)}, f32[2,1160,128]{2,1,0:T(8,128)S(1)}, u32[]{:S(2)}, u32[]{:S(2)}) collective-permute-start(f32[2,1160,128]{2,1,0:T(8,128)S(1)} %get-tuple-element.81.mine), channel_id=1, source_target_pairs={{0,1},{1,0},{2,3},{3,2},{4,5},{5,4},{6,7},{7,6},{8,9},{9,8},{10,11... | collective-permute-start | bytes 3563528 | tf_op jit(solution)/shard_map/ppermute | solution.py:525
  143.6 3.3 %collective-permute-start.16 = (f32[2,1160,128]{2,1,0:T(8,128)S(1)}, f32[2,1160,128]{2,1,0:T(8,128)S(1)}, u32[]{:S(2)}, u32[]{:S(2)}) collective-permute-start(f32[2,1160,128]{2,1,0:T(8,128)S(1)} %other_early.1.mine), channel_id=1, source_target_pairs={{0,1},{1,0},{2,3},{3,2},{4,5},{5,4},{6,7},{7,6},{8,9},{9,8},{10,11... | collective-permute-start | bytes 3563528 | tf_op jit(solution)/shard_map/ppermute | solution.py:533
  (9 other events, 94.3 us)

commit v4 on v2

--- a/solution.py
+++ b/solution.py
@@ -36,16 +36,16 @@
 
 def convolve(ref, value, kernel):
     images, height, width, lanes = ref.shape
-    ref[:, 1 : height - 1] = shifted_columns(value, width).reshape(images, height - 2, width, lanes)
-    total = None
-    for row_at in range(3):
-        part = jnp.dot(
-            rows_from(ref, row_at),
-            kernel[row_at * lanes : (row_at + 1) * lanes],
-            preferred_element_type=f32,
+    rows = (height - 2) * width
+    parts = []
+    for image in range(images):
+        moved = shifted_columns(value[image * rows : (image + 1) * rows], width)
+        ref[image, 1 : height - 1] = moved.reshape(height - 2, width, lanes)
+        window = [ref[image, at : at + height - 2].reshape(rows, lanes) for at in range(3)]
+        parts.append(
+            jnp.dot(jnp.concatenate(window, axis=1), kernel[...], preferred_element_type=f32)
         )
-        total = part if total is None else total + part
-    return total
+    return jnp.concatenate(parts, axis=0)
 
 
 def split(value):
@@ -198,7 +198,10 @@
     payload[...] = error
 
 
-def replay_body(spot, theirs, far1, far2, far3, locals_in, prefix_in, out, prefix, sem):
+def replay_body(
+    spot, theirs, far1, far2, far3, locals_in, prefix_in, result, prefix, out, sem, sems
+):
+    stores = [pltpu.make_async_copy(out.at[at], result.at[at], sems.at[at]) for at in range(GROUP)]
     copy = pltpu.make_async_copy(prefix_in, prefix, sem)
     copy.start()
     part = out.shape[1]
@@ -209,15 +212,20 @@
     longer = error + (times(error, theirs[part:]) + theirs[:part])
     error = jnp.where(spot[1] == 1, longer, error)
     out[0] = error
+    stores[0].start()
     copy.wait()
     for index in range(1, GROUP):
         out[index] = error + (times(error, prefix[index]) + locals_in[index])
+        stores[index].start()
+    for store in stores:
+        store.wait()
 
 
 def back_replay_body(
     spot, theirs, far1, far2, far3, theirs_full, full1, full2, locals_in, suffix_in,
-    out, suffix, sem,
+    result, suffix, out, sem, sems,
 ):
+    stores = [pltpu.make_async_copy(out.at[at], result.at[at], sems.at[at]) for at in range(GROUP)]
     copy = pltpu.make_async_copy(suffix_in, suffix, sem)
     copy.start()
     part = out.shape[1]
@@ -227,9 +235,13 @@
     longer = error + (times(error, theirs_full[part:], True) + theirs[...])
     error = jnp.where(spot[1] == 0, longer, error)
     out[GROUP - 1] = error
+    stores[GROUP - 1].start()
     copy.wait()
     for index in range(GROUP - 1):
         out[index] = error + (times(error, suffix[index], True) + locals_in[index])
+        stores[index].start()
+    for store in stores:
+        store.wait()
 
 
 def forward_sweep(state, weights, biases, ref, inputs, slopes, stores, fetches=None):
@@ -258,13 +270,12 @@
 
 
 def middle_body(
-    error, starts_in, ends_in, back_in, weights_in, transposed_in, biases_in,
-    corrected_out, ends_out, inputs_out, slopes_out, residual_out,
-    ref, corrected, ends, inputs, slopes, starts, ends_adj, back, weights, transposed, biases,
-    sems, loads,
+    corrected, ends_in, back_in, weights_in, transposed_in, biases_in,
+    ends_out, inputs_out, slopes_out, residual_out,
+    ref, ends, inputs, slopes, ends_adj, back, weights, transposed, biases, sems, loads,
 ):
     blocks = weights.shape[0]
-    pairs = [(starts_in, starts), (biases_in, biases)]
+    pairs = [(biases_in, biases)]
     pairs += [(weights_in.at[index], weights.at[index]) for index in range(blocks)]
     pairs += [(transposed_in, transposed), (ends_in, ends_adj), (back_in, back)]
     fetches = [pltpu.make_async_copy(a, b, loads.at[at]) for at, (a, b) in enumerate(pairs)]
@@ -273,23 +284,19 @@
     clear_border(ref)
     stores = sweep_stores(inputs, slopes, inputs_out, slopes_out, sems)
     fetches[0].wait()
-    fetches[1].wait()
-    corrected[...] = starts[...] + error[...]
-    first = pltpu.make_async_copy(corrected, corrected_out, sems.at[2 * blocks])
-    first.start()
     ends[...] = forward_sweep(
-        corrected[...], weights, biases, ref, inputs, slopes, stores, fetches[2 : 2 + blocks]
-    )
-    for fetch in fetches[2 + blocks :]:
+        corrected[...], weights, biases, ref, inputs, slopes, stores, fetches[1 : 1 + blocks]
+    )
+    for fetch in fetches[1 + blocks :]:
         fetch.wait()
-    last = pltpu.make_async_copy(ends, ends_out, sems.at[2 * blocks + 1])
+    last = pltpu.make_async_copy(ends, ends_out, sems.at[2 * blocks])
     last.start()
     adjoint = ends_adj[...]
     for index in reversed(range(blocks)):
         change = slopes[index] * adjoint
         adjoint = adjoint + convolve(ref, change, transposed.at[index])
     residual_out[...] = adjoint - back[...]
-    for store in sum(stores, [first, last]):
+    for store in sum(stores, [last]):
         store.wait()
 
 
@@ -347,23 +354,20 @@
         adjoint_out[...] = adjoint
 
 
-def join_body(first, mine, theirs, late_offsets, kernels_out, offsets_out, total, sems):
+def join_body(first, mine, theirs, late, kernels_out, offsets_out, total, offsets, sems):
     size = kernels_out.shape[1]
     count = mine.shape[0]
-    part = size // 3
-    copies = []
+    offsets[:count] = mine[:, size] + theirs[:, size]
+    if late is not None:
+        offsets[count:] = late[...]
+    copies = [pltpu.make_async_copy(offsets, offsets_out, sems.at[count])]
+    copies[0].start()
     for index in range(count):
-        for at in range(3):
-            rows = pl.ds(at * part, part)
-            total[index, rows] = mine[index, rows] + theirs[index, rows]
-            copy = pltpu.make_async_copy(
-                total.at[index, rows], kernels_out.at[first + index, rows], sems.at[3 * index + at]
-            )
-            copy.start()
-            copies.append(copy)
-    offsets_out[:count] = mine[:, size] + theirs[:, size]
-    if late_offsets is not None:
-        offsets_out[count:] = late_offsets[...]
+        total[index] = mine[index, :size] + theirs[index, :size]
+        copies.append(
+            pltpu.make_async_copy(total.at[index], kernels_out.at[first + index], sems.at[index])
+        )
+        copies[-1].start()
     for copy in copies:
         copy.wait()
 
@@ -434,11 +438,13 @@
         scratch=[ref], flops=blocks * per_conv, name="start",
     )
     first = exchange(payload, near)
-    first, after = lax.optimization_barrier((first, after))
     starts, ends_adj, back = call(
         ends_body, [kept] * 3, field, cotangent, own, before, after, name="ends"
     )
     (transposed,) = call(flip_body, [stored(sweep_shape, bf16)], flat, name="flip")
+    first, starts, ends_adj, back, transposed = lax.optimization_barrier(
+        (first, starts, ends_adj, back, transposed)
+    )
     full, prefixes = call(total_body, [both, pieces_shape], first, name="total")
     their_full = lax.ppermute(full, "layer", pair)
     (pair_full,) = call(
@@ -449,33 +455,33 @@
     prefix, suffix = call(
         lambda *refs: products_body(part, *refs), [matrices] * 2, first, name="products"
     )
-    replay_scratch = [pltpu.VMEM((GROUP, channels, channels), f32), dma(())]
+    replay_scratch = [
+        pltpu.VMEM((GROUP, channels, channels), f32), pltpu.VMEM((GROUP, part, channels), f32),
+        dma(()), dma((GROUP,)),
+    ]
     (error,) = call(
         replay_body, [pieces_kept], spot, their_full, *around_full, prefixes, in_hbm(prefix),
-        ins=[SMEM] + [VMEM] * 5 + [HBM], scratch=replay_scratch, name="replay",
-    )
-    error, suffix, ends_adj, back, transposed, starts = lax.optimization_barrier(
-        (error, suffix, ends_adj, back, transposed, starts)
-    )
-    error = exchange(error, near).reshape(rows, channels)
-
-    corrected, interval_ends, inputs, slopes, adj_residual = call(
-        middle_body, [kept, result, stored(inputs_dims, bf16), stored(slopes_dims), kept],
-        error, in_hbm(starts), in_hbm(ends_adj), in_hbm(back), in_hbm(kernels),
+        ins=[SMEM] + [VMEM] * 5 + [HBM], out_specs=[HBM], scratch=replay_scratch, name="replay",
+    )
+    error, suffix = lax.optimization_barrier((error, suffix))
+    corrected = starts + exchange(error, near).reshape(rows, channels)
+    other_corrected = lax.ppermute(corrected, "dp", partner)
+
+    interval_ends, inputs, slopes, adj_residual = call(
+        middle_body, [result, stored(inputs_dims, bf16), stored(slopes_dims), kept],
+        corrected, in_hbm(ends_adj), in_hbm(back), in_hbm(kernels),
         in_hbm(transposed), in_hbm(biases),
-        ins=[VMEM] + [HBM] * 6, out_specs=[HBM, HBM, HBM, HBM, VMEM],
-        scratch=[ref] + [pltpu.VMEM((rows, channels), f32)] * 2 + sweep_scratch
-        + [pltpu.VMEM((rows, channels), f32)] * 3 + [pltpu.VMEM(sweep_shape, bf16)] * 2
-        + [pltpu.VMEM((blocks, channels), f32), dma((2 * blocks + 2,)), dma((blocks + 5,))],
+        ins=[VMEM] + [HBM] * 5, out_specs=[HBM, HBM, HBM, VMEM],
+        scratch=[ref, pltpu.VMEM((rows, channels), f32)] + sweep_scratch
+        + [pltpu.VMEM((rows, channels), f32)] * 2 + [pltpu.VMEM(sweep_shape, bf16)] * 2
+        + [pltpu.VMEM((blocks, channels), f32), dma((2 * blocks + 1,)), dma((blocks + 4,))],
         flops=2 * blocks * per_conv, name="middle",
     )
-    other_corrected = lax.ppermute(corrected, "dp", partner)
     pieces = exchange(adj_residual.reshape(GROUP, part, channels), near)
     total, prefixes = call(
         lambda *refs: back_total_body(part, *refs), [piece, pieces_kept], pieces, first,
         name="back_total",
     )
-    total, other_corrected = lax.optimization_barrier((total, other_corrected))
     their_total = lax.ppermute(total, "layer", pair)
     (pair_total,) = call(
         lambda *refs: back_pair_body(part, *refs), [piece],
@@ -490,7 +496,8 @@
     (adj_error,) = call(
         back_replay_body, [pieces_kept], spot, their_total, *down_total, their_full,
         around_full[2], around_full[1], prefixes, in_hbm(suffix),
-        ins=[SMEM] + [VMEM] * 8 + [HBM], scratch=replay_scratch, name="back_replay",
+        ins=[SMEM] + [VMEM] * 8 + [HBM], out_specs=[HBM], scratch=replay_scratch,
+        name="back_replay",
     )
     adj_error, other_inputs, other_slopes = lax.optimization_barrier(
         (adj_error, other_inputs, other_slopes)
@@ -516,18 +523,19 @@
         scratch=[ref], flops=blocks * per_conv, name="other_early",
     )
     their_early = lax.ppermute(early, "dp", sibling)
-    join_scratch = [pltpu.VMEM((half, 9 * channels, channels), f32), dma((3 * half,))]
+    sums = pltpu.VMEM((half, 9 * channels, channels), f32)
     weight_grad, late_offsets = call(
         lambda mine, theirs, *refs: join_body(half, mine, theirs, None, *refs),
         [gradients, half_offsets], late, their_late,
-        out_specs=[HBM, VMEM], scratch=join_scratch, name="join_late",
+        out_specs=[HBM, HBM], name="join_late",
+        scratch=[sums, pltpu.VMEM((half, channels), f32), dma((half + 1,))],
     )
     weight_grad, bias_grad = call(
         lambda mine, theirs, offsets, _, *refs: join_body(0, mine, theirs, offsets, *refs),
         [gradients, jax.ShapeDtypeStruct((blocks, channels), f32)],
         early, their_early, late_offsets, weight_grad,
-        ins=[VMEM, VMEM, VMEM, HBM], out_specs=[HBM, VMEM], scratch=join_scratch,
-        aliases={3: 0}, name="join_early",
+        ins=[VMEM, VMEM, VMEM, HBM], out_specs=[HBM, HBM], aliases={3: 0}, name="join_early",
+        scratch=[sums, pltpu.VMEM((blocks, channels), f32), dma((half + 1,))],
     )
     dims = (1, count, height, width, channels)
     return (

time: 148 us -> 140 us (0.946)
  starting transfers between devices: 60.2 us -> 48.1 us
  waiting for transfers between devices: 26.2 us -> 32.6 us
  Pallas kernels: 37.8 us -> 35.6 us
    ppermute x1, starting transfers between devices: 13.5 us -> 3.46 us  [shards(): their_total = lax.ppermute(total, 'layer', pair)]
    ppermute x1, waiting for transfers between devices: 1.3 us -> 11.1 us  [shards(): their_total = lax.ppermute(total, 'layer', pair)]
    ppermute x1, waiting for transfers between devices: 3.32 us -> 0.01 us  [shards(): other_corrected = lax.ppermute(corrected, 'dp', partner)]
    ppermute x1, starting transfers between devices: 11.3 us -> 8.07 us  [shards(): their_late = lax.ppermute(late, 'dp', sibling)]
    ppermute x3, waiting for transfers between devices: 0.44 us -> 3.09 us  [shards(): around_full = [lax.ppermute(pair_full, 'layer', to) for to in around]]
    pallas_call x19, Pallas kernels: 37.8 us -> 35.6 us  [call(): pl.pallas_call(body, out_shape=tuple(outs), in_specs=list(ins) if ins els...]
    ppermute x1, waiting for transfers between devices: 6.05 us -> 4.45 us  [shards(): other_moving = lax.ppermute(moving, 'dp', partner)]
  transfers between devices with their start and end apart: 16 -> 16, of which waited for: 10 -> 9; matrix products, arithmetic and copies ran while one was open for 0% -> 0% of each run, Pallas kernels for 11% -> 11%
where the time goes in v4:
time: 140 us
  starting transfers between devices  48.1 us (34%)
  Pallas kernels  35.6 us (25%)
  waiting for transfers between devices  32.6 us (23%)
  blocking collectives  22.1 us (16%)
    pallas_call x19, Pallas kernels, call(): pl.pallas_call(body, out_shape=tuple(outs), in_specs=list(ins) if ins els...  35.6 us
    all_to_all x2, blocking collectives, exchange(): return lax.all_to_all(value, 'layer', 0, 0, axis_index_groups=groups)  22.1 us
    ppermute x1, waiting for transfers between devices, shards(): their_total = lax.ppermute(total, 'layer', pair)  11.1 us
    all_to_all x2, starting transfers between devices, exchange(): return lax.all_to_all(value, 'layer', 0, 0, axis_index_groups=groups)  9.49 us
    ppermute x1, waiting for transfers between devices, shards(): after = lax.ppermute(own, 'layer', [(i + 1, i) for i in range(layers - 1)])  8.98 us
    ppermute x1, starting transfers between devices, shards(): their_late = lax.ppermute(late, 'dp', sibling)  8.07 us
    ppermute x1, starting transfers between devices, shards(): other_corrected = lax.ppermute(corrected, 'dp', partner)  6.4 us
    ppermute x3, starting transfers between devices, shards(): around_full = [lax.ppermute(pair_full, 'layer', to) for to in around]  6.08 us
  transfers between devices with their start and end apart: 16, of which 9 were waited for; matrix products, arithmetic and copies ran while one was open for 0% of the time, Pallas kernels for 11%

profile of v4, /device:TPU:1, one launch (start us, length us, event | category | flops | bytes accessed | tf_op | source)
XLA Modules:
  0.0 139.7 jit_solution(5434174442715190324)
XLA Ops:
  1.6 3.9 %collective-permute-start = (f32[128,128]{1,0:T(8,128)S(1)}, f32[128,128]{1,0:T(8,128)S(1)}, u32[]{:S(2)}, u32[]{:S(2)}) collective-permute-start(f32[128,128]{1,0:T(8,128)S(1)} %coarse.1.own), channel_id=1, source_target_pairs={{0,4},{4,8},{8,12},{12,16},{16,20},{20,24},{24,28},{28,32},{32,36}... | collective-permute-start | bytes 196616 | tf_op jit(solution)/shard_map/ppermute | solution.py:427
  7.0 2.9 %start.1 = f32[8,192,128]{2,1,0:T(8,128)} custom-call(f32[512,128]{1,0:T(8,128)S(1)} %get-tuple-element.41.images, f32[128,128]{1,0:T(8,128)S(1)} %coarse.1.own, f32[128,128]{1,0:T(8,128)S(1)} %collective-permute-done.before, bf16[4,1152,128]{2,1,0:T(8,128)(2,1)S(1)} %bitcast.20, f32[4,128]{1,0:T(4,128)S(1)} %get-tuple-element.43.biases), custom_call_target="tpu_custom_call" | custom-call | flops 603979776 | bytes 2361344 | tf_op jit(solution)/shard_map/start/pallas_call | solution.py:73
  9.9 5.9 %all-to-all-start = ((f32[8,192,128]{2,1,0:T(8,128)}), f32[8,192,128]{2,1,0:T(8,128)S(1)}, u32[]{:S(2)}, u32[]{:S(2)}) async-start(f32[8,192,128]{2,1,0:T(8,128)} %start.1), calls=%async_computation | async-start | bytes 1572864 | tf_op jit(solution)/shard_map/all_to_all | solution.py:396
  18.5 9.0 %collective-permute-done.1.after = f32[128,128]{1,0:T(8,128)S(1)} collective-permute-done((f32[128,128]{1,0:T(8,128)S(1)}, f32[128,128]{1,0:T(8,128)S(1)}, u32[]{:S(2)}, u32[]{:S(2)}) %collective-permute-start.1) | collective-permute-done | bytes 65568 | tf_op jit(solution)/shard_map/ppermute | solution.py:428
  30.0 3.2 %collective-permute-start.2 = (f32[192,128]{1,0:T(8,128)S(1)}, f32[192,128]{1,0:T(8,128)S(1)}, u32[]{:S(2)}, u32[]{:S(2)}) collective-permute-start(f32[192,128]{1,0:T(8,128)S(1)} %get-tuple-element.50.refs_1_.refs_3_), channel_id=1, source_target_pairs={{0,32},{4,36},{8,40},{12,44},{16,48},{20,52},{24,56},{28,60},{32,0... | collective-permute-start | bytes 294920 | tf_op jit(solution)/shard_map/ppermute | solution.py:449
  33.3 1.9 %collective-permute-done.2.refs_2_.theirs.refs_4_.theirs_full = f32[192,128]{1,0:T(8,128)S(1)} collective-permute-done((f32[192,128]{1,0:T(8,128)S(1)}, f32[192,128]{1,0:T(8,128)S(1)}, u32[]{:S(2)}, u32[]{:S(2)}) %collective-permute-start.2) | collective-permute-done | bytes 98336 | tf_op jit(solution)/shard_map/ppermute | solution.py:449
  36.0 5.3 %collective-permute-start.5 = (f32[192,128]{1,0:T(8,128)S(1)}, f32[192,128]{1,0:T(8,128)S(1)}, u32[]{:S(2)}, u32[]{:S(2)}) collective-permute-start(f32[192,128]{1,0:T(8,128)S(1)} %pair.1), channel_id=1, source_target_pairs={{0,192},{4,196},{8,200},{12,204},{16,208},{20,212},{24,216},{28,22... | collective-permute-start | bytes 294920 | tf_op jit(solution)/shard_map/ppermute | solution.py:454
  42.1 2.0 %products.1 = (f32[8,128,128]{2,1,0:T(8,128)}, f32[8,128,128]{2,1,0:T(8,128)}) custom-call(f32[8,192,128]{2,1,0:T(8,128)S(1)} %all-to-all-done.pieces.refs_0_.refs_1_), custom_call_target="tpu_custom_call" | custom-call | bytes 1835008 | tf_op jit(solution)/shard_map/products/pallas_call | solution.py:73
  44.0 2.4 %collective-permute-done.4.far2.full2 = f32[192,128]{1,0:T(8,128)S(1)} collective-permute-done((f32[192,128]{1,0:T(8,128)S(1)}, f32[192,128]{1,0:T(8,128)S(1)}, u32[]{:S(2)}, u32[]{:S(2)}) %collective-permute-start.4) | collective-permute-done | bytes 98336 | tf_op jit(solution)/shard_map/ppermute | solution.py:454
  47.1 2.9 %replay.1 = f32[8,64,128]{2,1,0:T(8,128)} custom-call(s32[2]{0:T(128)S(1)} %pad_add_fusion.refs_0_.spot, f32[192,128]{1,0:T(8,128)S(1)} %collective-permute-done.2.refs_2_.theirs.refs_4_.theirs_full, f32[192,128]{1,0:T(8,128)S(1)} %collective-permute-done.3.far1, f32[192,128]{1,0:T(8,128)S(1)} %collective-permute-done.4.far2.full2, ...), custom_call_target="tpu_custom_call" | custom-call | bytes 1441800 | tf_op jit(solution)/shard_map/replay/pallas_call | solution.py:73
  50.0 12.0 %all_to_all.20 = f32[8,64,128]{2,1,0:T(8,128)S(1)} all-to-all(f32[8,64,128]{2,1,0:T(8,128)} %replay.1), channel_id=1, replica_groups={{0,4,8,12,16,20,24,28},{32,36,40,44,48,52,56,60},{64,68,72,76,80,84,88,..., dimensions={0} | all-to-all | bytes 524288 | tf_op jit(solution)/shard_map/all_to_all | solution.py:396
  62.1 5.3 %middle.1 = (f32[512,128]{1,0:T(8,128)}, bf16[4,2,18,16,128]{4,3,2,1,0:T(8,128)(2,1)}, f32[4,512,128]{2,1,0:T(8,128)}, f32[512,128]{1,0:T(8,128)}) custom-call(f32[512,128]{1,0:T(8,128)S(1)} %bitcast_add_fusion.1.corrected, f32[512,128]{1,0:T(8,128)} %get-tuple-element.55.ends_in, f32[512,128]{1,0:T(8,128)} %get-tuple-element.56.back_in, ...), custom_call_target="tpu_custom_call" | custom-call | flops 1207959552 | bytes 5310464 | tf_op jit(solution)/shard_map/middle/pallas_call | solution.py:73
  67.4 3.6 %all-to-all-start.2 = ((f32[8,64,128]{2,1,0:T(8,128)}), f32[8,64,128]{2,1,0:T(8,128)S(1)}, u32[]{:S(2)}, u32[]{:S(2)}) async-start(f32[8,64,128]{2,1,0:T(8,128)} %bitcast.22), calls=%async_computation.2 | async-start | bytes 524288 | tf_op jit(solution)/shard_map/all_to_all | solution.py:396
  71.0 6.4 %collective-permute-start.10 = (f32[512,128]{1,0:T(8,128)S(1)}, f32[512,128]{1,0:T(8,128)S(1)}, u32[]{:S(2)}, u32[]{:S(2)}) collective-permute-start(f32[512,128]{1,0:T(8,128)S(1)} %bitcast_add_fusion.1.corrected), channel_id=1, source_target_pairs={{0,2},{1,3},{2,0},{3,1},{4,6},{5,7},{6,4},{7,5},{8,10},{9,11},{10,... | collective-permute-start | bytes 786440 | tf_op jit(solution)/shard_map/ppermute | solution.py:468
  77.4 1.8 %back_total.1 = (f32[64,128]{1,0:T(8,128)S(1)}, f32[8,64,128]{2,1,0:T(8,128)}) custom-call(f32[8,64,128]{2,1,0:T(8,128)S(1)} %all-to-all-done.2.refs_0_, f32[8,192,128]{2,1,0:T(8,128)S(1)} %all-to-all-done.pieces.refs_0_.refs_1_), custom_call_target="tpu_custom_call" | custom-call | bytes 1343488 | tf_op jit(solution)/shard_map/back_total/pallas_call | solution.py:73
  79.2 3.5 %collective-permute-start.6 = (f32[64,128]{1,0:T(8,128)S(1)}, f32[64,128]{1,0:T(8,128)S(1)}, u32[]{:S(2)}, u32[]{:S(2)}) collective-permute-start(f32[64,128]{1,0:T(8,128)S(1)} %get-tuple-element.60.refs_1_), channel_id=1, source_target_pairs={{0,32},{4,36},{8,40},{12,44},{16,48},{20,52},{24,56},{28,60},{32,0... | collective-permute-start | bytes 98312 | tf_op jit(solution)/shard_map/ppermute | solution.py:485
  82.7 11.1 %collective-permute-done.6.refs_2_.theirs = f32[64,128]{1,0:T(8,128)S(1)} collective-permute-done((f32[64,128]{1,0:T(8,128)S(1)}, f32[64,128]{1,0:T(8,128)S(1)}, u32[]{:S(2)}, u32[]{:S(2)}) %collective-permute-start.6) | collective-permute-done | bytes 32800 | tf_op jit(solution)/shard_map/ppermute | solution.py:485
  98.6 2.5 %again.1 = (bf16[4,2,18,16,128]{4,3,2,1,0:T(8,128)(2,1)}, f32[4,512,128]{2,1,0:T(8,128)}) custom-call(f32[512,128]{1,0:T(8,128)S(1)} %collective-permute-done.10.corrected, bf16[4,1152,128]{2,1,0:T(8,128)(2,1)S(1)} %bitcast.19, f32[4,128]{1,0:T(4,128)S(1)} %get-tuple-element.43.biases), custom_call_target="tpu_custom_call" | custom-call | flops 603979776 | bytes 3082240 | tf_op jit(solution)/shard_map/again/pallas_call | solution.py:73
  102.2 3.3 %back_replay.1 = f32[8,64,128]{2,1,0:T(8,128)} custom-call(s32[2]{0:T(128)S(1)} %pad_add_fusion.refs_0_.spot, f32[64,128]{1,0:T(8,128)S(1)} %collective-permute-done.6.refs_2_.theirs, f32[64,128]{1,0:T(8,128)S(1)} %collective-permute-done.7.far1, f32[64,128]{1,0:T(8,128)S(1)} %collective-permute-done.8.far2, f32[64,128]{1,0:T(8,128)S(1)} %collective-permute-done.9.far3, ...), custom_call_target="tpu_custom_call" | custom-call | bytes 1474568 | tf_op jit(solution)/shard_map/back_replay/pallas_call | solution.py:73
  105.5 10.1 %all_to_all.21 = f32[8,64,128]{2,1,0:T(8,128)S(1)} all-to-all(f32[8,64,128]{2,1,0:T(8,128)} %back_replay.1), channel_id=1, replica_groups={{0,4,8,12,16,20,24,28},{32,36,40,44,48,52,56,60},{64,68,72,76,80,84,88,..., dimensions={0} | all-to-all | bytes 524288 | tf_op jit(solution)/shard_map/all_to_all | solution.py:396
  115.6 2.0 %collective-permute-start.11 = (f32[512,128]{1,0:T(8,128)S(1)}, f32[512,128]{1,0:T(8,128)S(1)}, u32[]{:S(2)}, u32[]{:S(2)}) collective-permute-start(f32[512,128]{1,0:T(8,128)S(1)} %bitcast_add_fusion.refs_0_), channel_id=1, source_target_pairs={{0,2},{1,3},{2,0},{3,1},{4,6},{5,7},{6,4},{7,5},{8,10},{9,11},{10,... | collective-permute-start | bytes 786440 | tf_op jit(solution)/shard_map/ppermute | solution.py:506
  117.6 2.8 %final.1 = (f32[512,128]{1,0:T(8,128)}, f32[4,1160,128]{2,1,0:T(8,128)S(1)}) custom-call(f32[512,128]{1,0:T(8,128)S(1)} %bitcast_add_fusion.refs_0_, bf16[4,1152,128]{2,1,0:T(8,128)(2,1)S(1)} %copy-done.2, bf16[4,2,18,16,128]{4,3,2,1,0:T(8,128)(2,1)S(1)} %copy-done.7, f32[4,512,128]{2,1,0:T(8,128)S(1)} %copy-done.6), custom_call_target="tpu_custom_call" | custom-call | flops 1207959552 | bytes 5718016 | tf_op jit(solution)/shard_map/final/pallas_call | solution.py:73
  120.4 4.5 %collective-permute-done.11.refs_0_ = f32[512,128]{1,0:T(8,128)S(1)} collective-permute-done((f32[512,128]{1,0:T(8,128)S(1)}, f32[512,128]{1,0:T(8,128)S(1)}, u32[]{:S(2)}, u32[]{:S(2)}) %collective-permute-start.11) | collective-permute-done | bytes 262176 | tf_op jit(solution)/shard_map/ppermute | solution.py:506
  126.1 8.1 %collective-permute-start.13 = (f32[2,1160,128]{2,1,0:T(8,128)S(1)}, f32[2,1160,128]{2,1,0:T(8,128)S(1)}, u32[]{:S(2)}, u32[]{:S(2)}) collective-permute-start(f32[2,1160,128]{2,1,0:T(8,128)S(1)} %get-tuple-element.73.mine), channel_id=1, source_target_pairs={{0,1},{1,0},{2,3},{3,2},{4,5},{5,4},{6,7},{7,6},{8,9},{9,8},{10,11... | collective-permute-start | bytes 3563528 | tf_op jit(solution)/shard_map/ppermute | solution.py:517
  (52 shorter events, 22.1 us)
Async XLA Ops:
  1.6 5.4 %collective-permute-start = (f32[128,128]{1,0:T(8,128)S(1)}, f32[128,128]{1,0:T(8,128)S(1)}, u32[]{:S(2)}, u32[]{:S(2)}) collective-permute-start(f32[128,128]{1,0:T(8,128)S(1)} %coarse.1.own), channel_id=1, source_target_pairs={{0,4},{4,8},{8,12},{12,16},{16,20},{20,24},{24,28},{28,32},{32,36}... | collective-permute-start | bytes 196616 | tf_op jit(solution)/shard_map/ppermute | solution.py:427
  9.9 18.9 %all-to-all-start = ((f32[8,192,128]{2,1,0:T(8,128)}), f32[8,192,128]{2,1,0:T(8,128)S(1)}, u32[]{:S(2)}, u32[]{:S(2)}) async-start(f32[8,192,128]{2,1,0:T(8,128)} %start.1), calls=%async_computation | async-start | bytes 1572864 | tf_op jit(solution)/shard_map/all_to_all | solution.py:396
  15.8 11.7 %collective-permute-start.1 = (f32[128,128]{1,0:T(8,128)S(1)}, f32[128,128]{1,0:T(8,128)S(1)}, u32[]{:S(2)}, u32[]{:S(2)}) collective-permute-start(f32[128,128]{1,0:T(8,128)S(1)} %coarse.1.own), channel_id=1, source_target_pairs={{4,0},{8,4},{12,8},{16,12},{20,16},{24,20},{28,24},{32,28},{36,32}... | collective-permute-start | bytes 196616 | tf_op jit(solution)/shard_map/ppermute | solution.py:428
  30.0 5.2 %collective-permute-start.2 = (f32[192,128]{1,0:T(8,128)S(1)}, f32[192,128]{1,0:T(8,128)S(1)}, u32[]{:S(2)}, u32[]{:S(2)}) collective-permute-start(f32[192,128]{1,0:T(8,128)S(1)} %get-tuple-element.50.refs_1_.refs_3_), channel_id=1, source_target_pairs={{0,32},{4,36},{8,40},{12,44},{16,48},{20,52},{24,56},{28,60},{32,0... | collective-permute-start | bytes 294920 | tf_op jit(solution)/shard_map/ppermute | solution.py:449
  36.0 26.1 %copy-start.9 = (f32[512,128]{1,0:T(8,128)S(1)}, f32[512,128]{1,0:T(8,128)}, u32[]{:S(2)}) copy-start(f32[512,128]{1,0:T(8,128)} %get-tuple-element.48) | copy-start | bytes 786436
  36.0 8.0 %collective-permute-start.5 = (f32[192,128]{1,0:T(8,128)S(1)}, f32[192,128]{1,0:T(8,128)S(1)}, u32[]{:S(2)}, u32[]{:S(2)}) collective-permute-start(f32[192,128]{1,0:T(8,128)S(1)} %pair.1), channel_id=1, source_target_pairs={{0,192},{4,196},{8,200},{12,204},{16,208},{20,212},{24,216},{28,22... | collective-permute-start | bytes 294920 | tf_op jit(solution)/shard_map/ppermute | solution.py:454
  41.3 5.1 %collective-permute-start.4 = (f32[192,128]{1,0:T(8,128)S(1)}, f32[192,128]{1,0:T(8,128)S(1)}, u32[]{:S(2)}, u32[]{:S(2)}) collective-permute-start(f32[192,128]{1,0:T(8,128)S(1)} %pair.1), channel_id=1, source_target_pairs={{0,128},{4,132},{8,136},{12,140},{16,144},{20,148},{24,152},{28,15... | collective-permute-start | bytes 294920 | tf_op jit(solution)/shard_map/ppermute | solution.py:454
  41.4 5.7 %collective-permute-start.3 = (f32[192,128]{1,0:T(8,128)S(1)}, f32[192,128]{1,0:T(8,128)S(1)}, u32[]{:S(2)}, u32[]{:S(2)}) collective-permute-start(f32[192,128]{1,0:T(8,128)S(1)} %pair.1), channel_id=1, source_target_pairs={{0,64},{4,68},{8,72},{12,76},{16,80},{20,84},{24,88},{28,92},{32,9... | collective-permute-start | bytes 294920 | tf_op jit(solution)/shard_map/ppermute | solution.py:454
  67.4 31.2 %copy-start.1 = (bf16[4,3,3,128,128]{4,3,2,1,0:T(8,128)(2,1)S(1)}, bf16[4,3,3,128,128]{4,3,2,1,0:T(8,128)(2,1)}, u32[]{:S(2)}) copy-start(bf16[4,3,3,128,128]{4,3,2,1,0:T(8,128)(2,1)} %param.5) | copy-start | bytes 3538948
  67.4 10.0 %all-to-all-start.2 = ((f32[8,64,128]{2,1,0:T(8,128)}), f32[8,64,128]{2,1,0:T(8,128)S(1)}, u32[]{:S(2)}, u32[]{:S(2)}) async-start(f32[8,64,128]{2,1,0:T(8,128)} %bitcast.22), calls=%async_computation.2 | async-start | bytes 524288 | tf_op jit(solution)/shard_map/all_to_all | solution.py:396
  71.0 27.6 %collective-permute-start.10 = (f32[512,128]{1,0:T(8,128)S(1)}, f32[512,128]{1,0:T(8,128)S(1)}, u32[]{:S(2)}, u32[]{:S(2)}) collective-permute-start(f32[512,128]{1,0:T(8,128)S(1)} %bitcast_add_fusion.1.corrected), channel_id=1, source_target_pairs={{0,2},{1,3},{2,0},{3,1},{4,6},{5,7},{6,4},{7,5},{8,10},{9,11},{10,... | collective-permute-start | bytes 786440 | tf_op jit(solution)/shard_map/ppermute | solution.py:468
  79.2 14.6 %collective-permute-start.6 = (f32[64,128]{1,0:T(8,128)S(1)}, f32[64,128]{1,0:T(8,128)S(1)}, u32[]{:S(2)}, u32[]{:S(2)}) collective-permute-start(f32[64,128]{1,0:T(8,128)S(1)} %get-tuple-element.60.refs_1_), channel_id=1, source_target_pairs={{0,32},{4,36},{8,40},{12,44},{16,48},{20,52},{24,56},{28,60},{32,0... | collective-permute-start | bytes 98312 | tf_op jit(solution)/shard_map/ppermute | solution.py:485
  94.5 7.6 %copy-start.5 = (f32[8,64,128]{2,1,0:T(8,128)S(1)}, f32[8,64,128]{2,1,0:T(8,128)}, u32[]{:S(2)}) copy-start(f32[8,64,128]{2,1,0:T(8,128)} %get-tuple-element.61.locals_in) | copy-start | bytes 786436
  94.6 6.6 %collective-permute-start.9 = (f32[64,128]{1,0:T(8,128)S(1)}, f32[64,128]{1,0:T(8,128)S(1)}, u32[]{:S(2)}, u32[]{:S(2)}) collective-permute-start(f32[64,128]{1,0:T(8,128)S(1)} %back_pair.1), channel_id=1, source_target_pairs={{192,0},{196,4},{200,8},{204,12},{208,16},{212,20},{216,24},{220,2... | collective-permute-start | bytes 98312 | tf_op jit(solution)/shard_map/ppermute | solution.py:490
  96.0 6.2 %collective-permute-start.8 = (f32[64,128]{1,0:T(8,128)S(1)}, f32[64,128]{1,0:T(8,128)S(1)}, u32[]{:S(2)}, u32[]{:S(2)}) collective-permute-start(f32[64,128]{1,0:T(8,128)S(1)} %back_pair.1), channel_id=1, source_target_pairs={{128,0},{132,4},{136,8},{140,12},{144,16},{148,20},{152,24},{156,2... | collective-permute-start | bytes 98312 | tf_op jit(solution)/shard_map/ppermute | solution.py:490
  97.3 4.9 %collective-permute-start.7 = (f32[64,128]{1,0:T(8,128)S(1)}, f32[64,128]{1,0:T(8,128)S(1)}, u32[]{:S(2)}, u32[]{:S(2)}) collective-permute-start(f32[64,128]{1,0:T(8,128)S(1)} %back_pair.1), channel_id=1, source_target_pairs={{64,0},{68,4},{72,8},{76,12},{80,16},{84,20},{88,24},{92,28},{96,3... | collective-permute-start | bytes 98312 | tf_op jit(solution)/shard_map/ppermute | solution.py:490
  98.6 19.0 %copy-start.7 = (bf16[4,2,18,16,128]{4,3,2,1,0:T(8,128)(2,1)S(1)}, bf16[4,2,18,16,128]{4,3,2,1,0:T(8,128)(2,1)}, u32[]{:S(2)}) copy-start(bf16[4,2,18,16,128]{4,3,2,1,0:T(8,128)(2,1)} %get-tuple-element.66.refs_2_) | copy-start | bytes 1769476
  101.1 14.4 %copy-start.8 = (f32[512,128]{1,0:T(8,128)S(1)}, f32[512,128]{1,0:T(8,128)}, u32[]{:S(2)}) copy-start(f32[512,128]{1,0:T(8,128)} %get-tuple-element.55.ends_in) | copy-start | bytes 786436
  102.2 15.4 %copy-start.2 = (bf16[4,1152,128]{2,1,0:T(8,128)(2,1)S(1)}, bf16[4,1152,128]{2,1,0:T(8,128)(2,1)}, u32[]{:S(2)}) copy-start(bf16[4,1152,128]{2,1,0:T(8,128)(2,1)} %flip.1.transposed_in.refs_1_.a) | copy-start | bytes 3538948
  102.2 15.4 %copy-start.6 = (f32[4,512,128]{2,1,0:T(8,128)S(1)}, f32[4,512,128]{2,1,0:T(8,128)}, u32[]{:S(2)}) copy-start(f32[4,512,128]{2,1,0:T(8,128)} %get-tuple-element.67.refs_3_) | copy-start | bytes 3145732
  115.6 9.3 %collective-permute-start.11 = (f32[512,128]{1,0:T(8,128)S(1)}, f32[512,128]{1,0:T(8,128)S(1)}, u32[]{:S(2)}, u32[]{:S(2)}) collective-permute-start(f32[512,128]{1,0:T(8,128)S(1)} %bitcast_add_fusion.refs_0_), channel_id=1, source_target_pairs={{0,2},{1,3},{2,0},{3,1},{4,6},{5,7},{6,4},{7,5},{8,10},{9,11},{10,... | collective-permute-start | bytes 786440 | tf_op jit(solution)/shard_map/ppermute | solution.py:506
  117.6 7.3 %copy-start.3 = (f32[4,512,128]{2,1,0:T(8,128)S(1)}, f32[4,512,128]{2,1,0:T(8,128)}, u32[]{:S(2)}) copy-start(f32[4,512,128]{2,1,0:T(8,128)} %get-tuple-element.70.refs_3_.c) | copy-start | bytes 3145732
  126.1 10.6 %collective-permute-start.13 = (f32[2,1160,128]{2,1,0:T(8,128)S(1)}, f32[2,1160,128]{2,1,0:T(8,128)S(1)}, u32[]{:S(2)}, u32[]{:S(2)}) collective-permute-start(f32[2,1160,128]{2,1,0:T(8,128)S(1)} %get-tuple-element.73.mine), channel_id=1, source_target_pairs={{0,1},{1,0},{2,3},{3,2},{4,5},{5,4},{6,7},{7,6},{8,9},{9,8},{10,11... | collective-permute-start | bytes 3563528 | tf_op jit(solution)/shard_map/ppermute | solution.py:517
  135.1 3.3 %collective-permute-start.12 = (f32[2,1160,128]{2,1,0:T(8,128)S(1)}, f32[2,1160,128]{2,1,0:T(8,128)S(1)}, u32[]{:S(2)}, u32[]{:S(2)}) collective-permute-start(f32[2,1160,128]{2,1,0:T(8,128)S(1)} %other_early.1.mine), channel_id=1, source_target_pairs={{0,1},{1,0},{2,3},{3,2},{4,5},{5,4},{6,7},{7,6},{8,9},{9,8},{10,11... | collective-permute-start | bytes 3563528 | tf_op jit(solution)/shard_map/ppermute | solution.py:525
  (2 other events, 14.5 us)

commit v5 on v4

--- a/solution.py
+++ b/solution.py
@@ -59,7 +59,9 @@
     high, low = split(value)
     mhigh, mlow = split(matrix)
     dot = lambda a, b: lax.dot_general(a, b, dims, preferred_element_type=f32)
-    return dot(high, mhigh) + (dot(low, mhigh) + dot(high, mlow))
+    rows = value.shape[0]
+    both = dot(jnp.concatenate([high, low], axis=0), mhigh)
+    return both[:rows] + (both[rows:] + dot(high, mlow))
 
 
 VMEM = pl.BlockSpec(memory_space=pltpu.VMEM)
@@ -438,13 +440,12 @@
         scratch=[ref], flops=blocks * per_conv, name="start",
     )
     first = exchange(payload, near)
+    first, after = lax.optimization_barrier((first, after))
     starts, ends_adj, back = call(
         ends_body, [kept] * 3, field, cotangent, own, before, after, name="ends"
     )
     (transposed,) = call(flip_body, [stored(sweep_shape, bf16)], flat, name="flip")
-    first, starts, ends_adj, back, transposed = lax.optimization_barrier(
-        (first, starts, ends_adj, back, transposed)
-    )
+    first, transposed = lax.optimization_barrier((first, transposed))
     full, prefixes = call(total_body, [both, pieces_shape], first, name="total")
     their_full = lax.ppermute(full, "layer", pair)
     (pair_full,) = call(
@@ -463,7 +464,9 @@
         replay_body, [pieces_kept], spot, their_full, *around_full, prefixes, in_hbm(prefix),
         ins=[SMEM] + [VMEM] * 5 + [HBM], out_specs=[HBM], scratch=replay_scratch, name="replay",
     )
-    error, suffix = lax.optimization_barrier((error, suffix))
+    error, suffix, starts, ends_adj, back = lax.optimization_barrier(
+        (error, suffix, starts, ends_adj, back)
+    )
     corrected = starts + exchange(error, near).reshape(rows, channels)
     other_corrected = lax.ppermute(corrected, "dp", partner)
 

time: 140 us -> 139 us (level)
  no operation moved by 1% of the time
where the time goes in v5:
time: 139 us; the launch traced here: 138 us
  starting transfers between devices  48.1 us (35%)
  Pallas kernels  35 us (25%)
  waiting for transfers between devices  31.5 us (23%)
  blocking collectives  22.1 us (16%)
    pallas_call x19, Pallas kernels, call(): pl.pallas_call(body, out_shape=tuple(outs), in_specs=list(ins) if ins els...  35 us
    all_to_all x2, blocking collectives, exchange(): return lax.all_to_all(value, 'layer', 0, 0, axis_index_groups=groups)  22.1 us
    ppermute x1, waiting for transfers between devices, shards(): their_total = lax.ppermute(total, 'layer', pair)  11.3 us
    all_to_all x2, starting transfers between devices, exchange(): return lax.all_to_all(value, 'layer', 0, 0, axis_index_groups=groups)  9.48 us
    ppermute x1, waiting for transfers between devices, shards(): after = lax.ppermute(own, 'layer', [(i + 1, i) for i in range(layers - 1)])  8.98 us
    ppermute x1, starting transfers between devices, shards(): their_late = lax.ppermute(late, 'dp', sibling)  8.04 us
    ppermute x1, starting transfers between devices, shards(): other_corrected = lax.ppermute(corrected, 'dp', partner)  6.4 us
    ppermute x3, starting transfers between devices, shards(): around_full = [lax.ppermute(pair_full, 'layer', to) for to in around]  6.08 us
  transfers between devices with their start and end apart: 16, of which 9 were waited for; matrix products, arithmetic and copies ran while one was open for 0% of the time, Pallas kernels for 11%

profile of v5, /device:TPU:1, one launch (start us, length us, event | category | flops | bytes accessed | tf_op | source)
XLA Modules:
  0.0 137.9 jit_solution(3543692753410908152)
XLA Ops:
  1.6 3.9 %collective-permute-start = (f32[128,128]{1,0:T(8,128)S(1)}, f32[128,128]{1,0:T(8,128)S(1)}, u32[]{:S(2)}, u32[]{:S(2)}) collective-permute-start(f32[128,128]{1,0:T(8,128)S(1)} %coarse.1.own), channel_id=1, source_target_pairs={{0,4},{4,8},{8,12},{12,16},{16,20},{20,24},{24,28},{28,32},{32,36}... | collective-permute-start | bytes 196616 | tf_op jit(solution)/shard_map/ppermute | solution.py:429
  7.0 2.9 %start.1 = f32[8,192,128]{2,1,0:T(8,128)} custom-call(f32[512,128]{1,0:T(8,128)S(1)} %get-tuple-element.43.images, f32[128,128]{1,0:T(8,128)S(1)} %coarse.1.own, f32[128,128]{1,0:T(8,128)S(1)} %collective-permute-done.before, bf16[4,1152,128]{2,1,0:T(8,128)(2,1)S(1)} %bitcast.20, f32[4,128]{1,0:T(4,128)S(1)} %get-tuple-element.45.biases), custom_call_target="tpu_custom_call" | custom-call | flops 603979776 | bytes 2361344 | tf_op jit(solution)/shard_map/start/pallas_call | solution.py:75
  9.9 5.9 %all-to-all-start = ((f32[8,192,128]{2,1,0:T(8,128)}), f32[8,192,128]{2,1,0:T(8,128)S(1)}, u32[]{:S(2)}, u32[]{:S(2)}) async-start(f32[8,192,128]{2,1,0:T(8,128)} %start.1), calls=%async_computation | async-start | bytes 1572864 | tf_op jit(solution)/shard_map/all_to_all | solution.py:398
  18.5 9.0 %collective-permute-done.1.after = f32[128,128]{1,0:T(8,128)S(1)} collective-permute-done((f32[128,128]{1,0:T(8,128)S(1)}, f32[128,128]{1,0:T(8,128)S(1)}, u32[]{:S(2)}, u32[]{:S(2)}) %collective-permute-start.1) | collective-permute-done | bytes 65568 | tf_op jit(solution)/shard_map/ppermute | solution.py:430
  28.6 3.2 %collective-permute-start.2 = (f32[192,128]{1,0:T(8,128)S(1)}, f32[192,128]{1,0:T(8,128)S(1)}, u32[]{:S(2)}, u32[]{:S(2)}) collective-permute-start(f32[192,128]{1,0:T(8,128)S(1)} %get-tuple-element.48.refs_1_.refs_3_), channel_id=1, source_target_pairs={{0,32},{4,36},{8,40},{12,44},{16,48},{20,52},{24,56},{28,60},{32,0... | collective-permute-start | bytes 294920 | tf_op jit(solution)/shard_map/ppermute | solution.py:450
  32.0 1.9 %collective-permute-done.2.refs_2_.theirs.refs_4_.theirs_full = f32[192,128]{1,0:T(8,128)S(1)} collective-permute-done((f32[192,128]{1,0:T(8,128)S(1)}, f32[192,128]{1,0:T(8,128)S(1)}, u32[]{:S(2)}, u32[]{:S(2)}) %collective-permute-start.2) | collective-permute-done | bytes 98336 | tf_op jit(solution)/shard_map/ppermute | solution.py:450
  34.6 5.3 %collective-permute-start.5 = (f32[192,128]{1,0:T(8,128)S(1)}, f32[192,128]{1,0:T(8,128)S(1)}, u32[]{:S(2)}, u32[]{:S(2)}) collective-permute-start(f32[192,128]{1,0:T(8,128)S(1)} %pair.1), channel_id=1, source_target_pairs={{0,192},{4,196},{8,200},{12,204},{16,208},{20,212},{24,216},{28,22... | collective-permute-start | bytes 294920 | tf_op jit(solution)/shard_map/ppermute | solution.py:455
  40.7 1.9 %products.1 = (f32[8,128,128]{2,1,0:T(8,128)}, f32[8,128,128]{2,1,0:T(8,128)}) custom-call(f32[8,192,128]{2,1,0:T(8,128)S(1)} %all-to-all-done.pieces.refs_0_.refs_1_), custom_call_target="tpu_custom_call" | custom-call | bytes 1835008 | tf_op jit(solution)/shard_map/products/pallas_call | solution.py:75
  45.7 2.9 %replay.1 = f32[8,64,128]{2,1,0:T(8,128)} custom-call(s32[2]{0:T(128)S(1)} %pad_add_fusion.refs_0_.spot, f32[192,128]{1,0:T(8,128)S(1)} %collective-permute-done.2.refs_2_.theirs.refs_4_.theirs_full, f32[192,128]{1,0:T(8,128)S(1)} %collective-permute-done.3.far1, f32[192,128]{1,0:T(8,128)S(1)} %collective-permute-done.4.far2.full2, ...), custom_call_target="tpu_custom_call" | custom-call | bytes 1441800 | tf_op jit(solution)/shard_map/replay/pallas_call | solution.py:75
  48.6 12.0 %all_to_all.20 = f32[8,64,128]{2,1,0:T(8,128)S(1)} all-to-all(f32[8,64,128]{2,1,0:T(8,128)} %replay.1), channel_id=1, replica_groups={{0,4,8,12,16,20,24,28},{32,36,40,44,48,52,56,60},{64,68,72,76,80,84,88,..., dimensions={0} | all-to-all | bytes 524288 | tf_op jit(solution)/shard_map/all_to_all | solution.py:398
  60.7 5.3 %middle.1 = (f32[512,128]{1,0:T(8,128)}, bf16[4,2,18,16,128]{4,3,2,1,0:T(8,128)(2,1)}, f32[4,512,128]{2,1,0:T(8,128)}, f32[512,128]{1,0:T(8,128)}) custom-call(f32[512,128]{1,0:T(8,128)S(1)} %bitcast_add_fusion.1.corrected, f32[512,128]{1,0:T(8,128)} %get-tuple-element.59.ends_in, f32[512,128]{1,0:T(8,128)} %get-tuple-element.60.back_in, ...), custom_call_target="tpu_custom_call" | custom-call | flops 1207959552 | bytes 5310464 | tf_op jit(solution)/shard_map/middle/pallas_call | solution.py:75
  66.0 3.6 %all-to-all-start.2 = ((f32[8,64,128]{2,1,0:T(8,128)}), f32[8,64,128]{2,1,0:T(8,128)S(1)}, u32[]{:S(2)}, u32[]{:S(2)}) async-start(f32[8,64,128]{2,1,0:T(8,128)} %bitcast.22), calls=%async_computation.2 | async-start | bytes 524288 | tf_op jit(solution)/shard_map/all_to_all | solution.py:398
  69.6 6.4 %collective-permute-start.10 = (f32[512,128]{1,0:T(8,128)S(1)}, f32[512,128]{1,0:T(8,128)S(1)}, u32[]{:S(2)}, u32[]{:S(2)}) collective-permute-start(f32[512,128]{1,0:T(8,128)S(1)} %bitcast_add_fusion.1.corrected), channel_id=1, source_target_pairs={{0,2},{1,3},{2,0},{3,1},{4,6},{5,7},{6,4},{7,5},{8,10},{9,11},{10,... | collective-permute-start | bytes 786440 | tf_op jit(solution)/shard_map/ppermute | solution.py:471
  76.0 1.6 %back_total.1 = (f32[64,128]{1,0:T(8,128)S(1)}, f32[8,64,128]{2,1,0:T(8,128)}) custom-call(f32[8,64,128]{2,1,0:T(8,128)S(1)} %all-to-all-done.2.refs_0_, f32[8,192,128]{2,1,0:T(8,128)S(1)} %all-to-all-done.pieces.refs_0_.refs_1_), custom_call_target="tpu_custom_call" | custom-call | bytes 1343488 | tf_op jit(solution)/shard_map/back_total/pallas_call | solution.py:75
  77.6 3.4 %collective-permute-start.6 = (f32[64,128]{1,0:T(8,128)S(1)}, f32[64,128]{1,0:T(8,128)S(1)}, u32[]{:S(2)}, u32[]{:S(2)}) collective-permute-start(f32[64,128]{1,0:T(8,128)S(1)} %get-tuple-element.64.refs_1_), channel_id=1, source_target_pairs={{0,32},{4,36},{8,40},{12,44},{16,48},{20,52},{24,56},{28,60},{32,0... | collective-permute-start | bytes 98312 | tf_op jit(solution)/shard_map/ppermute | solution.py:488
  81.1 11.3 %collective-permute-done.6.refs_2_.theirs = f32[64,128]{1,0:T(8,128)S(1)} collective-permute-done((f32[64,128]{1,0:T(8,128)S(1)}, f32[64,128]{1,0:T(8,128)S(1)}, u32[]{:S(2)}, u32[]{:S(2)}) %collective-permute-start.6) | collective-permute-done | bytes 32800 | tf_op jit(solution)/shard_map/ppermute | solution.py:488
  97.2 2.5 %again.1 = (bf16[4,2,18,16,128]{4,3,2,1,0:T(8,128)(2,1)}, f32[4,512,128]{2,1,0:T(8,128)}) custom-call(f32[512,128]{1,0:T(8,128)S(1)} %collective-permute-done.10.corrected, bf16[4,1152,128]{2,1,0:T(8,128)(2,1)S(1)} %bitcast.19, f32[4,128]{1,0:T(4,128)S(1)} %get-tuple-element.45.biases), custom_call_target="tpu_custom_call" | custom-call | flops 603979776 | bytes 3082240 | tf_op jit(solution)/shard_map/again/pallas_call | solution.py:75
  100.7 3.1 %back_replay.1 = f32[8,64,128]{2,1,0:T(8,128)} custom-call(s32[2]{0:T(128)S(1)} %pad_add_fusion.refs_0_.spot, f32[64,128]{1,0:T(8,128)S(1)} %collective-permute-done.6.refs_2_.theirs, f32[64,128]{1,0:T(8,128)S(1)} %collective-permute-done.7.far1, f32[64,128]{1,0:T(8,128)S(1)} %collective-permute-done.8.far2, f32[64,128]{1,0:T(8,128)S(1)} %collective-permute-done.9.far3, ...), custom_call_target="tpu_custom_call" | custom-call | bytes 1474568 | tf_op jit(solution)/shard_map/back_replay/pallas_call | solution.py:75
  103.8 10.1 %all_to_all.21 = f32[8,64,128]{2,1,0:T(8,128)S(1)} all-to-all(f32[8,64,128]{2,1,0:T(8,128)} %back_replay.1), channel_id=1, replica_groups={{0,4,8,12,16,20,24,28},{32,36,40,44,48,52,56,60},{64,68,72,76,80,84,88,..., dimensions={0} | all-to-all | bytes 524288 | tf_op jit(solution)/shard_map/all_to_all | solution.py:398
  113.9 2.1 %collective-permute-start.11 = (f32[512,128]{1,0:T(8,128)S(1)}, f32[512,128]{1,0:T(8,128)S(1)}, u32[]{:S(2)}, u32[]{:S(2)}) collective-permute-start(f32[512,128]{1,0:T(8,128)S(1)} %bitcast_add_fusion.refs_0_), channel_id=1, source_target_pairs={{0,2},{1,3},{2,0},{3,1},{4,6},{5,7},{6,4},{7,5},{8,10},{9,11},{10,... | collective-permute-start | bytes 786440 | tf_op jit(solution)/shard_map/ppermute | solution.py:509
  116.0 2.8 %final.1 = (f32[512,128]{1,0:T(8,128)}, f32[4,1160,128]{2,1,0:T(8,128)S(1)}) custom-call(f32[512,128]{1,0:T(8,128)S(1)} %bitcast_add_fusion.refs_0_, bf16[4,1152,128]{2,1,0:T(8,128)(2,1)S(1)} %copy-done.2, bf16[4,2,18,16,128]{4,3,2,1,0:T(8,128)(2,1)S(1)} %copy-done.7, f32[4,512,128]{2,1,0:T(8,128)S(1)} %copy-done.6), custom_call_target="tpu_custom_call" | custom-call | flops 1207959552 | bytes 5718016 | tf_op jit(solution)/shard_map/final/pallas_call | solution.py:75
  118.8 4.4 %collective-permute-done.11.refs_0_ = f32[512,128]{1,0:T(8,128)S(1)} collective-permute-done((f32[512,128]{1,0:T(8,128)S(1)}, f32[512,128]{1,0:T(8,128)S(1)}, u32[]{:S(2)}, u32[]{:S(2)}) %collective-permute-start.11) | collective-permute-done | bytes 262176 | tf_op jit(solution)/shard_map/ppermute | solution.py:509
  124.4 8.0 %collective-permute-start.13 = (f32[2,1160,128]{2,1,0:T(8,128)S(1)}, f32[2,1160,128]{2,1,0:T(8,128)S(1)}, u32[]{:S(2)}, u32[]{:S(2)}) collective-permute-start(f32[2,1160,128]{2,1,0:T(8,128)S(1)} %get-tuple-element.77.mine), channel_id=1, source_target_pairs={{0,1},{1,0},{2,3},{3,2},{4,5},{5,4},{6,7},{7,6},{8,9},{9,8},{10,11... | collective-permute-start | bytes 3563528 | tf_op jit(solution)/shard_map/ppermute | solution.py:520
  133.5 1.5 %collective-permute-done.13.theirs = f32[2,1160,128]{2,1,0:T(8,128)S(1)} collective-permute-done((f32[2,1160,128]{2,1,0:T(8,128)S(1)}, f32[2,1160,128]{2,1,0:T(8,128)S(1)}, u32[]{:S(2)}, u32[]{:S(2)}) %collective-permute-start.13) | collective-permute-done | bytes 1187872 | tf_op jit(solution)/shard_map/ppermute | solution.py:520
  (52 shorter events, 21.7 us)
Async XLA Ops:
  1.6 5.4 %collective-permute-start = (f32[128,128]{1,0:T(8,128)S(1)}, f32[128,128]{1,0:T(8,128)S(1)}, u32[]{:S(2)}, u32[]{:S(2)}) collective-permute-start(f32[128,128]{1,0:T(8,128)S(1)} %coarse.1.own), channel_id=1, source_target_pairs={{0,4},{4,8},{8,12},{12,16},{16,20},{20,24},{24,28},{28,32},{32,36}... | collective-permute-start | bytes 196616 | tf_op jit(solution)/shard_map/ppermute | solution.py:429
  9.9 7.2 %copy-start = (bf16[4,3,3,128,128]{4,3,2,1,0:T(8,128)(2,1)S(1)}, bf16[4,3,3,128,128]{4,3,2,1,0:T(8,128)(2,1)}, u32[]{:S(2)}) copy-start(bf16[4,3,3,128,128]{4,3,2,1,0:T(8,128)(2,1)} %param.5) | copy-start | bytes 3538948
  9.9 17.6 %all-to-all-start = ((f32[8,192,128]{2,1,0:T(8,128)}), f32[8,192,128]{2,1,0:T(8,128)S(1)}, u32[]{:S(2)}, u32[]{:S(2)}) async-start(f32[8,192,128]{2,1,0:T(8,128)} %start.1), calls=%async_computation | async-start | bytes 1572864 | tf_op jit(solution)/shard_map/all_to_all | solution.py:398
  15.8 11.7 %collective-permute-start.1 = (f32[128,128]{1,0:T(8,128)S(1)}, f32[128,128]{1,0:T(8,128)S(1)}, u32[]{:S(2)}, u32[]{:S(2)}) collective-permute-start(f32[128,128]{1,0:T(8,128)S(1)} %coarse.1.own), channel_id=1, source_target_pairs={{4,0},{8,4},{12,8},{16,12},{20,16},{24,20},{28,24},{32,28},{36,32}... | collective-permute-start | bytes 196616 | tf_op jit(solution)/shard_map/ppermute | solution.py:430
  28.6 5.3 %collective-permute-start.2 = (f32[192,128]{1,0:T(8,128)S(1)}, f32[192,128]{1,0:T(8,128)S(1)}, u32[]{:S(2)}, u32[]{:S(2)}) collective-permute-start(f32[192,128]{1,0:T(8,128)S(1)} %get-tuple-element.48.refs_1_.refs_3_), channel_id=1, source_target_pairs={{0,32},{4,36},{8,40},{12,44},{16,48},{20,52},{24,56},{28,60},{32,0... | collective-permute-start | bytes 294920 | tf_op jit(solution)/shard_map/ppermute | solution.py:450
  34.6 9.3 %collective-permute-start.5 = (f32[192,128]{1,0:T(8,128)S(1)}, f32[192,128]{1,0:T(8,128)S(1)}, u32[]{:S(2)}, u32[]{:S(2)}) collective-permute-start(f32[192,128]{1,0:T(8,128)S(1)} %pair.1), channel_id=1, source_target_pairs={{0,192},{4,196},{8,200},{12,204},{16,208},{20,212},{24,216},{28,22... | collective-permute-start | bytes 294920 | tf_op jit(solution)/shard_map/ppermute | solution.py:455
  40.0 5.1 %collective-permute-start.4 = (f32[192,128]{1,0:T(8,128)S(1)}, f32[192,128]{1,0:T(8,128)S(1)}, u32[]{:S(2)}, u32[]{:S(2)}) collective-permute-start(f32[192,128]{1,0:T(8,128)S(1)} %pair.1), channel_id=1, source_target_pairs={{0,128},{4,132},{8,136},{12,140},{16,144},{20,148},{24,152},{28,15... | collective-permute-start | bytes 294920 | tf_op jit(solution)/shard_map/ppermute | solution.py:455
  40.0 5.7 %collective-permute-start.3 = (f32[192,128]{1,0:T(8,128)S(1)}, f32[192,128]{1,0:T(8,128)S(1)}, u32[]{:S(2)}, u32[]{:S(2)}) collective-permute-start(f32[192,128]{1,0:T(8,128)S(1)} %pair.1), channel_id=1, source_target_pairs={{0,64},{4,68},{8,72},{12,76},{16,80},{20,84},{24,88},{28,92},{32,9... | collective-permute-start | bytes 294920 | tf_op jit(solution)/shard_map/ppermute | solution.py:455
  43.9 16.7 %copy-start.9 = (f32[512,128]{1,0:T(8,128)S(1)}, f32[512,128]{1,0:T(8,128)}, u32[]{:S(2)}) copy-start(f32[512,128]{1,0:T(8,128)} %get-tuple-element.57) | copy-start | bytes 786436
  66.0 31.2 %copy-start.1 = (bf16[4,3,3,128,128]{4,3,2,1,0:T(8,128)(2,1)S(1)}, bf16[4,3,3,128,128]{4,3,2,1,0:T(8,128)(2,1)}, u32[]{:S(2)}) copy-start(bf16[4,3,3,128,128]{4,3,2,1,0:T(8,128)(2,1)} %param.5) | copy-start | bytes 3538948
  66.0 10.0 %all-to-all-start.2 = ((f32[8,64,128]{2,1,0:T(8,128)}), f32[8,64,128]{2,1,0:T(8,128)S(1)}, u32[]{:S(2)}, u32[]{:S(2)}) async-start(f32[8,64,128]{2,1,0:T(8,128)} %bitcast.22), calls=%async_computation.2 | async-start | bytes 524288 | tf_op jit(solution)/shard_map/all_to_all | solution.py:398
  69.6 27.6 %collective-permute-start.10 = (f32[512,128]{1,0:T(8,128)S(1)}, f32[512,128]{1,0:T(8,128)S(1)}, u32[]{:S(2)}, u32[]{:S(2)}) collective-permute-start(f32[512,128]{1,0:T(8,128)S(1)} %bitcast_add_fusion.1.corrected), channel_id=1, source_target_pairs={{0,2},{1,3},{2,0},{3,1},{4,6},{5,7},{6,4},{7,5},{8,10},{9,11},{10,... | collective-permute-start | bytes 786440 | tf_op jit(solution)/shard_map/ppermute | solution.py:471
  77.6 14.8 %collective-permute-start.6 = (f32[64,128]{1,0:T(8,128)S(1)}, f32[64,128]{1,0:T(8,128)S(1)}, u32[]{:S(2)}, u32[]{:S(2)}) collective-permute-start(f32[64,128]{1,0:T(8,128)S(1)} %get-tuple-element.64.refs_1_), channel_id=1, source_target_pairs={{0,32},{4,36},{8,40},{12,44},{16,48},{20,52},{24,56},{28,60},{32,0... | collective-permute-start | bytes 98312 | tf_op jit(solution)/shard_map/ppermute | solution.py:488
  93.1 7.6 %copy-start.5 = (f32[8,64,128]{2,1,0:T(8,128)S(1)}, f32[8,64,128]{2,1,0:T(8,128)}, u32[]{:S(2)}) copy-start(f32[8,64,128]{2,1,0:T(8,128)} %get-tuple-element.65.locals_in) | copy-start | bytes 786436
  93.1 6.6 %collective-permute-start.9 = (f32[64,128]{1,0:T(8,128)S(1)}, f32[64,128]{1,0:T(8,128)S(1)}, u32[]{:S(2)}, u32[]{:S(2)}) collective-permute-start(f32[64,128]{1,0:T(8,128)S(1)} %back_pair.1), channel_id=1, source_target_pairs={{192,0},{196,4},{200,8},{204,12},{208,16},{212,20},{216,24},{220,2... | collective-permute-start | bytes 98312 | tf_op jit(solution)/shard_map/ppermute | solution.py:493
  94.5 6.2 %collective-permute-start.8 = (f32[64,128]{1,0:T(8,128)S(1)}, f32[64,128]{1,0:T(8,128)S(1)}, u32[]{:S(2)}, u32[]{:S(2)}) collective-permute-start(f32[64,128]{1,0:T(8,128)S(1)} %back_pair.1), channel_id=1, source_target_pairs={{128,0},{132,4},{136,8},{140,12},{144,16},{148,20},{152,24},{156,2... | collective-permute-start | bytes 98312 | tf_op jit(solution)/shard_map/ppermute | solution.py:493
  95.8 4.9 %collective-permute-start.7 = (f32[64,128]{1,0:T(8,128)S(1)}, f32[64,128]{1,0:T(8,128)S(1)}, u32[]{:S(2)}, u32[]{:S(2)}) collective-permute-start(f32[64,128]{1,0:T(8,128)S(1)} %back_pair.1), channel_id=1, source_target_pairs={{64,0},{68,4},{72,8},{76,12},{80,16},{84,20},{88,24},{92,28},{96,3... | collective-permute-start | bytes 98312 | tf_op jit(solution)/shard_map/ppermute | solution.py:493
  97.2 18.8 %copy-start.7 = (bf16[4,2,18,16,128]{4,3,2,1,0:T(8,128)(2,1)S(1)}, bf16[4,2,18,16,128]{4,3,2,1,0:T(8,128)(2,1)}, u32[]{:S(2)}) copy-start(bf16[4,2,18,16,128]{4,3,2,1,0:T(8,128)(2,1)} %get-tuple-element.70.refs_2_) | copy-start | bytes 1769476
  99.7 14.2 %copy-start.8 = (f32[512,128]{1,0:T(8,128)S(1)}, f32[512,128]{1,0:T(8,128)}, u32[]{:S(2)}) copy-start(f32[512,128]{1,0:T(8,128)} %get-tuple-element.59.ends_in) | copy-start | bytes 786436
  100.7 15.3 %copy-start.2 = (bf16[4,1152,128]{2,1,0:T(8,128)(2,1)S(1)}, bf16[4,1152,128]{2,1,0:T(8,128)(2,1)}, u32[]{:S(2)}) copy-start(bf16[4,1152,128]{2,1,0:T(8,128)(2,1)} %flip.1.transposed_in.refs_1_.a) | copy-start | bytes 3538948
  100.7 15.3 %copy-start.6 = (f32[4,512,128]{2,1,0:T(8,128)S(1)}, f32[4,512,128]{2,1,0:T(8,128)}, u32[]{:S(2)}) copy-start(f32[4,512,128]{2,1,0:T(8,128)} %get-tuple-element.71.refs_3_) | copy-start | bytes 3145732
  113.9 9.3 %collective-permute-start.11 = (f32[512,128]{1,0:T(8,128)S(1)}, f32[512,128]{1,0:T(8,128)S(1)}, u32[]{:S(2)}, u32[]{:S(2)}) collective-permute-start(f32[512,128]{1,0:T(8,128)S(1)} %bitcast_add_fusion.refs_0_), channel_id=1, source_target_pairs={{0,2},{1,3},{2,0},{3,1},{4,6},{5,7},{6,4},{7,5},{8,10},{9,11},{10,... | collective-permute-start | bytes 786440 | tf_op jit(solution)/shard_map/ppermute | solution.py:509
  124.4 10.5 %collective-permute-start.13 = (f32[2,1160,128]{2,1,0:T(8,128)S(1)}, f32[2,1160,128]{2,1,0:T(8,128)S(1)}, u32[]{:S(2)}, u32[]{:S(2)}) collective-permute-start(f32[2,1160,128]{2,1,0:T(8,128)S(1)} %get-tuple-element.77.mine), channel_id=1, source_target_pairs={{0,1},{1,0},{2,3},{3,2},{4,5},{5,4},{6,7},{7,6},{8,9},{9,8},{10,11... | collective-permute-start | bytes 3563528 | tf_op jit(solution)/shard_map/ppermute | solution.py:520
  133.4 3.3 %collective-permute-start.12 = (f32[2,1160,128]{2,1,0:T(8,128)S(1)}, f32[2,1160,128]{2,1,0:T(8,128)S(1)}, u32[]{:S(2)}, u32[]{:S(2)}) collective-permute-start(f32[2,1160,128]{2,1,0:T(8,128)S(1)} %other_early.1.mine), channel_id=1, source_target_pairs={{0,1},{1,0},{2,3},{3,2},{4,5},{5,4},{6,7},{7,6},{8,9},{9,8},{10,11... | collective-permute-start | bytes 3563528 | tf_op jit(solution)/shard_map/ppermute | solution.py:528
  (2 other events, 14.4 us)

commit v6 on v5

--- a/solution.py
+++ b/solution.py
@@ -468,7 +468,6 @@
         (error, suffix, starts, ends_adj, back)
     )
     corrected = starts + exchange(error, near).reshape(rows, channels)
-    other_corrected = lax.ppermute(corrected, "dp", partner)
 
     interval_ends, inputs, slopes, adj_residual = call(
         middle_body, [result, stored(inputs_dims, bf16), stored(slopes_dims), kept],
@@ -482,28 +481,28 @@
     )
     pieces = exchange(adj_residual.reshape(GROUP, part, channels), near)
     total, prefixes = call(
-        lambda *refs: back_total_body(part, *refs), [piece, pieces_kept], pieces, first,
+        lambda *refs: back_total_body(part, *refs), [piece, pieces_shape], pieces, first,
         name="back_total",
     )
     their_total = lax.ppermute(total, "layer", pair)
+    their_total, corrected = lax.optimization_barrier((their_total, corrected))
+    other_corrected = lax.ppermute(corrected, "dp", partner)
     (pair_total,) = call(
         lambda *refs: back_pair_body(part, *refs), [piece],
         spot, total, their_total, full, their_full, ins=[SMEM] + [VMEM] * 4, name="back_pair",
     )
     down_total = [lax.ppermute(pair_total, "layer", to) for to in down]
-    other_inputs, other_slopes = call(
-        again_body, [stored(inputs_dims, bf16), stored(slopes_dims)],
-        other_corrected, kernels, offsets, out_specs=[HBM] * 2,
-        scratch=[ref] + sweep_scratch + [dma((2 * blocks,))], flops=blocks * per_conv, name="again",
-    )
     (adj_error,) = call(
         back_replay_body, [pieces_kept], spot, their_total, *down_total, their_full,
         around_full[2], around_full[1], prefixes, in_hbm(suffix),
         ins=[SMEM] + [VMEM] * 8 + [HBM], out_specs=[HBM], scratch=replay_scratch,
         name="back_replay",
     )
-    adj_error, other_inputs, other_slopes = lax.optimization_barrier(
-        (adj_error, other_inputs, other_slopes)
+    adj_error, other_corrected = lax.optimization_barrier((adj_error, other_corrected))
+    other_inputs, other_slopes = call(
+        again_body, [stored(inputs_dims, bf16), stored(slopes_dims)],
+        other_corrected, kernels, offsets, out_specs=[HBM] * 2,
+        scratch=[ref] + sweep_scratch + [dma((2 * blocks,))], flops=blocks * per_conv, name="again",
     )
     moving = ends_adj + exchange(adj_error, near).reshape(rows, channels)
     other_moving = lax.ppermute(moving, "dp", partner)

time: 139 us -> 145 us (1.043)
  blocking collectives: 22.1 us -> 30.8 us
  waiting for transfers between devices: 31.5 us -> 28 us
  starting transfers between devices: 48.1 us -> 49.7 us
    all_to_all x2 -> x3, blocking collectives: 22.1 us -> 30.8 us  [exchange(): return lax.all_to_all(value, 'layer', 0, 0, axis_index_groups=groups)]
    ppermute x1, waiting for transfers between devices: 11.3 us -> 2.91 us  [shards(): their_total = lax.ppermute(total, 'layer', pair)]
    ppermute x1, starting transfers between devices: 8.04 us -> 16.3 us  [shards(): their_late = lax.ppermute(late, 'dp', sibling)]
    all_to_all x2 -> x1, starting transfers between devices: 9.48 us -> 5.93 us  [exchange(): return lax.all_to_all(value, 'layer', 0, 0, axis_index_groups=groups)]
    ppermute x3, waiting for transfers between devices: 1.01 us -> 3.57 us  [shards(): down_total = [lax.ppermute(pair_total, 'layer', to) for to in down]]
    ppermute x1, waiting for transfers between devices: 4.41 us -> 6.67 us  [shards(): other_moving = lax.ppermute(moving, 'dp', partner)]
    ppermute x1, starting transfers between devices: 3.44 us -> 1.48 us  [shards(): their_total = lax.ppermute(total, 'layer', pair)]
    ppermute x1, starting transfers between devices: 2.1 us -> 0.18 us  [shards(): other_moving = lax.ppermute(moving, 'dp', partner)]
  transfers between devices with their start and end apart: 16 -> 15, of which waited for: 9 -> 10; matrix products, arithmetic and copies ran while one was open for 0% -> 0% of each run, Pallas kernels for 11% -> 12%
where the time goes in v6:
time: 145 us; the launch traced here: 144 us
  starting transfers between devices  49.7 us (34%)
  Pallas kernels  34.4 us (24%)
  blocking collectives  30.8 us (21%)
  waiting for transfers between devices  28 us (19%)
    pallas_call x19, Pallas kernels, call(): pl.pallas_call(body, out_shape=tuple(outs), in_specs=list(ins) if ins els...  34.4 us
    all_to_all x3, blocking collectives, exchange(): return lax.all_to_all(value, 'layer', 0, 0, axis_index_groups=groups)  30.8 us
    ppermute x1, starting transfers between devices, shards(): their_late = lax.ppermute(late, 'dp', sibling)  16.3 us
    ppermute x1, waiting for transfers between devices, shards(): after = lax.ppermute(own, 'layer', [(i + 1, i) for i in range(layers - 1)])  8.98 us
    ppermute x1, starting transfers between devices, shards(): other_corrected = lax.ppermute(corrected, 'dp', partner)  7.09 us
    ppermute x1, waiting for transfers between devices, shards(): other_moving = lax.ppermute(moving, 'dp', partner)  6.67 us
    ppermute x3, starting transfers between devices, shards(): around_full = [lax.ppermute(pair_full, 'layer', to) for to in around]  6.08 us
    all_to_all x1, starting transfers between devices, exchange(): return lax.all_to_all(value, 'layer', 0, 0, axis_index_groups=groups)  5.93 us
  transfers between devices with their start and end apart: 15, of which 10 were waited for; matrix products, arithmetic and copies ran while one was open for 0% of the time, Pallas kernels for 12%

profile of v6, /device:TPU:1, one launch (start us, length us, event | category | flops | bytes accessed | tf_op | source)
XLA Modules:
  0.0 144.0 jit_solution(9188521211018789409)
XLA Ops:
  1.6 3.9 %collective-permute-start = (f32[128,128]{1,0:T(8,128)S(1)}, f32[128,128]{1,0:T(8,128)S(1)}, u32[]{:S(2)}, u32[]{:S(2)}) collective-permute-start(f32[128,128]{1,0:T(8,128)S(1)} %coarse.1.own), channel_id=1, source_target_pairs={{0,4},{4,8},{8,12},{12,16},{16,20},{20,24},{24,28},{28,32},{32,36}... | collective-permute-start | bytes 196616 | tf_op jit(solution)/shard_map/ppermute | solution.py:429
  7.0 2.8 %start.1 = f32[8,192,128]{2,1,0:T(8,128)} custom-call(f32[512,128]{1,0:T(8,128)S(1)} %get-tuple-element.44.images, f32[128,128]{1,0:T(8,128)S(1)} %coarse.1.own, f32[128,128]{1,0:T(8,128)S(1)} %collective-permute-done.before, bf16[4,1152,128]{2,1,0:T(8,128)(2,1)S(1)} %bitcast.20, f32[4,128]{1,0:T(4,128)S(1)} %get-tuple-element.46.biases), custom_call_target="tpu_custom_call" | custom-call | flops 603979776 | bytes 2361344 | tf_op jit(solution)/shard_map/start/pallas_call | solution.py:75
  9.8 5.9 %all-to-all-start = ((f32[8,192,128]{2,1,0:T(8,128)}), f32[8,192,128]{2,1,0:T(8,128)S(1)}, u32[]{:S(2)}, u32[]{:S(2)}) async-start(f32[8,192,128]{2,1,0:T(8,128)} %start.1), calls=%async_computation | async-start | bytes 1572864 | tf_op jit(solution)/shard_map/all_to_all | solution.py:398
  18.5 9.0 %collective-permute-done.1.after = f32[128,128]{1,0:T(8,128)S(1)} collective-permute-done((f32[128,128]{1,0:T(8,128)S(1)}, f32[128,128]{1,0:T(8,128)S(1)}, u32[]{:S(2)}, u32[]{:S(2)}) %collective-permute-start.1) | collective-permute-done | bytes 65568 | tf_op jit(solution)/shard_map/ppermute | solution.py:430
  28.6 3.2 %collective-permute-start.2 = (f32[192,128]{1,0:T(8,128)S(1)}, f32[192,128]{1,0:T(8,128)S(1)}, u32[]{:S(2)}, u32[]{:S(2)}) collective-permute-start(f32[192,128]{1,0:T(8,128)S(1)} %get-tuple-element.49.refs_1_.refs_3_), channel_id=1, source_target_pairs={{0,32},{4,36},{8,40},{12,44},{16,48},{20,52},{24,56},{28,60},{32,0... | collective-permute-start | bytes 294920 | tf_op jit(solution)/shard_map/ppermute | solution.py:450
  31.9 1.9 %collective-permute-done.2.refs_2_.theirs.refs_4_.theirs_full = f32[192,128]{1,0:T(8,128)S(1)} collective-permute-done((f32[192,128]{1,0:T(8,128)S(1)}, f32[192,128]{1,0:T(8,128)S(1)}, u32[]{:S(2)}, u32[]{:S(2)}) %collective-permute-start.2) | collective-permute-done | bytes 98336 | tf_op jit(solution)/shard_map/ppermute | solution.py:450
  34.6 5.3 %collective-permute-start.5 = (f32[192,128]{1,0:T(8,128)S(1)}, f32[192,128]{1,0:T(8,128)S(1)}, u32[]{:S(2)}, u32[]{:S(2)}) collective-permute-start(f32[192,128]{1,0:T(8,128)S(1)} %pair.1), channel_id=1, source_target_pairs={{0,192},{4,196},{8,200},{12,204},{16,208},{20,212},{24,216},{28,22... | collective-permute-start | bytes 294920 | tf_op jit(solution)/shard_map/ppermute | solution.py:455
  40.7 2.0 %products.1 = (f32[8,128,128]{2,1,0:T(8,128)}, f32[8,128,128]{2,1,0:T(8,128)}) custom-call(f32[8,192,128]{2,1,0:T(8,128)S(1)} %all-to-all-done.pieces.refs_0_.refs_1_), custom_call_target="tpu_custom_call" | custom-call | bytes 1835008 | tf_op jit(solution)/shard_map/products/pallas_call | solution.py:75
  45.7 2.9 %replay.1 = f32[8,64,128]{2,1,0:T(8,128)} custom-call(s32[2]{0:T(128)S(1)} %pad_add_fusion.refs_0_.spot, f32[192,128]{1,0:T(8,128)S(1)} %collective-permute-done.2.refs_2_.theirs.refs_4_.theirs_full, f32[192,128]{1,0:T(8,128)S(1)} %collective-permute-done.3.far1, f32[192,128]{1,0:T(8,128)S(1)} %collective-permute-done.4.far2.full2, ...), custom_call_target="tpu_custom_call" | custom-call | bytes 1441800 | tf_op jit(solution)/shard_map/replay/pallas_call | solution.py:75
  48.6 12.0 %all_to_all.20 = f32[8,64,128]{2,1,0:T(8,128)S(1)} all-to-all(f32[8,64,128]{2,1,0:T(8,128)} %replay.1), channel_id=1, replica_groups={{0,4,8,12,16,20,24,28},{32,36,40,44,48,52,56,60},{64,68,72,76,80,84,88,..., dimensions={0} | all-to-all | bytes 524288 | tf_op jit(solution)/shard_map/all_to_all | solution.py:398
  60.6 5.3 %middle.1 = (f32[512,128]{1,0:T(8,128)}, bf16[4,2,18,16,128]{4,3,2,1,0:T(8,128)(2,1)}, f32[4,512,128]{2,1,0:T(8,128)}, f32[512,128]{1,0:T(8,128)}) custom-call(f32[512,128]{1,0:T(8,128)S(1)} %bitcast_add_fusion.1.corrected, f32[512,128]{1,0:T(8,128)} %get-tuple-element.60.ends_in, f32[512,128]{1,0:T(8,128)} %get-tuple-element.61.back_in, ...), custom_call_target="tpu_custom_call" | custom-call | flops 1207959552 | bytes 5310464 | tf_op jit(solution)/shard_map/middle/pallas_call | solution.py:75
  66.0 9.4 %all_to_all.21.refs_0_ = f32[8,64,128]{2,1,0:T(8,128)S(1)} all-to-all(f32[8,64,128]{2,1,0:T(8,128)} %bitcast.22), channel_id=1, replica_groups={{0,4,8,12,16,20,24,28},{32,36,40,44,48,52,56,60},{64,68,72,76,80,84,88,..., dimensions={0} | all-to-all | bytes 524288 | tf_op jit(solution)/shard_map/all_to_all | solution.py:398
  76.5 1.5 %collective-permute-start.6 = (f32[64,128]{1,0:T(8,128)S(1)}, f32[64,128]{1,0:T(8,128)S(1)}, u32[]{:S(2)}, u32[]{:S(2)}) collective-permute-start(f32[64,128]{1,0:T(8,128)S(1)} %get-tuple-element.65.refs_1_), channel_id=1, source_target_pairs={{0,32},{4,36},{8,40},{12,44},{16,48},{20,52},{24,56},{28,60},{32,0... | collective-permute-start | bytes 98312 | tf_op jit(solution)/shard_map/ppermute | solution.py:487
  77.9 2.9 %collective-permute-done.6.refs_2_.theirs = f32[64,128]{1,0:T(8,128)S(1)} collective-permute-done((f32[64,128]{1,0:T(8,128)S(1)}, f32[64,128]{1,0:T(8,128)S(1)}, u32[]{:S(2)}, u32[]{:S(2)}) %collective-permute-start.6) | collective-permute-done | bytes 32800 | tf_op jit(solution)/shard_map/ppermute | solution.py:487
  80.9 7.1 %collective-permute-start.10 = (f32[512,128]{1,0:T(8,128)S(1)}, f32[512,128]{1,0:T(8,128)S(1)}, u32[]{:S(2)}, u32[]{:S(2)}) collective-permute-start(f32[512,128]{1,0:T(8,128)S(1)} %bitcast_add_fusion.1.corrected), channel_id=1, source_target_pairs={{0,2},{1,3},{2,0},{3,1},{4,6},{5,7},{6,4},{7,5},{8,10},{9,11},{10,... | collective-permute-start | bytes 786440 | tf_op jit(solution)/shard_map/ppermute | solution.py:489
  88.7 1.5 %collective-permute-start.9 = (f32[64,128]{1,0:T(8,128)S(1)}, f32[64,128]{1,0:T(8,128)S(1)}, u32[]{:S(2)}, u32[]{:S(2)}) collective-permute-start(f32[64,128]{1,0:T(8,128)S(1)} %back_pair.1), channel_id=1, source_target_pairs={{192,0},{196,4},{200,8},{204,12},{208,16},{212,20},{216,24},{220,2... | collective-permute-start | bytes 98312 | tf_op jit(solution)/shard_map/ppermute | solution.py:494
  92.7 2.0 %collective-permute-done.9.far3 = f32[64,128]{1,0:T(8,128)S(1)} collective-permute-done((f32[64,128]{1,0:T(8,128)S(1)}, f32[64,128]{1,0:T(8,128)S(1)}, u32[]{:S(2)}, u32[]{:S(2)}) %collective-permute-start.9) | collective-permute-done | bytes 32800 | tf_op jit(solution)/shard_map/ppermute | solution.py:494
  94.7 1.6 %collective-permute-done.8.far2 = f32[64,128]{1,0:T(8,128)S(1)} collective-permute-done((f32[64,128]{1,0:T(8,128)S(1)}, f32[64,128]{1,0:T(8,128)S(1)}, u32[]{:S(2)}, u32[]{:S(2)}) %collective-permute-start.8) | collective-permute-done | bytes 32800 | tf_op jit(solution)/shard_map/ppermute | solution.py:494
  96.3 3.1 %back_replay.1 = f32[8,64,128]{2,1,0:T(8,128)} custom-call(s32[2]{0:T(128)S(1)} %pad_add_fusion.refs_0_.spot, f32[64,128]{1,0:T(8,128)S(1)} %collective-permute-done.6.refs_2_.theirs, f32[64,128]{1,0:T(8,128)S(1)} %collective-permute-done.7.far1, f32[64,128]{1,0:T(8,128)S(1)} %collective-permute-done.8.far2, f32[64,128]{1,0:T(8,128)S(1)} %collective-permute-done.9.far3, ...), custom_call_target="tpu_custom_call" | custom-call | bytes 1474568 | tf_op jit(solution)/shard_map/back_replay/pallas_call | solution.py:75
  99.4 9.4 %all_to_all.22 = f32[8,64,128]{2,1,0:T(8,128)S(1)} all-to-all(f32[8,64,128]{2,1,0:T(8,128)} %back_replay.1), channel_id=1, replica_groups={{0,4,8,12,16,20,24,28},{32,36,40,44,48,52,56,60},{64,68,72,76,80,84,88,..., dimensions={0} | all-to-all | bytes 524288 | tf_op jit(solution)/shard_map/all_to_all | solution.py:398
  109.0 2.5 %again.1 = (bf16[4,2,18,16,128]{4,3,2,1,0:T(8,128)(2,1)}, f32[4,512,128]{2,1,0:T(8,128)}) custom-call(f32[512,128]{1,0:T(8,128)S(1)} %collective-permute-done.10.corrected, bf16[4,1152,128]{2,1,0:T(8,128)(2,1)S(1)} %bitcast.19, f32[4,128]{1,0:T(4,128)S(1)} %get-tuple-element.46.biases), custom_call_target="tpu_custom_call" | custom-call | flops 603979776 | bytes 3082240 | tf_op jit(solution)/shard_map/again/pallas_call | solution.py:75
  111.6 2.8 %final.1 = (f32[512,128]{1,0:T(8,128)}, f32[4,1160,128]{2,1,0:T(8,128)S(1)}) custom-call(f32[512,128]{1,0:T(8,128)S(1)} %bitcast_add_fusion.refs_0_, bf16[4,1152,128]{2,1,0:T(8,128)(2,1)S(1)} %copy-done.2, bf16[4,2,18,16,128]{4,3,2,1,0:T(8,128)(2,1)S(1)} %copy-done.6, f32[4,512,128]{2,1,0:T(8,128)S(1)} %copy-done.5), custom_call_target="tpu_custom_call" | custom-call | flops 1207959552 | bytes 5718016 | tf_op jit(solution)/shard_map/final/pallas_call | solution.py:75
  114.4 6.7 %collective-permute-done.11.refs_0_ = f32[512,128]{1,0:T(8,128)S(1)} collective-permute-done((f32[512,128]{1,0:T(8,128)S(1)}, f32[512,128]{1,0:T(8,128)S(1)}, u32[]{:S(2)}, u32[]{:S(2)}) %collective-permute-start.11) | collective-permute-done | bytes 262176 | tf_op jit(solution)/shard_map/ppermute | solution.py:508
  122.3 16.3 %collective-permute-start.13 = (f32[2,1160,128]{2,1,0:T(8,128)S(1)}, f32[2,1160,128]{2,1,0:T(8,128)S(1)}, u32[]{:S(2)}, u32[]{:S(2)}) collective-permute-start(f32[2,1160,128]{2,1,0:T(8,128)S(1)} %get-tuple-element.79.mine), channel_id=1, source_target_pairs={{0,1},{1,0},{2,3},{3,2},{4,5},{5,4},{6,7},{7,6},{8,9},{9,8},{10,11... | collective-permute-start | bytes 3563528 | tf_op jit(solution)/shard_map/ppermute | solution.py:519
  (49 shorter events, 22.0 us)
Async XLA Ops:
  1.6 5.4 %collective-permute-start = (f32[128,128]{1,0:T(8,128)S(1)}, f32[128,128]{1,0:T(8,128)S(1)}, u32[]{:S(2)}, u32[]{:S(2)}) collective-permute-start(f32[128,128]{1,0:T(8,128)S(1)} %coarse.1.own), channel_id=1, source_target_pairs={{0,4},{4,8},{8,12},{12,16},{16,20},{20,24},{24,28},{28,32},{32,36}... | collective-permute-start | bytes 196616 | tf_op jit(solution)/shard_map/ppermute | solution.py:429
  9.8 7.2 %copy-start = (bf16[4,3,3,128,128]{4,3,2,1,0:T(8,128)(2,1)S(1)}, bf16[4,3,3,128,128]{4,3,2,1,0:T(8,128)(2,1)}, u32[]{:S(2)}) copy-start(bf16[4,3,3,128,128]{4,3,2,1,0:T(8,128)(2,1)} %param.5) | copy-start | bytes 3538948
  9.8 17.6 %all-to-all-start = ((f32[8,192,128]{2,1,0:T(8,128)}), f32[8,192,128]{2,1,0:T(8,128)S(1)}, u32[]{:S(2)}, u32[]{:S(2)}) async-start(f32[8,192,128]{2,1,0:T(8,128)} %start.1), calls=%async_computation | async-start | bytes 1572864 | tf_op jit(solution)/shard_map/all_to_all | solution.py:398
  15.8 11.7 %collective-permute-start.1 = (f32[128,128]{1,0:T(8,128)S(1)}, f32[128,128]{1,0:T(8,128)S(1)}, u32[]{:S(2)}, u32[]{:S(2)}) collective-permute-start(f32[128,128]{1,0:T(8,128)S(1)} %coarse.1.own), channel_id=1, source_target_pairs={{4,0},{8,4},{12,8},{16,12},{20,16},{24,20},{28,24},{32,28},{36,32}... | collective-permute-start | bytes 196616 | tf_op jit(solution)/shard_map/ppermute | solution.py:430
  28.6 5.3 %collective-permute-start.2 = (f32[192,128]{1,0:T(8,128)S(1)}, f32[192,128]{1,0:T(8,128)S(1)}, u32[]{:S(2)}, u32[]{:S(2)}) collective-permute-start(f32[192,128]{1,0:T(8,128)S(1)} %get-tuple-element.49.refs_1_.refs_3_), channel_id=1, source_target_pairs={{0,32},{4,36},{8,40},{12,44},{16,48},{20,52},{24,56},{28,60},{32,0... | collective-permute-start | bytes 294920 | tf_op jit(solution)/shard_map/ppermute | solution.py:450
  34.6 9.3 %collective-permute-start.5 = (f32[192,128]{1,0:T(8,128)S(1)}, f32[192,128]{1,0:T(8,128)S(1)}, u32[]{:S(2)}, u32[]{:S(2)}) collective-permute-start(f32[192,128]{1,0:T(8,128)S(1)} %pair.1), channel_id=1, source_target_pairs={{0,192},{4,196},{8,200},{12,204},{16,208},{20,212},{24,216},{28,22... | collective-permute-start | bytes 294920 | tf_op jit(solution)/shard_map/ppermute | solution.py:455
  39.9 5.1 %collective-permute-start.4 = (f32[192,128]{1,0:T(8,128)S(1)}, f32[192,128]{1,0:T(8,128)S(1)}, u32[]{:S(2)}, u32[]{:S(2)}) collective-permute-start(f32[192,128]{1,0:T(8,128)S(1)} %pair.1), channel_id=1, source_target_pairs={{0,128},{4,132},{8,136},{12,140},{16,144},{20,148},{24,152},{28,15... | collective-permute-start | bytes 294920 | tf_op jit(solution)/shard_map/ppermute | solution.py:455
  40.0 5.7 %collective-permute-start.3 = (f32[192,128]{1,0:T(8,128)S(1)}, f32[192,128]{1,0:T(8,128)S(1)}, u32[]{:S(2)}, u32[]{:S(2)}) collective-permute-start(f32[192,128]{1,0:T(8,128)S(1)} %pair.1), channel_id=1, source_target_pairs={{0,64},{4,68},{8,72},{12,76},{16,80},{20,84},{24,88},{28,92},{32,9... | collective-permute-start | bytes 294920 | tf_op jit(solution)/shard_map/ppermute | solution.py:455
  43.9 16.7 %copy-start.8 = (f32[512,128]{1,0:T(8,128)S(1)}, f32[512,128]{1,0:T(8,128)}, u32[]{:S(2)}) copy-start(f32[512,128]{1,0:T(8,128)} %get-tuple-element.58) | copy-start | bytes 786436
  76.4 32.4 %copy-start.7 = (f32[512,128]{1,0:T(8,128)S(1)}, f32[512,128]{1,0:T(8,128)}, u32[]{:S(2)}) copy-start(f32[512,128]{1,0:T(8,128)} %get-tuple-element.60.ends_in) | copy-start | bytes 786436
  76.5 4.4 %collective-permute-start.6 = (f32[64,128]{1,0:T(8,128)S(1)}, f32[64,128]{1,0:T(8,128)S(1)}, u32[]{:S(2)}, u32[]{:S(2)}) collective-permute-start(f32[64,128]{1,0:T(8,128)S(1)} %get-tuple-element.65.refs_1_), channel_id=1, source_target_pairs={{0,32},{4,36},{8,40},{12,44},{16,48},{20,52},{24,56},{28,60},{32,0... | collective-permute-start | bytes 98312 | tf_op jit(solution)/shard_map/ppermute | solution.py:487
  80.9 18.5 %collective-permute-start.10 = (f32[512,128]{1,0:T(8,128)S(1)}, f32[512,128]{1,0:T(8,128)S(1)}, u32[]{:S(2)}, u32[]{:S(2)}) collective-permute-start(f32[512,128]{1,0:T(8,128)S(1)} %bitcast_add_fusion.1.corrected), channel_id=1, source_target_pairs={{0,2},{1,3},{2,0},{3,1},{4,6},{5,7},{6,4},{7,5},{8,10},{9,11},{10,... | collective-permute-start | bytes 786440 | tf_op jit(solution)/shard_map/ppermute | solution.py:489
  88.7 6.0 %collective-permute-start.9 = (f32[64,128]{1,0:T(8,128)S(1)}, f32[64,128]{1,0:T(8,128)S(1)}, u32[]{:S(2)}, u32[]{:S(2)}) collective-permute-start(f32[64,128]{1,0:T(8,128)S(1)} %back_pair.1), channel_id=1, source_target_pairs={{192,0},{196,4},{200,8},{204,12},{208,16},{212,20},{216,24},{220,2... | collective-permute-start | bytes 98312 | tf_op jit(solution)/shard_map/ppermute | solution.py:494
  90.1 6.2 %collective-permute-start.8 = (f32[64,128]{1,0:T(8,128)S(1)}, f32[64,128]{1,0:T(8,128)S(1)}, u32[]{:S(2)}, u32[]{:S(2)}) collective-permute-start(f32[64,128]{1,0:T(8,128)S(1)} %back_pair.1), channel_id=1, source_target_pairs={{128,0},{132,4},{136,8},{140,12},{144,16},{148,20},{152,24},{156,2... | collective-permute-start | bytes 98312 | tf_op jit(solution)/shard_map/ppermute | solution.py:494
  91.4 4.9 %collective-permute-start.7 = (f32[64,128]{1,0:T(8,128)S(1)}, f32[64,128]{1,0:T(8,128)S(1)}, u32[]{:S(2)}, u32[]{:S(2)}) collective-permute-start(f32[64,128]{1,0:T(8,128)S(1)} %back_pair.1), channel_id=1, source_target_pairs={{64,0},{68,4},{72,8},{76,12},{80,16},{84,20},{88,24},{92,28},{96,3... | collective-permute-start | bytes 98312 | tf_op jit(solution)/shard_map/ppermute | solution.py:494
  96.3 12.7 %copy-start.1 = (bf16[4,3,3,128,128]{4,3,2,1,0:T(8,128)(2,1)S(1)}, bf16[4,3,3,128,128]{4,3,2,1,0:T(8,128)(2,1)}, u32[]{:S(2)}) copy-start(bf16[4,3,3,128,128]{4,3,2,1,0:T(8,128)(2,1)} %param.5) | copy-start | bytes 3538948
  108.8 2.7 %copy-start.6 = (bf16[4,2,18,16,128]{4,3,2,1,0:T(8,128)(2,1)S(1)}, bf16[4,2,18,16,128]{4,3,2,1,0:T(8,128)(2,1)}, u32[]{:S(2)}) copy-start(bf16[4,2,18,16,128]{4,3,2,1,0:T(8,128)(2,1)} %get-tuple-element.71.refs_2_) | copy-start | bytes 1769476
  108.8 2.7 %copy-start.2 = (bf16[4,1152,128]{2,1,0:T(8,128)(2,1)S(1)}, bf16[4,1152,128]{2,1,0:T(8,128)(2,1)}, u32[]{:S(2)}) copy-start(bf16[4,1152,128]{2,1,0:T(8,128)(2,1)} %flip.1.transposed_in.refs_1_.a) | copy-start | bytes 3538948
  108.8 2.7 %copy-start.5 = (f32[4,512,128]{2,1,0:T(8,128)S(1)}, f32[4,512,128]{2,1,0:T(8,128)}, u32[]{:S(2)}) copy-start(f32[4,512,128]{2,1,0:T(8,128)} %get-tuple-element.72.refs_3_) | copy-start | bytes 3145732
  108.9 12.2 %collective-permute-start.11 = (f32[512,128]{1,0:T(8,128)S(1)}, f32[512,128]{1,0:T(8,128)S(1)}, u32[]{:S(2)}, u32[]{:S(2)}) collective-permute-start(f32[512,128]{1,0:T(8,128)S(1)} %bitcast_add_fusion.refs_0_), channel_id=1, source_target_pairs={{0,2},{1,3},{2,0},{3,1},{4,6},{5,7},{6,4},{7,5},{8,10},{9,11},{10,... | collective-permute-start | bytes 786440 | tf_op jit(solution)/shard_map/ppermute | solution.py:508
  111.6 9.5 %copy-start.3 = (f32[4,512,128]{2,1,0:T(8,128)S(1)}, f32[4,512,128]{2,1,0:T(8,128)}, u32[]{:S(2)}) copy-start(f32[4,512,128]{2,1,0:T(8,128)} %get-tuple-element.76.refs_3_.c) | copy-start | bytes 3145732
  111.6 9.5 %copy-start.4 = (bf16[4,2,18,16,128]{4,3,2,1,0:T(8,128)(2,1)S(1)}, bf16[4,2,18,16,128]{4,3,2,1,0:T(8,128)(2,1)}, u32[]{:S(2)}) copy-start(bf16[4,2,18,16,128]{4,3,2,1,0:T(8,128)(2,1)} %get-tuple-element.75.refs_2_.b) | copy-start | bytes 1769476
  122.3 18.7 %collective-permute-start.13 = (f32[2,1160,128]{2,1,0:T(8,128)S(1)}, f32[2,1160,128]{2,1,0:T(8,128)S(1)}, u32[]{:S(2)}, u32[]{:S(2)}) collective-permute-start(f32[2,1160,128]{2,1,0:T(8,128)S(1)} %get-tuple-element.79.mine), channel_id=1, source_target_pairs={{0,1},{1,0},{2,3},{3,2},{4,5},{5,4},{6,7},{7,6},{8,9},{9,8},{10,11... | collective-permute-start | bytes 3563528 | tf_op jit(solution)/shard_map/ppermute | solution.py:519
  139.5 3.3 %collective-permute-start.12 = (f32[2,1160,128]{2,1,0:T(8,128)S(1)}, f32[2,1160,128]{2,1,0:T(8,128)S(1)}, u32[]{:S(2)}, u32[]{:S(2)}) collective-permute-start(f32[2,1160,128]{2,1,0:T(8,128)S(1)} %other_early.1.mine), channel_id=1, source_target_pairs={{0,1},{1,0},{2,3},{3,2},{4,5},{5,4},{6,7},{7,6},{8,9},{9,8},{10,11... | collective-permute-start | bytes 3563528 | tf_op jit(solution)/shard_map/ppermute | solution.py:527

commit v7 on v5

--- a/solution.py
+++ b/solution.py
@@ -482,7 +482,7 @@
     )
     pieces = exchange(adj_residual.reshape(GROUP, part, channels), near)
     total, prefixes = call(
-        lambda *refs: back_total_body(part, *refs), [piece, pieces_kept], pieces, first,
+        lambda *refs: back_total_body(part, *refs), [piece, pieces_shape], pieces, first,
         name="back_total",
     )
     their_total = lax.ppermute(total, "layer", pair)

time: 139 us -> 138 us (level)
  no operation moved by 1% of the time
where the time goes in v7:
time: 138 us; the launch traced here: 137 us
  starting transfers between devices  48.3 us (35%)
  Pallas kernels  34.4 us (25%)
  waiting for transfers between devices  31.5 us (23%)
  blocking collectives  22.1 us (16%)
    pallas_call x19, Pallas kernels, call(): pl.pallas_call(body, out_shape=tuple(outs), in_specs=list(ins) if ins els...  34.4 us
    all_to_all x2, blocking collectives, exchange(): return lax.all_to_all(value, 'layer', 0, 0, axis_index_groups=groups)  22.1 us
    ppermute x1, waiting for transfers between devices, shards(): their_total = lax.ppermute(total, 'layer', pair)  11.6 us
    all_to_all x2, starting transfers between devices, exchange(): return lax.all_to_all(value, 'layer', 0, 0, axis_index_groups=groups)  9.48 us
    ppermute x1, waiting for transfers between devices, shards(): after = lax.ppermute(own, 'layer', [(i + 1, i) for i in range(layers - 1)])  8.98 us
    ppermute x1, starting transfers between devices, shards(): their_late = lax.ppermute(late, 'dp', sibling)  7.68 us
    ppermute x1, starting transfers between devices, shards(): other_corrected = lax.ppermute(corrected, 'dp', partner)  6.41 us
    ppermute x3, starting transfers between devices, shards(): around_full = [lax.ppermute(pair_full, 'layer', to) for to in around]  6.08 us
  transfers between devices with their start and end apart: 16, of which 9 were waited for; matrix products, arithmetic and copies ran while one was open for 0% of the time, Pallas kernels for 11%

profile of v7, /device:TPU:1, one launch (start us, length us, event | category | flops | bytes accessed | tf_op | source)
XLA Modules:
  0.0 137.4 jit_solution(17707313816662104008)
XLA Ops:
  1.6 3.9 %collective-permute-start = (f32[128,128]{1,0:T(8,128)S(1)}, f32[128,128]{1,0:T(8,128)S(1)}, u32[]{:S(2)}, u32[]{:S(2)}) collective-permute-start(f32[128,128]{1,0:T(8,128)S(1)} %coarse.1.own), channel_id=1, source_target_pairs={{0,4},{4,8},{8,12},{12,16},{16,20},{20,24},{24,28},{28,32},{32,36}... | collective-permute-start | bytes 196616 | tf_op jit(solution)/shard_map/ppermute | solution.py:429
  5.5 1.4 %load.1 = (bf16[4,9,128,128]{3,2,1,0:T(8,128)(2,1)S(1)}, f32[512,128]{1,0:T(8,128)S(1)}, f32[4,128]{1,0:T(4,128)S(1)}, f32[512,128]{1,0:T(8,128)S(1)}) custom-call(bf16[4,9,128,128]{3,2,1,0:T(8,128)(2,1)} %bitcast.16, f32[512,128]{1,0:T(8,128)} %bitcast.23, f32[4,128]{1,0:T(4,128)} %biases_in.1, f32[512,128]{1,0:T(8,128)} %bitcast.24), custom_call_target="tpu_custom_call" | custom-call | bytes 3411968 | tf_op jit(solution)/shard_map/load/pallas_call | solution.py:75
  7.0 2.9 %start.1 = f32[8,192,128]{2,1,0:T(8,128)} custom-call(f32[512,128]{1,0:T(8,128)S(1)} %get-tuple-element.43.images, f32[128,128]{1,0:T(8,128)S(1)} %coarse.1.own, f32[128,128]{1,0:T(8,128)S(1)} %collective-permute-done.before, bf16[4,1152,128]{2,1,0:T(8,128)(2,1)S(1)} %bitcast.20, f32[4,128]{1,0:T(4,128)S(1)} %get-tuple-element.45.biases), custom_call_target="tpu_custom_call" | custom-call | flops 603979776 | bytes 2361344 | tf_op jit(solution)/shard_map/start/pallas_call | solution.py:75
  9.9 5.9 %all-to-all-start = ((f32[8,192,128]{2,1,0:T(8,128)}), f32[8,192,128]{2,1,0:T(8,128)S(1)}, u32[]{:S(2)}, u32[]{:S(2)}) async-start(f32[8,192,128]{2,1,0:T(8,128)} %start.1), calls=%async_computation | async-start | bytes 1572864 | tf_op jit(solution)/shard_map/all_to_all | solution.py:398
  18.5 9.0 %collective-permute-done.1.after = f32[128,128]{1,0:T(8,128)S(1)} collective-permute-done((f32[128,128]{1,0:T(8,128)S(1)}, f32[128,128]{1,0:T(8,128)S(1)}, u32[]{:S(2)}, u32[]{:S(2)}) %collective-permute-start.1) | collective-permute-done | bytes 65568 | tf_op jit(solution)/shard_map/ppermute | solution.py:430
  28.6 3.2 %collective-permute-start.2 = (f32[192,128]{1,0:T(8,128)S(1)}, f32[192,128]{1,0:T(8,128)S(1)}, u32[]{:S(2)}, u32[]{:S(2)}) collective-permute-start(f32[192,128]{1,0:T(8,128)S(1)} %get-tuple-element.48.refs_1_.refs_3_), channel_id=1, source_target_pairs={{0,32},{4,36},{8,40},{12,44},{16,48},{20,52},{24,56},{28,60},{32,0... | collective-permute-start | bytes 294920 | tf_op jit(solution)/shard_map/ppermute | solution.py:450
  31.9 1.9 %collective-permute-done.2.refs_2_.theirs.refs_4_.theirs_full = f32[192,128]{1,0:T(8,128)S(1)} collective-permute-done((f32[192,128]{1,0:T(8,128)S(1)}, f32[192,128]{1,0:T(8,128)S(1)}, u32[]{:S(2)}, u32[]{:S(2)}) %collective-permute-start.2) | collective-permute-done | bytes 98336 | tf_op jit(solution)/shard_map/ppermute | solution.py:450
  34.6 5.3 %collective-permute-start.5 = (f32[192,128]{1,0:T(8,128)S(1)}, f32[192,128]{1,0:T(8,128)S(1)}, u32[]{:S(2)}, u32[]{:S(2)}) collective-permute-start(f32[192,128]{1,0:T(8,128)S(1)} %pair.1), channel_id=1, source_target_pairs={{0,192},{4,196},{8,200},{12,204},{16,208},{20,212},{24,216},{28,22... | collective-permute-start | bytes 294920 | tf_op jit(solution)/shard_map/ppermute | solution.py:455
  40.7 1.9 %products.1 = (f32[8,128,128]{2,1,0:T(8,128)}, f32[8,128,128]{2,1,0:T(8,128)}) custom-call(f32[8,192,128]{2,1,0:T(8,128)S(1)} %all-to-all-done.pieces.refs_0_.refs_1_), custom_call_target="tpu_custom_call" | custom-call | bytes 1835008 | tf_op jit(solution)/shard_map/products/pallas_call | solution.py:75
  45.7 2.9 %replay.1 = f32[8,64,128]{2,1,0:T(8,128)} custom-call(s32[2]{0:T(128)S(1)} %pad_add_fusion.refs_0_.spot, f32[192,128]{1,0:T(8,128)S(1)} %collective-permute-done.2.refs_2_.theirs.refs_4_.theirs_full, f32[192,128]{1,0:T(8,128)S(1)} %collective-permute-done.3.far1, f32[192,128]{1,0:T(8,128)S(1)} %collective-permute-done.4.far2.full2, ...), custom_call_target="tpu_custom_call" | custom-call | bytes 1441800 | tf_op jit(solution)/shard_map/replay/pallas_call | solution.py:75
  48.6 12.0 %all_to_all.20 = f32[8,64,128]{2,1,0:T(8,128)S(1)} all-to-all(f32[8,64,128]{2,1,0:T(8,128)} %replay.1), channel_id=1, replica_groups={{0,4,8,12,16,20,24,28},{32,36,40,44,48,52,56,60},{64,68,72,76,80,84,88,..., dimensions={0} | all-to-all | bytes 524288 | tf_op jit(solution)/shard_map/all_to_all | solution.py:398
  60.7 5.3 %middle.1 = (f32[512,128]{1,0:T(8,128)}, bf16[4,2,18,16,128]{4,3,2,1,0:T(8,128)(2,1)}, f32[4,512,128]{2,1,0:T(8,128)}, f32[512,128]{1,0:T(8,128)}) custom-call(f32[512,128]{1,0:T(8,128)S(1)} %bitcast_add_fusion.1.corrected, f32[512,128]{1,0:T(8,128)} %get-tuple-element.59.ends_in, f32[512,128]{1,0:T(8,128)} %get-tuple-element.60.back_in, ...), custom_call_target="tpu_custom_call" | custom-call | flops 1207959552 | bytes 5310464 | tf_op jit(solution)/shard_map/middle/pallas_call | solution.py:75
  66.0 3.6 %all-to-all-start.2 = ((f32[8,64,128]{2,1,0:T(8,128)}), f32[8,64,128]{2,1,0:T(8,128)S(1)}, u32[]{:S(2)}, u32[]{:S(2)}) async-start(f32[8,64,128]{2,1,0:T(8,128)} %bitcast.22), calls=%async_computation.2 | async-start | bytes 524288 | tf_op jit(solution)/shard_map/all_to_all | solution.py:398
  69.6 6.4 %collective-permute-start.10 = (f32[512,128]{1,0:T(8,128)S(1)}, f32[512,128]{1,0:T(8,128)S(1)}, u32[]{:S(2)}, u32[]{:S(2)}) collective-permute-start(f32[512,128]{1,0:T(8,128)S(1)} %bitcast_add_fusion.1.corrected), channel_id=1, source_target_pairs={{0,2},{1,3},{2,0},{3,1},{4,6},{5,7},{6,4},{7,5},{8,10},{9,11},{10,... | collective-permute-start | bytes 786440 | tf_op jit(solution)/shard_map/ppermute | solution.py:471
  77.0 3.7 %collective-permute-start.6 = (f32[64,128]{1,0:T(8,128)S(1)}, f32[64,128]{1,0:T(8,128)S(1)}, u32[]{:S(2)}, u32[]{:S(2)}) collective-permute-start(f32[64,128]{1,0:T(8,128)S(1)} %get-tuple-element.64.refs_1_), channel_id=1, source_target_pairs={{0,32},{4,36},{8,40},{12,44},{16,48},{20,52},{24,56},{28,60},{32,0... | collective-permute-start | bytes 98312 | tf_op jit(solution)/shard_map/ppermute | solution.py:488
  80.7 11.6 %collective-permute-done.6.refs_2_.theirs = f32[64,128]{1,0:T(8,128)S(1)} collective-permute-done((f32[64,128]{1,0:T(8,128)S(1)}, f32[64,128]{1,0:T(8,128)S(1)}, u32[]{:S(2)}, u32[]{:S(2)}) %collective-permute-start.6) | collective-permute-done | bytes 32800 | tf_op jit(solution)/shard_map/ppermute | solution.py:488
  97.0 2.5 %again.1 = (bf16[4,2,18,16,128]{4,3,2,1,0:T(8,128)(2,1)}, f32[4,512,128]{2,1,0:T(8,128)}) custom-call(f32[512,128]{1,0:T(8,128)S(1)} %collective-permute-done.10.corrected, bf16[4,1152,128]{2,1,0:T(8,128)(2,1)S(1)} %bitcast.19, f32[4,128]{1,0:T(4,128)S(1)} %get-tuple-element.45.biases), custom_call_target="tpu_custom_call" | custom-call | flops 603979776 | bytes 3082240 | tf_op jit(solution)/shard_map/again/pallas_call | solution.py:75
  100.6 3.1 %back_replay.1 = f32[8,64,128]{2,1,0:T(8,128)} custom-call(s32[2]{0:T(128)S(1)} %pad_add_fusion.refs_0_.spot, f32[64,128]{1,0:T(8,128)S(1)} %collective-permute-done.6.refs_2_.theirs, f32[64,128]{1,0:T(8,128)S(1)} %collective-permute-done.7.far1, f32[64,128]{1,0:T(8,128)S(1)} %collective-permute-done.8.far2, f32[64,128]{1,0:T(8,128)S(1)} %collective-permute-done.9.far3, ...), custom_call_target="tpu_custom_call" | custom-call | bytes 1474568 | tf_op jit(solution)/shard_map/back_replay/pallas_call | solution.py:75
  103.6 10.1 %all_to_all.21 = f32[8,64,128]{2,1,0:T(8,128)S(1)} all-to-all(f32[8,64,128]{2,1,0:T(8,128)} %back_replay.1), channel_id=1, replica_groups={{0,4,8,12,16,20,24,28},{32,36,40,44,48,52,56,60},{64,68,72,76,80,84,88,..., dimensions={0} | all-to-all | bytes 524288 | tf_op jit(solution)/shard_map/all_to_all | solution.py:398
  113.7 2.5 %collective-permute-start.11 = (f32[512,128]{1,0:T(8,128)S(1)}, f32[512,128]{1,0:T(8,128)S(1)}, u32[]{:S(2)}, u32[]{:S(2)}) collective-permute-start(f32[512,128]{1,0:T(8,128)S(1)} %bitcast_add_fusion.refs_0_), channel_id=1, source_target_pairs={{0,2},{1,3},{2,0},{3,1},{4,6},{5,7},{6,4},{7,5},{8,10},{9,11},{10,... | collective-permute-start | bytes 786440 | tf_op jit(solution)/shard_map/ppermute | solution.py:509
  116.2 2.8 %final.1 = (f32[512,128]{1,0:T(8,128)}, f32[4,1160,128]{2,1,0:T(8,128)S(1)}) custom-call(f32[512,128]{1,0:T(8,128)S(1)} %bitcast_add_fusion.refs_0_, bf16[4,1152,128]{2,1,0:T(8,128)(2,1)S(1)} %copy-done.2, bf16[4,2,18,16,128]{4,3,2,1,0:T(8,128)(2,1)S(1)} %copy-done.6, f32[4,512,128]{2,1,0:T(8,128)S(1)} %copy-done.5), custom_call_target="tpu_custom_call" | custom-call | flops 1207959552 | bytes 5718016 | tf_op jit(solution)/shard_map/final/pallas_call | solution.py:75
  119.0 4.1 %collective-permute-done.11.refs_0_ = f32[512,128]{1,0:T(8,128)S(1)} collective-permute-done((f32[512,128]{1,0:T(8,128)S(1)}, f32[512,128]{1,0:T(8,128)S(1)}, u32[]{:S(2)}, u32[]{:S(2)}) %collective-permute-start.11) | collective-permute-done | bytes 262176 | tf_op jit(solution)/shard_map/ppermute | solution.py:509
  124.3 7.7 %collective-permute-start.13 = (f32[2,1160,128]{2,1,0:T(8,128)S(1)}, f32[2,1160,128]{2,1,0:T(8,128)S(1)}, u32[]{:S(2)}, u32[]{:S(2)}) collective-permute-start(f32[2,1160,128]{2,1,0:T(8,128)S(1)} %get-tuple-element.77.mine), channel_id=1, source_target_pairs={{0,1},{1,0},{2,3},{3,2},{4,5},{5,4},{6,7},{7,6},{8,9},{9,8},{10,11... | collective-permute-start | bytes 3563528 | tf_op jit(solution)/shard_map/ppermute | solution.py:520
  133.0 1.5 %collective-permute-done.13.theirs = f32[2,1160,128]{2,1,0:T(8,128)S(1)} collective-permute-done((f32[2,1160,128]{2,1,0:T(8,128)S(1)}, f32[2,1160,128]{2,1,0:T(8,128)S(1)}, u32[]{:S(2)}, u32[]{:S(2)}) %collective-permute-start.13) | collective-permute-done | bytes 1187872 | tf_op jit(solution)/shard_map/ppermute | solution.py:520
  (50 shorter events, 21.2 us)
Async XLA Ops:
  1.6 5.4 %collective-permute-start = (f32[128,128]{1,0:T(8,128)S(1)}, f32[128,128]{1,0:T(8,128)S(1)}, u32[]{:S(2)}, u32[]{:S(2)}) collective-permute-start(f32[128,128]{1,0:T(8,128)S(1)} %coarse.1.own), channel_id=1, source_target_pairs={{0,4},{4,8},{8,12},{12,16},{16,20},{20,24},{24,28},{28,32},{32,36}... | collective-permute-start | bytes 196616 | tf_op jit(solution)/shard_map/ppermute | solution.py:429
  9.9 7.2 %copy-start = (bf16[4,3,3,128,128]{4,3,2,1,0:T(8,128)(2,1)S(1)}, bf16[4,3,3,128,128]{4,3,2,1,0:T(8,128)(2,1)}, u32[]{:S(2)}) copy-start(bf16[4,3,3,128,128]{4,3,2,1,0:T(8,128)(2,1)} %param.5) | copy-start | bytes 3538948
  9.9 17.6 %all-to-all-start = ((f32[8,192,128]{2,1,0:T(8,128)}), f32[8,192,128]{2,1,0:T(8,128)S(1)}, u32[]{:S(2)}, u32[]{:S(2)}) async-start(f32[8,192,128]{2,1,0:T(8,128)} %start.1), calls=%async_computation | async-start | bytes 1572864 | tf_op jit(solution)/shard_map/all_to_all | solution.py:398
  15.8 11.7 %collective-permute-start.1 = (f32[128,128]{1,0:T(8,128)S(1)}, f32[128,128]{1,0:T(8,128)S(1)}, u32[]{:S(2)}, u32[]{:S(2)}) collective-permute-start(f32[128,128]{1,0:T(8,128)S(1)} %coarse.1.own), channel_id=1, source_target_pairs={{4,0},{8,4},{12,8},{16,12},{20,16},{24,20},{28,24},{32,28},{36,32}... | collective-permute-start | bytes 196616 | tf_op jit(solution)/shard_map/ppermute | solution.py:430
  28.6 5.2 %collective-permute-start.2 = (f32[192,128]{1,0:T(8,128)S(1)}, f32[192,128]{1,0:T(8,128)S(1)}, u32[]{:S(2)}, u32[]{:S(2)}) collective-permute-start(f32[192,128]{1,0:T(8,128)S(1)} %get-tuple-element.48.refs_1_.refs_3_), channel_id=1, source_target_pairs={{0,32},{4,36},{8,40},{12,44},{16,48},{20,52},{24,56},{28,60},{32,0... | collective-permute-start | bytes 294920 | tf_op jit(solution)/shard_map/ppermute | solution.py:450
  34.6 9.3 %collective-permute-start.5 = (f32[192,128]{1,0:T(8,128)S(1)}, f32[192,128]{1,0:T(8,128)S(1)}, u32[]{:S(2)}, u32[]{:S(2)}) collective-permute-start(f32[192,128]{1,0:T(8,128)S(1)} %pair.1), channel_id=1, source_target_pairs={{0,192},{4,196},{8,200},{12,204},{16,208},{20,212},{24,216},{28,22... | collective-permute-start | bytes 294920 | tf_op jit(solution)/shard_map/ppermute | solution.py:455
  40.0 5.1 %collective-permute-start.4 = (f32[192,128]{1,0:T(8,128)S(1)}, f32[192,128]{1,0:T(8,128)S(1)}, u32[]{:S(2)}, u32[]{:S(2)}) collective-permute-start(f32[192,128]{1,0:T(8,128)S(1)} %pair.1), channel_id=1, source_target_pairs={{0,128},{4,132},{8,136},{12,140},{16,144},{20,148},{24,152},{28,15... | collective-permute-start | bytes 294920 | tf_op jit(solution)/shard_map/ppermute | solution.py:455
  40.0 5.7 %collective-permute-start.3 = (f32[192,128]{1,0:T(8,128)S(1)}, f32[192,128]{1,0:T(8,128)S(1)}, u32[]{:S(2)}, u32[]{:S(2)}) collective-permute-start(f32[192,128]{1,0:T(8,128)S(1)} %pair.1), channel_id=1, source_target_pairs={{0,64},{4,68},{8,72},{12,76},{16,80},{20,84},{24,88},{28,92},{32,9... | collective-permute-start | bytes 294920 | tf_op jit(solution)/shard_map/ppermute | solution.py:455
  43.9 16.7 %copy-start.8 = (f32[512,128]{1,0:T(8,128)S(1)}, f32[512,128]{1,0:T(8,128)}, u32[]{:S(2)}) copy-start(f32[512,128]{1,0:T(8,128)} %get-tuple-element.57) | copy-start | bytes 786436
  66.0 31.0 %copy-start.1 = (bf16[4,3,3,128,128]{4,3,2,1,0:T(8,128)(2,1)S(1)}, bf16[4,3,3,128,128]{4,3,2,1,0:T(8,128)(2,1)}, u32[]{:S(2)}) copy-start(bf16[4,3,3,128,128]{4,3,2,1,0:T(8,128)(2,1)} %param.5) | copy-start | bytes 3538948
  66.0 10.0 %all-to-all-start.2 = ((f32[8,64,128]{2,1,0:T(8,128)}), f32[8,64,128]{2,1,0:T(8,128)S(1)}, u32[]{:S(2)}, u32[]{:S(2)}) async-start(f32[8,64,128]{2,1,0:T(8,128)} %bitcast.22), calls=%async_computation.2 | async-start | bytes 524288 | tf_op jit(solution)/shard_map/all_to_all | solution.py:398
  69.6 27.4 %collective-permute-start.10 = (f32[512,128]{1,0:T(8,128)S(1)}, f32[512,128]{1,0:T(8,128)S(1)}, u32[]{:S(2)}, u32[]{:S(2)}) collective-permute-start(f32[512,128]{1,0:T(8,128)S(1)} %bitcast_add_fusion.1.corrected), channel_id=1, source_target_pairs={{0,2},{1,3},{2,0},{3,1},{4,6},{5,7},{6,4},{7,5},{8,10},{9,11},{10,... | collective-permute-start | bytes 786440 | tf_op jit(solution)/shard_map/ppermute | solution.py:471
  77.0 15.3 %collective-permute-start.6 = (f32[64,128]{1,0:T(8,128)S(1)}, f32[64,128]{1,0:T(8,128)S(1)}, u32[]{:S(2)}, u32[]{:S(2)}) collective-permute-start(f32[64,128]{1,0:T(8,128)S(1)} %get-tuple-element.64.refs_1_), channel_id=1, source_target_pairs={{0,32},{4,36},{8,40},{12,44},{16,48},{20,52},{24,56},{28,60},{32,0... | collective-permute-start | bytes 98312 | tf_op jit(solution)/shard_map/ppermute | solution.py:488
  93.1 6.4 %collective-permute-start.9 = (f32[64,128]{1,0:T(8,128)S(1)}, f32[64,128]{1,0:T(8,128)S(1)}, u32[]{:S(2)}, u32[]{:S(2)}) collective-permute-start(f32[64,128]{1,0:T(8,128)S(1)} %back_pair.1), channel_id=1, source_target_pairs={{192,0},{196,4},{200,8},{204,12},{208,16},{212,20},{216,24},{220,2... | collective-permute-start | bytes 98312 | tf_op jit(solution)/shard_map/ppermute | solution.py:493
  94.4 6.2 %collective-permute-start.8 = (f32[64,128]{1,0:T(8,128)S(1)}, f32[64,128]{1,0:T(8,128)S(1)}, u32[]{:S(2)}, u32[]{:S(2)}) collective-permute-start(f32[64,128]{1,0:T(8,128)S(1)} %back_pair.1), channel_id=1, source_target_pairs={{128,0},{132,4},{136,8},{140,12},{144,16},{148,20},{152,24},{156,2... | collective-permute-start | bytes 98312 | tf_op jit(solution)/shard_map/ppermute | solution.py:493
  95.7 4.9 %collective-permute-start.7 = (f32[64,128]{1,0:T(8,128)S(1)}, f32[64,128]{1,0:T(8,128)S(1)}, u32[]{:S(2)}, u32[]{:S(2)}) collective-permute-start(f32[64,128]{1,0:T(8,128)S(1)} %back_pair.1), channel_id=1, source_target_pairs={{64,0},{68,4},{72,8},{76,12},{80,16},{84,20},{88,24},{92,28},{96,3... | collective-permute-start | bytes 98312 | tf_op jit(solution)/shard_map/ppermute | solution.py:493
  97.0 19.2 %copy-start.6 = (bf16[4,2,18,16,128]{4,3,2,1,0:T(8,128)(2,1)S(1)}, bf16[4,2,18,16,128]{4,3,2,1,0:T(8,128)(2,1)}, u32[]{:S(2)}) copy-start(bf16[4,2,18,16,128]{4,3,2,1,0:T(8,128)(2,1)} %get-tuple-element.70.refs_2_) | copy-start | bytes 1769476
  99.5 14.2 %copy-start.7 = (f32[512,128]{1,0:T(8,128)S(1)}, f32[512,128]{1,0:T(8,128)}, u32[]{:S(2)}) copy-start(f32[512,128]{1,0:T(8,128)} %get-tuple-element.59.ends_in) | copy-start | bytes 786436
  100.6 15.6 %copy-start.2 = (bf16[4,1152,128]{2,1,0:T(8,128)(2,1)S(1)}, bf16[4,1152,128]{2,1,0:T(8,128)(2,1)}, u32[]{:S(2)}) copy-start(bf16[4,1152,128]{2,1,0:T(8,128)(2,1)} %flip.1.transposed_in.refs_1_.a) | copy-start | bytes 3538948
  100.6 15.6 %copy-start.5 = (f32[4,512,128]{2,1,0:T(8,128)S(1)}, f32[4,512,128]{2,1,0:T(8,128)}, u32[]{:S(2)}) copy-start(f32[4,512,128]{2,1,0:T(8,128)} %get-tuple-element.71.refs_3_) | copy-start | bytes 3145732
  113.7 9.3 %collective-permute-start.11 = (f32[512,128]{1,0:T(8,128)S(1)}, f32[512,128]{1,0:T(8,128)S(1)}, u32[]{:S(2)}, u32[]{:S(2)}) collective-permute-start(f32[512,128]{1,0:T(8,128)S(1)} %bitcast_add_fusion.refs_0_), channel_id=1, source_target_pairs={{0,2},{1,3},{2,0},{3,1},{4,6},{5,7},{6,4},{7,5},{8,10},{9,11},{10,... | collective-permute-start | bytes 786440 | tf_op jit(solution)/shard_map/ppermute | solution.py:509
  116.2 6.9 %copy-start.3 = (f32[4,512,128]{2,1,0:T(8,128)S(1)}, f32[4,512,128]{2,1,0:T(8,128)}, u32[]{:S(2)}) copy-start(f32[4,512,128]{2,1,0:T(8,128)} %get-tuple-element.74.refs_3_.c) | copy-start | bytes 3145732
  124.3 10.2 %collective-permute-start.13 = (f32[2,1160,128]{2,1,0:T(8,128)S(1)}, f32[2,1160,128]{2,1,0:T(8,128)S(1)}, u32[]{:S(2)}, u32[]{:S(2)}) collective-permute-start(f32[2,1160,128]{2,1,0:T(8,128)S(1)} %get-tuple-element.77.mine), channel_id=1, source_target_pairs={{0,1},{1,0},{2,3},{3,2},{4,5},{5,4},{6,7},{7,6},{8,9},{9,8},{10,11... | collective-permute-start | bytes 3563528 | tf_op jit(solution)/shard_map/ppermute | solution.py:520
  132.9 3.3 %collective-permute-start.12 = (f32[2,1160,128]{2,1,0:T(8,128)S(1)}, f32[2,1160,128]{2,1,0:T(8,128)S(1)}, u32[]{:S(2)}, u32[]{:S(2)}) collective-permute-start(f32[2,1160,128]{2,1,0:T(8,128)S(1)} %other_early.1.mine), channel_id=1, source_target_pairs={{0,1},{1,0},{2,3},{3,2},{4,5},{5,4},{6,7},{7,6},{8,9},{9,8},{10,11... | collective-permute-start | bytes 3563528 | tf_op jit(solution)/shard_map/ppermute | solution.py:528
  (1 other events, 6.9 us)

commit v8 on v7

--- a/solution.py
+++ b/solution.py
@@ -248,9 +248,10 @@
 
 def forward_sweep(state, weights, biases, ref, inputs, slopes, stores, fetches=None):
     for index in range(weights.shape[0]):
-        if fetches is not None:
-            fetches[index].wait()
-        activation = jnp.tanh(convolve(ref, state, weights.at[index]) + biases[index : index + 1])
+        preact = convolve(ref, state, weights.at[index])
+        if fetches is not None and index == 0:
+            fetches[0].wait()
+        activation = jnp.tanh(preact + biases[index : index + 1])
         channels = state.shape[1]
         inputs[index] = ref[:, :, :, channels : 2 * channels]
         slopes[index] = 0.25 * (1.0 - activation * activation)
@@ -272,24 +273,22 @@
 
 
 def middle_body(
-    corrected, ends_in, back_in, weights_in, transposed_in, biases_in,
+    corrected, weights, ends_in, back_in, transposed_in, biases_in,
     ends_out, inputs_out, slopes_out, residual_out,
-    ref, ends, inputs, slopes, ends_adj, back, weights, transposed, biases, sems, loads,
+    ref, ends, inputs, slopes, ends_adj, back, transposed, biases, sems, loads,
 ):
     blocks = weights.shape[0]
     pairs = [(biases_in, biases)]
-    pairs += [(weights_in.at[index], weights.at[index]) for index in range(blocks)]
     pairs += [(transposed_in, transposed), (ends_in, ends_adj), (back_in, back)]
     fetches = [pltpu.make_async_copy(a, b, loads.at[at]) for at, (a, b) in enumerate(pairs)]
     for fetch in fetches:
         fetch.start()
     clear_border(ref)
     stores = sweep_stores(inputs, slopes, inputs_out, slopes_out, sems)
-    fetches[0].wait()
     ends[...] = forward_sweep(
-        corrected[...], weights, biases, ref, inputs, slopes, stores, fetches[1 : 1 + blocks]
-    )
-    for fetch in fetches[1 + blocks :]:
+        corrected[...], weights, biases, ref, inputs, slopes, stores, fetches[:1]
+    )
+    for fetch in fetches[1:]:
         fetch.wait()
     last = pltpu.make_async_copy(ends, ends_out, sems.at[2 * blocks])
     last.start()
@@ -472,12 +471,12 @@
 
     interval_ends, inputs, slopes, adj_residual = call(
         middle_body, [result, stored(inputs_dims, bf16), stored(slopes_dims), kept],
-        corrected, in_hbm(ends_adj), in_hbm(back), in_hbm(kernels),
+        corrected, kernels, in_hbm(ends_adj), in_hbm(back),
         in_hbm(transposed), in_hbm(biases),
-        ins=[VMEM] + [HBM] * 5, out_specs=[HBM, HBM, HBM, VMEM],
+        ins=[VMEM] * 2 + [HBM] * 4, out_specs=[HBM, HBM, HBM, VMEM],
         scratch=[ref, pltpu.VMEM((rows, channels), f32)] + sweep_scratch
-        + [pltpu.VMEM((rows, channels), f32)] * 2 + [pltpu.VMEM(sweep_shape, bf16)] * 2
-        + [pltpu.VMEM((blocks, channels), f32), dma((2 * blocks + 1,)), dma((blocks + 4,))],
+        + [pltpu.VMEM((rows, channels), f32)] * 2 + [pltpu.VMEM(sweep_shape, bf16)]
+        + [pltpu.VMEM((blocks, channels), f32), dma((2 * blocks + 1,)), dma((4,))],
         flops=2 * blocks * per_conv, name="middle",
     )
     pieces = exchange(adj_residual.reshape(GROUP, part, channels), near)

time: 138 us -> 137 us (level)
  no operation moved by 1% of the time
where the time goes in v8:
time: 137 us; the launch traced here: 136 us
  starting transfers between devices  48.2 us (35%)
  Pallas kernels  33.5 us (24%)
  waiting for transfers between devices  31.5 us (23%)
  blocking collectives  22.1 us (16%)
    pallas_call x19, Pallas kernels, call(): pl.pallas_call(body, out_shape=tuple(outs), in_specs=list(ins) if ins els...  33.5 us
    all_to_all x2, blocking collectives, exchange(): return lax.all_to_all(value, 'layer', 0, 0, axis_index_groups=groups)  22.1 us
    ppermute x1, waiting for transfers between devices, shards(): their_total = lax.ppermute(total, 'layer', pair)  11.8 us
    all_to_all x2, starting transfers between devices, exchange(): return lax.all_to_all(value, 'layer', 0, 0, axis_index_groups=groups)  9.35 us
    ppermute x1, waiting for transfers between devices, shards(): after = lax.ppermute(own, 'layer', [(i + 1, i) for i in range(layers - 1)])  8.98 us
    ppermute x1, starting transfers between devices, shards(): their_late = lax.ppermute(late, 'dp', sibling)  7.7 us
    ppermute x1, starting transfers between devices, shards(): other_corrected = lax.ppermute(corrected, 'dp', partner)  6.4 us
    ppermute x3, starting transfers between devices, shards(): around_full = [lax.ppermute(pair_full, 'layer', to) for to in around]  6.08 us
  transfers between devices with their start and end apart: 16, of which 9 were waited for; matrix products, arithmetic and copies ran while one was open for 0% of the time, Pallas kernels for 11%

profile of v8, /device:TPU:1, one launch (start us, length us, event | category | flops | bytes accessed | tf_op | source)
XLA Modules:
  0.0 136.4 jit_solution(15339474699808689044)
XLA Ops:
  1.6 3.9 %collective-permute-start = (f32[128,128]{1,0:T(8,128)S(1)}, f32[128,128]{1,0:T(8,128)S(1)}, u32[]{:S(2)}, u32[]{:S(2)}) collective-permute-start(f32[128,128]{1,0:T(8,128)S(1)} %coarse.1.own), channel_id=1, source_target_pairs={{0,4},{4,8},{8,12},{12,16},{16,20},{20,24},{24,28},{28,32},{32,36}... | collective-permute-start | bytes 196616 | tf_op jit(solution)/shard_map/ppermute | solution.py:428
  7.0 2.9 %start.1 = f32[8,192,128]{2,1,0:T(8,128)} custom-call(f32[512,128]{1,0:T(8,128)S(1)} %get-tuple-element.43.images, f32[128,128]{1,0:T(8,128)S(1)} %coarse.1.own, f32[128,128]{1,0:T(8,128)S(1)} %collective-permute-done.before, bf16[4,1152,128]{2,1,0:T(8,128)(2,1)S(1)} %bitcast.20, f32[4,128]{1,0:T(4,128)S(1)} %get-tuple-element.45.biases), custom_call_target="tpu_custom_call" | custom-call | flops 603979776 | bytes 2361344 | tf_op jit(solution)/shard_map/start/pallas_call | solution.py:75
  9.9 5.9 %all-to-all-start = ((f32[8,192,128]{2,1,0:T(8,128)}), f32[8,192,128]{2,1,0:T(8,128)S(1)}, u32[]{:S(2)}, u32[]{:S(2)}) async-start(f32[8,192,128]{2,1,0:T(8,128)} %start.1), calls=%async_computation | async-start | bytes 1572864 | tf_op jit(solution)/shard_map/all_to_all | solution.py:397
  18.5 9.0 %collective-permute-done.1.after = f32[128,128]{1,0:T(8,128)S(1)} collective-permute-done((f32[128,128]{1,0:T(8,128)S(1)}, f32[128,128]{1,0:T(8,128)S(1)}, u32[]{:S(2)}, u32[]{:S(2)}) %collective-permute-start.1) | collective-permute-done | bytes 65568 | tf_op jit(solution)/shard_map/ppermute | solution.py:429
  28.6 3.2 %collective-permute-start.2 = (f32[192,128]{1,0:T(8,128)S(1)}, f32[192,128]{1,0:T(8,128)S(1)}, u32[]{:S(2)}, u32[]{:S(2)}) collective-permute-start(f32[192,128]{1,0:T(8,128)S(1)} %get-tuple-element.48.refs_1_.refs_3_), channel_id=1, source_target_pairs={{0,32},{4,36},{8,40},{12,44},{16,48},{20,52},{24,56},{28,60},{32,0... | collective-permute-start | bytes 294920 | tf_op jit(solution)/shard_map/ppermute | solution.py:449
  32.0 1.9 %collective-permute-done.2.refs_2_.theirs.refs_4_.theirs_full = f32[192,128]{1,0:T(8,128)S(1)} collective-permute-done((f32[192,128]{1,0:T(8,128)S(1)}, f32[192,128]{1,0:T(8,128)S(1)}, u32[]{:S(2)}, u32[]{:S(2)}) %collective-permute-start.2) | collective-permute-done | bytes 98336 | tf_op jit(solution)/shard_map/ppermute | solution.py:449
  34.6 5.3 %collective-permute-start.5 = (f32[192,128]{1,0:T(8,128)S(1)}, f32[192,128]{1,0:T(8,128)S(1)}, u32[]{:S(2)}, u32[]{:S(2)}) collective-permute-start(f32[192,128]{1,0:T(8,128)S(1)} %pair.1), channel_id=1, source_target_pairs={{0,192},{4,196},{8,200},{12,204},{16,208},{20,212},{24,216},{28,22... | collective-permute-start | bytes 294920 | tf_op jit(solution)/shard_map/ppermute | solution.py:454
  40.7 1.9 %products.1 = (f32[8,128,128]{2,1,0:T(8,128)}, f32[8,128,128]{2,1,0:T(8,128)}) custom-call(f32[8,192,128]{2,1,0:T(8,128)S(1)} %all-to-all-done.pieces.refs_0_.refs_1_), custom_call_target="tpu_custom_call" | custom-call | bytes 1835008 | tf_op jit(solution)/shard_map/products/pallas_call | solution.py:75
  45.7 2.9 %replay.1 = f32[8,64,128]{2,1,0:T(8,128)} custom-call(s32[2]{0:T(128)S(1)} %pad_add_fusion.refs_0_.spot, f32[192,128]{1,0:T(8,128)S(1)} %collective-permute-done.2.refs_2_.theirs.refs_4_.theirs_full, f32[192,128]{1,0:T(8,128)S(1)} %collective-permute-done.3.far1, f32[192,128]{1,0:T(8,128)S(1)} %collective-permute-done.4.far2.full2, ...), custom_call_target="tpu_custom_call" | custom-call | bytes 1441800 | tf_op jit(solution)/shard_map/replay/pallas_call | solution.py:75
  48.6 12.0 %all_to_all.20 = f32[8,64,128]{2,1,0:T(8,128)S(1)} all-to-all(f32[8,64,128]{2,1,0:T(8,128)} %replay.1), channel_id=1, replica_groups={{0,4,8,12,16,20,24,28},{32,36,40,44,48,52,56,60},{64,68,72,76,80,84,88,..., dimensions={0} | all-to-all | bytes 524288 | tf_op jit(solution)/shard_map/all_to_all | solution.py:397
  60.7 4.4 %middle.1 = (f32[512,128]{1,0:T(8,128)}, bf16[4,2,18,16,128]{4,3,2,1,0:T(8,128)(2,1)}, f32[4,512,128]{2,1,0:T(8,128)}, f32[512,128]{1,0:T(8,128)}) custom-call(f32[512,128]{1,0:T(8,128)S(1)} %bitcast_add_fusion.1.corrected, bf16[4,1152,128]{2,1,0:T(8,128)(2,1)S(1)} %bitcast.18, f32[512,128]{1,0:T(8,128)} %get-tuple-element.59.ends_in, ...), custom_call_target="tpu_custom_call" | custom-call | flops 1207959552 | bytes 5310464 | tf_op jit(solution)/shard_map/middle/pallas_call | solution.py:75
  65.1 3.4 %all-to-all-start.2 = ((f32[8,64,128]{2,1,0:T(8,128)}), f32[8,64,128]{2,1,0:T(8,128)S(1)}, u32[]{:S(2)}, u32[]{:S(2)}) async-start(f32[8,64,128]{2,1,0:T(8,128)} %bitcast.22), calls=%async_computation.2 | async-start | bytes 524288 | tf_op jit(solution)/shard_map/all_to_all | solution.py:397
  68.6 6.4 %collective-permute-start.10 = (f32[512,128]{1,0:T(8,128)S(1)}, f32[512,128]{1,0:T(8,128)S(1)}, u32[]{:S(2)}, u32[]{:S(2)}) collective-permute-start(f32[512,128]{1,0:T(8,128)S(1)} %bitcast_add_fusion.1.corrected), channel_id=1, source_target_pairs={{0,2},{1,3},{2,0},{3,1},{4,6},{5,7},{6,4},{7,5},{8,10},{9,11},{10,... | collective-permute-start | bytes 786440 | tf_op jit(solution)/shard_map/ppermute | solution.py:470
  76.0 3.5 %collective-permute-start.6 = (f32[64,128]{1,0:T(8,128)S(1)}, f32[64,128]{1,0:T(8,128)S(1)}, u32[]{:S(2)}, u32[]{:S(2)}) collective-permute-start(f32[64,128]{1,0:T(8,128)S(1)} %get-tuple-element.64.refs_1_), channel_id=1, source_target_pairs={{0,32},{4,36},{8,40},{12,44},{16,48},{20,52},{24,56},{28,60},{32,0... | collective-permute-start | bytes 98312 | tf_op jit(solution)/shard_map/ppermute | solution.py:487
  79.5 11.8 %collective-permute-done.6.refs_2_.theirs = f32[64,128]{1,0:T(8,128)S(1)} collective-permute-done((f32[64,128]{1,0:T(8,128)S(1)}, f32[64,128]{1,0:T(8,128)S(1)}, u32[]{:S(2)}, u32[]{:S(2)}) %collective-permute-start.6) | collective-permute-done | bytes 32800 | tf_op jit(solution)/shard_map/ppermute | solution.py:487
  94.7 1.5 %collective-permute-start.7 = (f32[64,128]{1,0:T(8,128)S(1)}, f32[64,128]{1,0:T(8,128)S(1)}, u32[]{:S(2)}, u32[]{:S(2)}) collective-permute-start(f32[64,128]{1,0:T(8,128)S(1)} %back_pair.1), channel_id=1, source_target_pairs={{64,0},{68,4},{72,8},{76,12},{80,16},{84,20},{88,24},{92,28},{96,3... | collective-permute-start | bytes 98312 | tf_op jit(solution)/shard_map/ppermute | solution.py:492
  96.2 2.5 %again.1 = (bf16[4,2,18,16,128]{4,3,2,1,0:T(8,128)(2,1)}, f32[4,512,128]{2,1,0:T(8,128)}) custom-call(f32[512,128]{1,0:T(8,128)S(1)} %collective-permute-done.10.corrected, bf16[4,1152,128]{2,1,0:T(8,128)(2,1)S(1)} %bitcast.19, f32[4,128]{1,0:T(4,128)S(1)} %get-tuple-element.45.biases), custom_call_target="tpu_custom_call" | custom-call | flops 603979776 | bytes 3082240 | tf_op jit(solution)/shard_map/again/pallas_call | solution.py:75
  99.6 3.1 %back_replay.1 = f32[8,64,128]{2,1,0:T(8,128)} custom-call(s32[2]{0:T(128)S(1)} %pad_add_fusion.refs_0_.spot, f32[64,128]{1,0:T(8,128)S(1)} %collective-permute-done.6.refs_2_.theirs, f32[64,128]{1,0:T(8,128)S(1)} %collective-permute-done.7.far1, f32[64,128]{1,0:T(8,128)S(1)} %collective-permute-done.8.far2, f32[64,128]{1,0:T(8,128)S(1)} %collective-permute-done.9.far3, ...), custom_call_target="tpu_custom_call" | custom-call | bytes 1474568 | tf_op jit(solution)/shard_map/back_replay/pallas_call | solution.py:75
  102.6 10.1 %all_to_all.21 = f32[8,64,128]{2,1,0:T(8,128)S(1)} all-to-all(f32[8,64,128]{2,1,0:T(8,128)} %back_replay.1), channel_id=1, replica_groups={{0,4,8,12,16,20,24,28},{32,36,40,44,48,52,56,60},{64,68,72,76,80,84,88,..., dimensions={0} | all-to-all | bytes 524288 | tf_op jit(solution)/shard_map/all_to_all | solution.py:397
  112.7 2.5 %collective-permute-start.11 = (f32[512,128]{1,0:T(8,128)S(1)}, f32[512,128]{1,0:T(8,128)S(1)}, u32[]{:S(2)}, u32[]{:S(2)}) collective-permute-start(f32[512,128]{1,0:T(8,128)S(1)} %bitcast_add_fusion.refs_0_), channel_id=1, source_target_pairs={{0,2},{1,3},{2,0},{3,1},{4,6},{5,7},{6,4},{7,5},{8,10},{9,11},{10,... | collective-permute-start | bytes 786440 | tf_op jit(solution)/shard_map/ppermute | solution.py:508
  115.2 2.8 %final.1 = (f32[512,128]{1,0:T(8,128)}, f32[4,1160,128]{2,1,0:T(8,128)S(1)}) custom-call(f32[512,128]{1,0:T(8,128)S(1)} %bitcast_add_fusion.refs_0_, bf16[4,1152,128]{2,1,0:T(8,128)(2,1)S(1)} %copy-done.1, bf16[4,2,18,16,128]{4,3,2,1,0:T(8,128)(2,1)S(1)} %copy-done.5, f32[4,512,128]{2,1,0:T(8,128)S(1)} %copy-done.4), custom_call_target="tpu_custom_call" | custom-call | flops 1207959552 | bytes 5718016 | tf_op jit(solution)/shard_map/final/pallas_call | solution.py:75
  118.0 4.0 %collective-permute-done.11.refs_0_ = f32[512,128]{1,0:T(8,128)S(1)} collective-permute-done((f32[512,128]{1,0:T(8,128)S(1)}, f32[512,128]{1,0:T(8,128)S(1)}, u32[]{:S(2)}, u32[]{:S(2)}) %collective-permute-start.11) | collective-permute-done | bytes 262176 | tf_op jit(solution)/shard_map/ppermute | solution.py:508
  123.3 7.7 %collective-permute-start.13 = (f32[2,1160,128]{2,1,0:T(8,128)S(1)}, f32[2,1160,128]{2,1,0:T(8,128)S(1)}, u32[]{:S(2)}, u32[]{:S(2)}) collective-permute-start(f32[2,1160,128]{2,1,0:T(8,128)S(1)} %get-tuple-element.77.mine), channel_id=1, source_target_pairs={{0,1},{1,0},{2,3},{3,2},{4,5},{5,4},{6,7},{7,6},{8,9},{9,8},{10,11... | collective-permute-start | bytes 3563528 | tf_op jit(solution)/shard_map/ppermute | solution.py:519
  132.0 1.5 %collective-permute-done.13.theirs = f32[2,1160,128]{2,1,0:T(8,128)S(1)} collective-permute-done((f32[2,1160,128]{2,1,0:T(8,128)S(1)}, f32[2,1160,128]{2,1,0:T(8,128)S(1)}, u32[]{:S(2)}, u32[]{:S(2)}) %collective-permute-start.13) | collective-permute-done | bytes 1187872 | tf_op jit(solution)/shard_map/ppermute | solution.py:519
  (48 shorter events, 21.2 us)
Async XLA Ops:
  1.6 5.4 %collective-permute-start = (f32[128,128]{1,0:T(8,128)S(1)}, f32[128,128]{1,0:T(8,128)S(1)}, u32[]{:S(2)}, u32[]{:S(2)}) collective-permute-start(f32[128,128]{1,0:T(8,128)S(1)} %coarse.1.own), channel_id=1, source_target_pairs={{0,4},{4,8},{8,12},{12,16},{16,20},{20,24},{24,28},{28,32},{32,36}... | collective-permute-start | bytes 196616 | tf_op jit(solution)/shard_map/ppermute | solution.py:428
  9.9 7.2 %copy-start = (bf16[4,3,3,128,128]{4,3,2,1,0:T(8,128)(2,1)S(1)}, bf16[4,3,3,128,128]{4,3,2,1,0:T(8,128)(2,1)}, u32[]{:S(2)}) copy-start(bf16[4,3,3,128,128]{4,3,2,1,0:T(8,128)(2,1)} %param.5) | copy-start | bytes 3538948
  9.9 17.6 %all-to-all-start = ((f32[8,192,128]{2,1,0:T(8,128)}), f32[8,192,128]{2,1,0:T(8,128)S(1)}, u32[]{:S(2)}, u32[]{:S(2)}) async-start(f32[8,192,128]{2,1,0:T(8,128)} %start.1), calls=%async_computation | async-start | bytes 1572864 | tf_op jit(solution)/shard_map/all_to_all | solution.py:397
  15.8 11.7 %collective-permute-start.1 = (f32[128,128]{1,0:T(8,128)S(1)}, f32[128,128]{1,0:T(8,128)S(1)}, u32[]{:S(2)}, u32[]{:S(2)}) collective-permute-start(f32[128,128]{1,0:T(8,128)S(1)} %coarse.1.own), channel_id=1, source_target_pairs={{4,0},{8,4},{12,8},{16,12},{20,16},{24,20},{28,24},{32,28},{36,32}... | collective-permute-start | bytes 196616 | tf_op jit(solution)/shard_map/ppermute | solution.py:429
  28.6 5.3 %collective-permute-start.2 = (f32[192,128]{1,0:T(8,128)S(1)}, f32[192,128]{1,0:T(8,128)S(1)}, u32[]{:S(2)}, u32[]{:S(2)}) collective-permute-start(f32[192,128]{1,0:T(8,128)S(1)} %get-tuple-element.48.refs_1_.refs_3_), channel_id=1, source_target_pairs={{0,32},{4,36},{8,40},{12,44},{16,48},{20,52},{24,56},{28,60},{32,0... | collective-permute-start | bytes 294920 | tf_op jit(solution)/shard_map/ppermute | solution.py:449
  34.6 9.3 %collective-permute-start.5 = (f32[192,128]{1,0:T(8,128)S(1)}, f32[192,128]{1,0:T(8,128)S(1)}, u32[]{:S(2)}, u32[]{:S(2)}) collective-permute-start(f32[192,128]{1,0:T(8,128)S(1)} %pair.1), channel_id=1, source_target_pairs={{0,192},{4,196},{8,200},{12,204},{16,208},{20,212},{24,216},{28,22... | collective-permute-start | bytes 294920 | tf_op jit(solution)/shard_map/ppermute | solution.py:454
  40.0 5.1 %collective-permute-start.4 = (f32[192,128]{1,0:T(8,128)S(1)}, f32[192,128]{1,0:T(8,128)S(1)}, u32[]{:S(2)}, u32[]{:S(2)}) collective-permute-start(f32[192,128]{1,0:T(8,128)S(1)} %pair.1), channel_id=1, source_target_pairs={{0,128},{4,132},{8,136},{12,140},{16,144},{20,148},{24,152},{28,15... | collective-permute-start | bytes 294920 | tf_op jit(solution)/shard_map/ppermute | solution.py:454
  40.0 5.7 %collective-permute-start.3 = (f32[192,128]{1,0:T(8,128)S(1)}, f32[192,128]{1,0:T(8,128)S(1)}, u32[]{:S(2)}, u32[]{:S(2)}) collective-permute-start(f32[192,128]{1,0:T(8,128)S(1)} %pair.1), channel_id=1, source_target_pairs={{0,64},{4,68},{8,72},{12,76},{16,80},{20,84},{24,88},{28,92},{32,9... | collective-permute-start | bytes 294920 | tf_op jit(solution)/shard_map/ppermute | solution.py:454
  43.9 16.7 %copy-start.7 = (f32[512,128]{1,0:T(8,128)S(1)}, f32[512,128]{1,0:T(8,128)}, u32[]{:S(2)}) copy-start(f32[512,128]{1,0:T(8,128)} %get-tuple-element.57) | copy-start | bytes 786436
  65.1 9.8 %all-to-all-start.2 = ((f32[8,64,128]{2,1,0:T(8,128)}), f32[8,64,128]{2,1,0:T(8,128)S(1)}, u32[]{:S(2)}, u32[]{:S(2)}) async-start(f32[8,64,128]{2,1,0:T(8,128)} %bitcast.22), calls=%async_computation.2 | async-start | bytes 524288 | tf_op jit(solution)/shard_map/all_to_all | solution.py:397
  68.6 27.6 %collective-permute-start.10 = (f32[512,128]{1,0:T(8,128)S(1)}, f32[512,128]{1,0:T(8,128)S(1)}, u32[]{:S(2)}, u32[]{:S(2)}) collective-permute-start(f32[512,128]{1,0:T(8,128)S(1)} %bitcast_add_fusion.1.corrected), channel_id=1, source_target_pairs={{0,2},{1,3},{2,0},{3,1},{4,6},{5,7},{6,4},{7,5},{8,10},{9,11},{10,... | collective-permute-start | bytes 786440 | tf_op jit(solution)/shard_map/ppermute | solution.py:470
  76.0 15.3 %collective-permute-start.6 = (f32[64,128]{1,0:T(8,128)S(1)}, f32[64,128]{1,0:T(8,128)S(1)}, u32[]{:S(2)}, u32[]{:S(2)}) collective-permute-start(f32[64,128]{1,0:T(8,128)S(1)} %get-tuple-element.64.refs_1_), channel_id=1, source_target_pairs={{0,32},{4,36},{8,40},{12,44},{16,48},{20,52},{24,56},{28,60},{32,0... | collective-permute-start | bytes 98312 | tf_op jit(solution)/shard_map/ppermute | solution.py:487
  92.1 6.6 %collective-permute-start.9 = (f32[64,128]{1,0:T(8,128)S(1)}, f32[64,128]{1,0:T(8,128)S(1)}, u32[]{:S(2)}, u32[]{:S(2)}) collective-permute-start(f32[64,128]{1,0:T(8,128)S(1)} %back_pair.1), channel_id=1, source_target_pairs={{192,0},{196,4},{200,8},{204,12},{208,16},{212,20},{216,24},{220,2... | collective-permute-start | bytes 98312 | tf_op jit(solution)/shard_map/ppermute | solution.py:492
  93.4 6.2 %collective-permute-start.8 = (f32[64,128]{1,0:T(8,128)S(1)}, f32[64,128]{1,0:T(8,128)S(1)}, u32[]{:S(2)}, u32[]{:S(2)}) collective-permute-start(f32[64,128]{1,0:T(8,128)S(1)} %back_pair.1), channel_id=1, source_target_pairs={{128,0},{132,4},{136,8},{140,12},{144,16},{148,20},{152,24},{156,2... | collective-permute-start | bytes 98312 | tf_op jit(solution)/shard_map/ppermute | solution.py:492
  94.7 4.9 %collective-permute-start.7 = (f32[64,128]{1,0:T(8,128)S(1)}, f32[64,128]{1,0:T(8,128)S(1)}, u32[]{:S(2)}, u32[]{:S(2)}) collective-permute-start(f32[64,128]{1,0:T(8,128)S(1)} %back_pair.1), channel_id=1, source_target_pairs={{64,0},{68,4},{72,8},{76,12},{80,16},{84,20},{88,24},{92,28},{96,3... | collective-permute-start | bytes 98312 | tf_op jit(solution)/shard_map/ppermute | solution.py:492
  96.2 19.0 %copy-start.5 = (bf16[4,2,18,16,128]{4,3,2,1,0:T(8,128)(2,1)S(1)}, bf16[4,2,18,16,128]{4,3,2,1,0:T(8,128)(2,1)}, u32[]{:S(2)}) copy-start(bf16[4,2,18,16,128]{4,3,2,1,0:T(8,128)(2,1)} %get-tuple-element.70.refs_2_) | copy-start | bytes 1769476
  98.7 14.0 %copy-start.6 = (f32[512,128]{1,0:T(8,128)S(1)}, f32[512,128]{1,0:T(8,128)}, u32[]{:S(2)}) copy-start(f32[512,128]{1,0:T(8,128)} %get-tuple-element.59.ends_in) | copy-start | bytes 786436
  99.5 15.6 %copy-start.1 = (bf16[4,1152,128]{2,1,0:T(8,128)(2,1)S(1)}, bf16[4,1152,128]{2,1,0:T(8,128)(2,1)}, u32[]{:S(2)}) copy-start(bf16[4,1152,128]{2,1,0:T(8,128)(2,1)} %flip.1.transposed_in.refs_1_.a) | copy-start | bytes 3538948
  99.6 15.6 %copy-start.4 = (f32[4,512,128]{2,1,0:T(8,128)S(1)}, f32[4,512,128]{2,1,0:T(8,128)}, u32[]{:S(2)}) copy-start(f32[4,512,128]{2,1,0:T(8,128)} %get-tuple-element.71.refs_3_) | copy-start | bytes 3145732
  112.7 9.3 %collective-permute-start.11 = (f32[512,128]{1,0:T(8,128)S(1)}, f32[512,128]{1,0:T(8,128)S(1)}, u32[]{:S(2)}, u32[]{:S(2)}) collective-permute-start(f32[512,128]{1,0:T(8,128)S(1)} %bitcast_add_fusion.refs_0_), channel_id=1, source_target_pairs={{0,2},{1,3},{2,0},{3,1},{4,6},{5,7},{6,4},{7,5},{8,10},{9,11},{10,... | collective-permute-start | bytes 786440 | tf_op jit(solution)/shard_map/ppermute | solution.py:508
  115.2 6.8 %copy-start.2 = (f32[4,512,128]{2,1,0:T(8,128)S(1)}, f32[4,512,128]{2,1,0:T(8,128)}, u32[]{:S(2)}) copy-start(f32[4,512,128]{2,1,0:T(8,128)} %get-tuple-element.74.refs_3_.c) | copy-start | bytes 3145732
  115.2 6.8 %copy-start.3 = (bf16[4,2,18,16,128]{4,3,2,1,0:T(8,128)(2,1)S(1)}, bf16[4,2,18,16,128]{4,3,2,1,0:T(8,128)(2,1)}, u32[]{:S(2)}) copy-start(bf16[4,2,18,16,128]{4,3,2,1,0:T(8,128)(2,1)} %get-tuple-element.73.refs_2_.b) | copy-start | bytes 1769476
  123.3 10.2 %collective-permute-start.13 = (f32[2,1160,128]{2,1,0:T(8,128)S(1)}, f32[2,1160,128]{2,1,0:T(8,128)S(1)}, u32[]{:S(2)}, u32[]{:S(2)}) collective-permute-start(f32[2,1160,128]{2,1,0:T(8,128)S(1)} %get-tuple-element.77.mine), channel_id=1, source_target_pairs={{0,1},{1,0},{2,3},{3,2},{4,5},{5,4},{6,7},{7,6},{8,9},{9,8},{10,11... | collective-permute-start | bytes 3563528 | tf_op jit(solution)/shard_map/ppermute | solution.py:519
  131.9 3.3 %collective-permute-start.12 = (f32[2,1160,128]{2,1,0:T(8,128)S(1)}, f32[2,1160,128]{2,1,0:T(8,128)S(1)}, u32[]{:S(2)}, u32[]{:S(2)}) collective-permute-start(f32[2,1160,128]{2,1,0:T(8,128)S(1)} %other_early.1.mine), channel_id=1, source_target_pairs={{0,1},{1,0},{2,3},{3,2},{4,5},{5,4},{6,7},{7,6},{8,9},{9,8},{10,11... | collective-permute-start | bytes 3563528 | tf_op jit(solution)/shard_map/ppermute | solution.py:527
